TPU v7x, 32 devices: a whole 2x2x4 slice. The times are simulated.
32 devices in a mesh: space: 16 (over z, x, core), band: 2 (over y).
Axes of the slice: x: 2, y: 2, z: 4, core: 2. Of those that a mesh axis runs over, the one named last changes fastest.
Arguments:
- wave_in: bfloat16 [256, 16, 16, 256], P('space', None, None, 'band'), parts along dimension 3, may hold values from -6 to 6
- mass_scale: float32 [256, 256], P('space'), may hold values from 0.5 to 1
- potential: float32 [256, 256], P('space'), may hold values from -2 to 1
- elem_scale: float32 [32, 2, 2], P('space'), may hold values from 0.5 to 1.5
- stiffness: bfloat16 [729, 729], replicated, as said below
- proj_lower: bfloat16 [16, 729, 32], P('space'), may hold values from -0.21875 to 0.21875
- proj_upper: bfloat16 [16, 729, 32], P('space'), may hold values from -0.21875 to 0.21875
- kb_coef: float32 [16, 32], P('space'), may hold values from -3 to 3
- atom_column: int32 [16], P('space'), may hold values from 0 to 3
- chan_count: int32 [16], P('space'), may hold values from 8 to 32
- upper_column: int32 [16], P('space'), may hold values from 0 to 3
Outputs:
- filtered: bfloat16 [256, 16, 16, 256], P('space', None, None, 'band'), parts along dimension 3
- coefficients: float32 [16, 32, 256], P('space', None, 'band'), parts along dimension 2
There are 2 independent parts, one for each index of `band`. A program takes and returns all parts, laid end to end along the dimension named above; an argument that names none is the same for every part. Nothing has to cross between parts.
Inputs may be any that keep to these rules, and one draw needn't show every extreme that they name: stiffness is symmetric.
All inputs are finite; a program needn't handle non-finite values.
Results may differ from a plain program's by a relative error of at most 0.006.
Values may be sent and summed in bfloat16 or wider, within the bound.
No kernel may reach another device: no remote copies, remote signals or barrier semaphores. Data moves between devices by JAX's collectives and lax.ppermute only.
A program may use at most 64 MiB of HBM per device.

v0:
```python
import jax
import jax.numpy as jnp
from jax import lax
from jax.sharding import PartitionSpec as P

spectrum_center = 1.0
spectrum_half = 6.0
highest = lax.Precision.HIGHEST


def shifted(value, axis, steps):
    count = lax.axis_size(axis)
    pairs = [(source, (source + steps) % count) for source in range(count)]
    return lax.ppermute(value, axis, pairs)


def wrap_sides(planes):
    planes = jnp.concatenate([planes, planes[:, :1]], axis=1)
    return jnp.concatenate([planes, planes[:, :, :1]], axis=2)


def layer_blocks(layer_nodes, degree):
    points = degree + 1
    gathered = []
    for across in range(2):
        for column in range(2):
            portion = layer_nodes[
                :,
                across * degree : across * degree + points,
                column * degree : column * degree + points,
            ]
            gathered.append(portion.reshape(points * points * points, layer_nodes.shape[-1]))
    return jnp.stack(gathered)


def cut_piece(values, start, stop, axis):
    return lax.slice_in_dim(values, start, stop, axis=axis)


def join_pair(lower, upper, axis, wrapped, degree):
    first = cut_piece(lower, 0, 1, axis)
    if wrapped:
        first = first + cut_piece(upper, degree, degree + 1, axis)
    middle = cut_piece(lower, degree, degree + 1, axis) + cut_piece(upper, 0, 1, axis)
    pieces = [first, cut_piece(lower, 1, degree, axis), middle, cut_piece(upper, 1, degree, axis)]
    if not wrapped:
        pieces.append(cut_piece(upper, degree, degree + 1, axis))
    return jnp.concatenate(pieces, axis=axis)


def assemble_blocks(results, degree):
    points = degree + 1
    band_count = results.shape[-1]
    grouped = results.reshape(2, 2, 2, points, points, points, band_count)
    joined_columns = join_pair(grouped[:, :, 0], grouped[:, :, 1], 4, True, degree)
    joined_across = join_pair(joined_columns[:, 0], joined_columns[:, 1], 2, True, degree)
    return join_pair(joined_across[0], joined_across[1], 0, False, degree)


def split_layers(nodal_field, degree):
    upper_rim = shifted(nodal_field[:1], "space", -1)
    bottom_blocks = layer_blocks(wrap_sides(nodal_field[: degree + 1]), degree)
    top_blocks = layer_blocks(
        wrap_sides(jnp.concatenate([nodal_field[degree:], upper_rim], axis=0)), degree
    )
    return (bottom_blocks, top_blocks)


def column_onehot(columns):
    return (columns[:, None] == jnp.arange(4, dtype=jnp.int32)[None, :]).astype(jnp.float32)


def projections(projector, blocks, columns):
    every_column = jnp.einsum(
        "anc,knb->akcb", projector, blocks, preferred_element_type=jnp.float32
    )
    return jnp.einsum("ak,akcb->acb", column_onehot(columns), every_column, precision=highest)


def scatter_columns(projector, coef_block, columns):
    placed = (
        column_onehot(columns).astype(jnp.bfloat16)[:, :, None, None] * coef_block[:, None, :, :]
    )
    return jnp.einsum("anc,akcb->knb", projector, placed, preferred_element_type=jnp.float32)


def gather_partials(bottom_blocks, top_blocks, proj_lower, proj_upper, atom_column, upper_column):
    held_part = projections(proj_upper, bottom_blocks, upper_column)
    incoming = shifted(held_part, "space", -1)
    own_part = projections(proj_lower, top_blocks, atom_column)
    return (held_part, own_part, incoming)


def per_device(
    wave_in,
    mass_scale,
    potential,
    elem_scale,
    stiffness,
    proj_lower,
    proj_upper,
    kb_coef,
    atom_column,
    chan_count,
    upper_column,
):
    extent = wave_in.shape[0]
    degree = extent // 2
    channels = kb_coef.shape[-1]
    mass_nodes = mass_scale.reshape(extent, extent, extent, 1)
    local_potential = potential.reshape(extent, extent, extent, 1)
    scales = elem_scale.reshape(8)
    live_channels = (jnp.arange(channels, dtype=jnp.int32)[None, :] < chan_count[:, None]).astype(
        jnp.float32
    )
    weights = kb_coef * live_channels

    def operator(nodal_field):
        bottom_blocks, top_blocks = split_layers(nodal_field, degree)
        held_part, own_part, incoming = gather_partials(
            bottom_blocks, top_blocks, proj_lower, proj_upper, atom_column, upper_column
        )
        own_coef = ((own_part + incoming) * weights[:, :, None]).astype(jnp.bfloat16)
        below_coef = shifted(own_coef, "space", 1)
        local_bottom = (
            jnp.einsum("ij,ejb->eib", stiffness, bottom_blocks, preferred_element_type=jnp.float32)
            * scales[:4, None, None]
        )
        local_top = (
            jnp.einsum("ij,ejb->eib", stiffness, top_blocks, preferred_element_type=jnp.float32)
            * scales[4:, None, None]
        )
        results = jnp.concatenate(
            [
                local_bottom + scatter_columns(proj_upper, below_coef, upper_column),
                local_top + scatter_columns(proj_lower, own_coef, atom_column),
            ]
        )
        summed = assemble_blocks(results, degree)
        received = shifted(summed[-1], "space", 1)
        assembled = jnp.concatenate([summed[:1] + received[None], summed[1:-1]], axis=0)
        return mass_nodes * (assembled + local_potential * nodal_field.astype(jnp.float32))

    initial = wave_in.astype(jnp.float32)
    scaled_start = (mass_nodes * initial).astype(jnp.bfloat16)
    image_one = operator(scaled_start)
    step_one = ((image_one - spectrum_center * initial) / spectrum_half).astype(jnp.bfloat16)
    scaled_step = (mass_nodes * step_one.astype(jnp.float32)).astype(jnp.bfloat16)
    image_two = operator(scaled_step)
    filtered = (
        2.0 * (image_two - spectrum_center * step_one.astype(jnp.float32)) / spectrum_half - initial
    ).astype(jnp.bfloat16)
    bottom_blocks, top_blocks = split_layers(filtered, degree)
    held_part, own_part, incoming = gather_partials(
        bottom_blocks, top_blocks, proj_lower, proj_upper, atom_column, upper_column
    )
    coefficients = own_part + incoming
    return (filtered, coefficients)


def solution(mesh):
    in_specs = (
        P("space", None, None, "band"),
        P("space", None),
        P("space", None),
        P("space", None, None),
        P(),
        P("space", None, None),
        P("space", None, None),
        P("space", None),
        P("space"),
        P("space"),
        P("space"),
    )
    out_specs = (P("space", None, None, "band"), P("space", None, "band"))
    return jax.shard_map(
        per_device, mesh=mesh, in_specs=in_specs, out_specs=out_specs, check_vma=False
    )
```

profile of v0, /device:TPU:0, one launch (start us, length us, event | category | flops | bytes accessed | tf_op | source)
XLA Modules:
  0.0 113.7 jit_solution(1972892534403874691)
XLA Ops:
  0.6 0.9 mul.169
  1.6 1.8 %fusion.2 = bf16[16,16,16,128]{3,2,1,0:T(8,128)(2,1)S(1)} fusion(bf16[16,16,16,128]{3,2,1,0:T(8,128)(2,1)} %param.11, f32[16,16,16]{2,1,0:T(8,128)S(1)} %mul.169), kind=kLoop, calls=%fused_computation.15 | loop fusion | flops 1572864 | bytes 2113536 | tf_op jit(solution)/shard_map/convert_element_type | solution.py:145
  3.3 0.6 slice.424
  3.9 5.4 %collective-permute-start = (bf16[1,16,16,128]{3,2,1,0:T(8,128)(2,1)}, bf16[1,16,16,128]{3,2,1,0:T(8,128)(2,1)S(1)}, u32[]{:S(2)}, u32[]{:S(2)}) collective-permute-start(bf16[1,16,16,128]{3,2,1,0:T(8,128)(2,1)} %slice.424), channel_id=1, source_target_pairs={{0,30},{2,0},{4,2},{6,4},{8,6},{10,8},{12,10},{14,12},{16,14},{18,... | collective-permute-start | bytes 196616 | tf_op jit(solution)/shard_map/ppermute | solution.py:14
  9.4 0.6 slice.422
  10.9 1.9 %fusion.38 = (bf16[9,9,9,128]{3,2,1,0:T(8,128)(2,1)}, bf16[9,9,9,128]{3,2,1,0:T(8,128)(2,1)}, bf16[9,9,9,128]{3,2,1,0:T(8,128)(2,1)S(1)}) fusion(bf16[9,1,16,128]{3,2,1,0:T(8,128)(2,1)} %slice.422, bf16[9,16,16,128]{3,2,1,0:T(8,128)(2,1)S(1)} %slice.421), kind=kLoop, calls=%fused_computation.104 | loop fusion | flops 1866240 | bytes 1186560 | tf_op jit(solution)/shard_map/concatenate | solution.py:19
  12.8 1.1 stack_reshape.75
  13.8 1.1 stack_reshape.73
  16.0 0.7 collective-permute-start.1
  18.3 0.7 mul.190
  19.0 3.0 %fusion.14 = f32[4,128,729]{1,2,0:T(8,128)} fusion(bf16[4,729,128]{2,1,0:T(8,128)(2,1)} %copy-done.12, bf16[729,729]{1,0:T(8,128)(2,1)S(1)} %copy-done), kind=kOutput, calls=%fused_computation.35 | convolution fusion | flops 544195584 | bytes 3302370 | tf_op jit(solution)/shard_map/ij,ejb->eib/dot_general | solution.py:126
  22.9 0.8 fusion.12
  24.4 0.4 add_bitcast_fusion.2
  24.9 5.3 %collective-permute-done.2 = bf16[1,32,128]{2,1,0:T(8,128)(2,1)S(1)} collective-permute-done((bf16[1,32,128]{2,1,0:T(8,128)(2,1)S(1)}, bf16[1,32,128]{2,1,0:T(8,128)(2,1)S(1)}, u32[]{:S(2)}, u32[]{:S(2)}) %collective-permute-start.2) | collective-permute-done | bytes 8224 | tf_op jit(solution)/shard_map/ppermute | solution.py:14
  30.2 0.4 add_bitcast_fusion.3
  30.8 1.7 %copy.17 = f32[8,729,128]{2,0,1:T(8,128)S(1)} copy(f32[8,729,128]{2,1,0:T(8,128)S(1)} %pad_maximum_fusion) | data formatting | bytes 5971968 | tf_op jit(solution)/shard_map/concatenate | solution.py:133
  32.6 2.3 %fusion.94 = (f32[2,2,1,9,9,9,128]{6,2,1,0,5,4,3:T(1,128)S(1)}, f32[2,2,1,9,9,9,128]{6,2,1,0,5,4,3:T(1,128)S(1)}) fusion(f32[2,2,2,9,9,9,128]{6,2,1,0,5,4,3:T(2,128)S(1)} %bitcast.193), kind=kLoop, calls=%fused_computation.206 | loop fusion | bytes 5971968 | tf_op jit(solution)/shard_map/slice | solution.py:55
  34.9 0.4 slice.431
  35.9 1.5 %pad_maximum_fusion.2 = f32[2,2,9,9,16,128]{5,1,0,4,3,2:T(2,128)S(1)} fusion(f32[2,2,9,9,7,128]{5,1,0,4,3,2:T(2,128)S(1)} %slice.434, f32[2,2,9,9,1,128]{5,1,0,4,3,2:T(2,128)S(1)} %get-tuple-element.7, f32[2,2,9,9,7,128]{5,1,0,4,3,2:T(2,128)S(1)} %slice.431, f32[2,2,9,9,1,128]{5,1,0,4,3,2:T(2,128)S(1)} %get-tuple-element.6), kind=kLoop, calls=%fused_computation.5 | loop fusion | flops 1990656 | bytes 5308416 | tf_op jit(solution)/shard_map/concatenate | solution.py:48
  37.4 3.0 %fusion.95 = (f32[2,1,9,9,16,128]{5,1,0,4,3,2:T(1,128)S(1)}, f32[2,1,9,9,16,128]{5,1,0,4,3,2:T(1,128)S(1)}) fusion(f32[2,2,9,9,16,128]{5,1,0,4,3,2:T(2,128)S(1)} %pad_maximum_fusion.2), kind=kLoop, calls=%fused_computation.207 | loop fusion | bytes 5308416 | tf_op jit(solution)/shard_map/slice | solution.py:56
  40.7 0.4 pad_maximum_fusion.36
  41.1 1.3 %pad_maximum_fusion.6 = f32[1,7,16,16,128]{4,0,3,2,1:T(1,128)S(1)} fusion(f32[2,9,7,16,128]{4,0,3,2,1:T(2,128)S(1)} %slice.442, f32[2,9,1,16,128]{4,0,3,2,1:T(2,128)S(1)} %get-tuple-element.15, f32[2,9,7,16,128]{4,0,3,2,1:T(2,128)S(1)} %slice.439, f32[2,9,1,16,128]{4,0,3,2,1:T(2,128)S(1)} %get-tuple-element.14), kind=kLoop, calls=%fused_computation.45 | loop fusion | flops 688128 | bytes 3276800 | tf_op jit(solution)/shard_map/slice | solution.py:37
  42.4 1.3 %pad_maximum_fusion.4 = f32[2,9,16,16,128]{4,0,3,2,1:T(2,128)S(1)} fusion(f32[2,9,7,16,128]{4,0,3,2,1:T(2,128)S(1)} %slice.442, f32[2,9,1,16,128]{4,0,3,2,1:T(2,128)S(1)} %get-tuple-element.15, f32[2,9,7,16,128]{4,0,3,2,1:T(2,128)S(1)} %slice.439, f32[2,9,1,16,128]{4,0,3,2,1:T(2,128)S(1)} %get-tuple-element.14), kind=kLoop, calls=%fused_computation.11 | loop fusion | flops 1769472 | bytes 4718592 | tf_op jit(solution)/shard_map/concatenate | solution.py:48
  44.0 0.7 slice.443
  44.8 6.3 %collective-permute-done.3 = f32[16,16,128]{2,1,0:T(8,128)S(1)} collective-permute-done((f32[16,16,128]{2,1,0:T(8,128)S(1)}, f32[16,16,128]{2,1,0:T(8,128)S(1)}, u32[]{:S(2)}, u32[]{:S(2)}) %collective-permute-start.3) | collective-permute-done | bytes 131104 | tf_op jit(solution)/shard_map/ppermute | solution.py:14
  51.2 1.5 %fusion = bf16[16,16,16,128]{3,2,1,0:T(8,128)(2,1)S(1)} fusion(f32[16,16,16]{2,1,0:T(8,128)S(1)} %mul.169, bf16[16,16,16,128]{3,2,1,0:T(8,128)(2,1)S(1)} %copy-done.2, f32[16,16,16]{2,1,0:T(8,128)S(1)} %copy-done.10, f32[7,16,16,128]{3,2,1,0:T(8,128)S(1)} %bitcast.197, f32[1,16,16,128]{3,2,1,0:T(8,128)S(1)} %add_bitcast_fusion.4, ...), kind=kLoop, calls=%fused_computation.13 | loop fusion | flops 8388608 | bytes 4227072 | tf_op jit(solution)/shard_map/convert_element_type | solution.py:148
  52.6 0.7 slice.446
  53.3 0.6 slice.448
  53.9 0.7 slice.444
  54.7 0.9 slice.445
  55.6 1.7 %stack_reshape.80 = bf16[1,729,128]{2,1,0:T(8,128)(2,1)} reshape(bf16[9,9,9,128]{3,2,1,0:T(8,128)(2,1)} %slice.444) | data formatting | bytes 373248 | tf_op jit(solution)/shard_map/stack;reshape | solution.py:33
  57.4 2.4 %fusion.36 = (bf16[9,9,9,128]{3,2,1,0:T(8,128)(2,1)}, bf16[9,9,9,128]{3,2,1,0:T(8,128)(2,1)}, bf16[9,9,9,128]{3,2,1,0:T(8,128)(2,1)}) fusion(bf16[9,1,16,128]{3,2,1,0:T(8,128)(2,1)} %slice.446, bf16[9,16,16,128]{3,2,1,0:T(8,128)(2,1)} %slice.445), kind=kLoop, calls=%fused_computation.91 | loop fusion | flops 1866240 | bytes 1186560 | tf_op jit(solution)/shard_map/concatenate | solution.py:19
  59.7 1.7 %stack_reshape.83 = bf16[1,729,128]{2,1,0:T(8,128)(2,1)} reshape(bf16[9,9,9,128]{3,2,1,0:T(8,128)(2,1)} %get-tuple-element.30) | data formatting | bytes 373248 | tf_op jit(solution)/shard_map/stack;reshape | solution.py:33
  61.4 1.7 %stack_reshape.81 = bf16[1,729,128]{2,1,0:T(8,128)(2,1)} reshape(bf16[9,9,9,128]{3,2,1,0:T(8,128)(2,1)} %get-tuple-element.31) | data formatting | bytes 373248 | tf_op jit(solution)/shard_map/stack;reshape | solution.py:33
  63.2 1.7 %stack_reshape.82 = bf16[1,729,128]{2,1,0:T(8,128)(2,1)} reshape(bf16[9,9,9,128]{3,2,1,0:T(8,128)(2,1)} %get-tuple-element.32) | data formatting | bytes 373248 | tf_op jit(solution)/shard_map/stack;reshape | solution.py:33
  64.9 0.9 constant_dynamic-update-slice_fusion.11
  65.9 1.0 constant_dynamic-update-slice_fusion.10
  66.8 1.0 constant_dynamic-update-slice_fusion.9
  67.8 1.0 constant_dynamic-update-slice_fusion.8
  69.0 1.9 %fusion.10 = f32[4,128,729]{1,2,0:T(8,128)} fusion(bf16[4,729,128]{2,1,0:T(8,128)(2,1)S(1)} %constant_dynamic-update-slice_fusion.8, bf16[729,729]{1,0:T(8,128)(2,1)S(1)} %copy-done), kind=kOutput, calls=%fused_computation.31 | convolution fusion | flops 544195584 | bytes 3302370 | tf_op jit(solution)/shard_map/ij,ejb->eib/dot_general | solution.py:126
  71.2 1.6 %collective-permute-done.4 = bf16[1,16,16,128]{3,2,1,0:T(8,128)(2,1)S(1)} collective-permute-done((bf16[1,16,16,128]{3,2,1,0:T(8,128)(2,1)S(1)}, bf16[1,16,16,128]{3,2,1,0:T(8,128)(2,1)S(1)}, u32[]{:S(2)}, u32[]{:S(2)}) %collective-permute-start.4) | collective-permute-done | bytes 65568 | tf_op jit(solution)/shard_map/ppermute | solution.py:14
  72.8 1.1 fusion.35
  73.9 1.7 %stack_reshape.87 = bf16[1,729,128]{2,1,0:T(8,128)(2,1)} reshape(bf16[9,9,9,128]{3,2,1,0:T(8,128)(2,1)} %get-tuple-element.33) | data formatting | bytes 373248 | tf_op jit(solution)/shard_map/stack;reshape | solution.py:33
  75.7 1.8 %stack_reshape.86 = bf16[1,729,128]{2,1,0:T(8,128)(2,1)} reshape(bf16[9,9,9,128]{3,2,1,0:T(8,128)(2,1)} %get-tuple-element.34) | data formatting | bytes 373248 | tf_op jit(solution)/shard_map/stack;reshape | solution.py:33
  77.4 1.7 %stack_reshape.85 = bf16[1,729,128]{2,1,0:T(8,128)(2,1)} reshape(bf16[9,9,9,128]{3,2,1,0:T(8,128)(2,1)} %get-tuple-element.35) | data formatting | bytes 373248 | tf_op jit(solution)/shard_map/stack;reshape | solution.py:33
  79.1 1.7 %stack_reshape.84 = bf16[1,729,128]{2,1,0:T(8,128)(2,1)} reshape(bf16[9,9,9,128]{3,2,1,0:T(8,128)(2,1)} %get-tuple-element.43) | data formatting | bytes 373248 | tf_op jit(solution)/shard_map/stack;reshape | solution.py:33
  80.9 0.9 constant_dynamic-update-slice_fusion.15
  81.8 1.0 constant_dynamic-update-slice_fusion.14
  82.8 1.0 constant_dynamic-update-slice_fusion.13
  83.7 1.0 constant_dynamic-update-slice_fusion.12
  84.7 1.1 convolution_bitcast_fusion.3
  85.8 0.8 fusion.8
  86.8 0.9 multiply_convert_fusion
  87.8 0.4 add_bitcast_fusion
  88.2 5.4 %collective-permute-done.6 = bf16[1,32,128]{2,1,0:T(8,128)(2,1)S(1)} collective-permute-done((bf16[1,32,128]{2,1,0:T(8,128)(2,1)S(1)}, bf16[1,32,128]{2,1,0:T(8,128)(2,1)S(1)}, u32[]{:S(2)}, u32[]{:S(2)}) %collective-permute-start.6) | collective-permute-done | bytes 8224 | tf_op jit(solution)/shard_map/ppermute | solution.py:14
  93.6 0.4 add_bitcast_fusion.1
  94.2 1.7 %copy.25 = f32[8,729,128]{2,0,1:T(8,128)S(1)} copy(f32[8,729,128]{2,1,0:T(8,128)S(1)} %pad_maximum_fusion.1) | data formatting | bytes 5971968 | tf_op jit(solution)/shard_map/concatenate | solution.py:133
  96.0 2.3 %fusion.93 = (f32[2,2,1,9,9,9,128]{6,2,1,0,5,4,3:T(1,128)S(1)}, f32[2,2,1,9,9,9,128]{6,2,1,0,5,4,3:T(1,128)S(1)}) fusion(f32[2,2,2,9,9,9,128]{6,2,1,0,5,4,3:T(2,128)S(1)} %bitcast.194), kind=kLoop, calls=%fused_computation.205 | loop fusion | bytes 5971968 | tf_op jit(solution)/shard_map/slice | solution.py:55
  98.3 0.6 copy_bitcast_fusion
  99.4 0.7 pad_maximum_fusion.3
  101.1 7.0 %collective-permute-done.7 = f32[16,16,128]{2,1,0:T(8,128)S(1)} collective-permute-done((f32[16,16,128]{2,1,0:T(8,128)S(1)}, f32[16,16,128]{2,1,0:T(8,128)S(1)}, u32[]{:S(2)}, u32[]{:S(2)}) %collective-permute-start.7) | collective-permute-done | bytes 131104 | tf_op jit(solution)/shard_map/ppermute | solution.py:14
  108.1 1.5 %fusion.5 = bf16[16,16,16,128]{3,2,1,0:T(8,128)(2,1)S(1)} fusion(bf16[16,16,16,128]{3,2,1,0:T(8,128)(2,1)S(1)} %copy-done.2, f32[7,16,16,128]{3,2,1,0:T(8,128)S(1)} %maximum_bitcast_fusion, f32[1,16,16,128]{3,2,1,0:T(8,128)S(1)} %get-tuple-element.19, f32[7,16,16,128]{3,2,1,0:T(8,128)S(1)} %slice_bitcast_fusion.2, f32[1,16,16,128]{3,2,1,0:T(8,128)S(1)} %fusion.41, ...), kind=kLoop, calls=%fused_computation.18 | loop fusion | flops 14155776 | bytes 6324224 | tf_op jit(solution)/shard_map/convert_element_type | solution.py:152
  111.0 0.8 collective-permute-done.8
  113.1 0.6 add.131
  (150 shorter events, 9.2 us)
Async XLA Ops:
  0.6 18.4 %copy-start = (bf16[729,729]{1,0:T(8,128)(2,1)S(1)}, bf16[729,729]{1,0:T(8,128)(2,1)}, u32[]{:S(2)}) copy-start(bf16[729,729]{1,0:T(8,128)(2,1)} %param.15) | copy-start | bytes 3188650
  3.9 18.2 %collective-permute-start = (bf16[1,16,16,128]{3,2,1,0:T(8,128)(2,1)}, bf16[1,16,16,128]{3,2,1,0:T(8,128)(2,1)S(1)}, u32[]{:S(2)}, u32[]{:S(2)}) collective-permute-start(bf16[1,16,16,128]{3,2,1,0:T(8,128)(2,1)} %slice.424), channel_id=1, source_target_pairs={{0,30},{2,0},{4,2},{6,4},{8,6},{10,8},{12,10},{14,12},{16,14},{18,... | collective-permute-start | bytes 196616 | tf_op jit(solution)/shard_map/ppermute | solution.py:14
  10.9 4.3 %copy-start.13 = (bf16[1,729,32]{1,2,0:T(8,128)(2,1)S(1)}, bf16[1,729,32]{1,2,0:T(8,128)(2,1)}, u32[]{:S(2)}) copy-start(bf16[1,729,32]{1,2,0:T(8,128)(2,1)} %param.17) | copy-start | bytes 139972
  14.9 3.2 %copy-start.19 = (f32[2,2,2]{2,1,0:T(2,128)S(1)}, f32[2,2,2]{2,1,0:T(2,128)}, u32[]{:S(2)}) copy-start(f32[2,2,2]{2,1,0:T(2,128)} %param.14) | copy-start | bytes 100
  14.9 3.4 %copy-start.18 = (f32[16,256]{1,0:T(8,128)S(1)}, f32[16,256]{1,0:T(8,128)}, u32[]{:S(2)}) copy-start(f32[16,256]{1,0:T(8,128)} %param.13) | copy-start | bytes 49156
  15.2 0.9 copy-start.12
  16.0 8.1 %collective-permute-start.1 = (f32[1,32,128]{2,1,0:T(8,128)S(1)}, f32[1,32,128]{2,1,0:T(8,128)S(1)}, u32[]{:S(2)}, u32[]{:S(2)}) collective-permute-start(f32[1,32,128]{2,1,0:T(8,128)S(1)} %bitcast.216), channel_id=1, source_target_pairs={{0,30},{2,0},{4,2},{6,4},{8,6},{10,8},{12,10},{14,12},{16,14},{18,... | collective-permute-start | bytes 49160 | tf_op jit(solution)/shard_map/ppermute | solution.py:14
  16.8 5.3 %copy-start.30 = (f32[1,32]{1,0:T(1,128)S(1)}, f32[1,32]{1,0:T(1,128)}, u32[]{:S(2)}) copy-start(f32[1,32]{1,0:T(1,128)} %param.18) | copy-start | bytes 388
  18.1 6.3 %copy-start.24 = (bf16[4]{0:T(256)(128)(2,1)}, bf16[4]{0:T(256)(128)(2,1)S(1)}, u32[]{:S(2)}) copy-start(bf16[4]{0:T(256)(128)(2,1)S(1)} %fusion.84) | copy-start | bytes 28
  18.2 12.0 %copy-start.22 = (f32[4]{0:T(128)}, f32[4]{0:T(128)S(1)}, u32[]{:S(2)}) copy-start(f32[4]{0:T(128)S(1)} %mul.172) | copy-start | bytes 52
  18.3 6.1 %copy-start.28 = (f32[4]{0:T(128)}, f32[4]{0:T(128)S(1)}, u32[]{:S(2)}) copy-start(f32[4]{0:T(128)S(1)} %mul.183) | copy-start | bytes 52
  22.1 2.1 %copy-start.20 = (f32[32]{0:T(128)}, f32[32]{0:T(128)S(1)}, u32[]{:S(2)}) copy-start(f32[32]{0:T(128)S(1)} %fusion.83) | copy-start | bytes 388
  22.1 8.1 %copy-start.26 = (bf16[4]{0:T(256)(128)(2,1)}, bf16[4]{0:T(256)(128)(2,1)S(1)}, u32[]{:S(2)}) copy-start(bf16[4]{0:T(256)(128)(2,1)S(1)} %fusion.82) | copy-start | bytes 28
  22.8 0.8 copy-start.14
  23.7 6.5 %copy-start.9 = (f32[4,128,729]{1,2,0:T(8,128)S(1)}, f32[4,128,729]{1,2,0:T(8,128)}, u32[]{:S(2)}) copy-start(f32[4,128,729]{1,2,0:T(8,128)} %fusion.14) | copy-start | bytes 4478980
  24.2 5.9 %collective-permute-start.2 = (bf16[1,32,128]{2,1,0:T(8,128)(2,1)S(1)}, bf16[1,32,128]{2,1,0:T(8,128)(2,1)S(1)}, u32[]{:S(2)}, u32[]{:S(2)}) collective-permute-start(bf16[1,32,128]{2,1,0:T(8,128)(2,1)S(1)} %multiply_convert_fusion.1), channel_id=1, source_target_pairs={{0,2},{2,4},{4,6},{6,8},{8,10},{10,12},{12,14},{14,16},{16,18},{18... | collective-permute-start | bytes 24584 | tf_op jit(solution)/shard_map/ppermute | solution.py:14
  42.4 8.7 %copy-start.3 = (f32[1,7,16,16,128]{4,0,3,2,1:T(1,128)}, f32[1,7,16,16,128]{4,0,3,2,1:T(1,128)S(1)}, u32[]{:S(2)}) copy-start(f32[1,7,16,16,128]{4,0,3,2,1:T(1,128)S(1)} %pad_maximum_fusion.6) | copy-start | bytes 2752516
  43.7 7.4 %copy-start.2 = (bf16[16,16,16,128]{3,2,1,0:T(8,128)(2,1)S(1)}, bf16[16,16,16,128]{3,2,1,0:T(8,128)(2,1)}, u32[]{:S(2)}) copy-start(bf16[16,16,16,128]{3,2,1,0:T(8,128)(2,1)} %param.11) | copy-start | bytes 3145732
  43.7 7.4 %copy-start.10 = (f32[16,16,16]{2,1,0:T(8,128)S(1)}, f32[16,16,16]{2,1,0:T(8,128)}, u32[]{:S(2)}) copy-start(f32[16,16,16]{2,1,0:T(8,128)} %mul.190) | copy-start | bytes 49156
  43.7 7.4 %collective-permute-start.3 = (f32[16,16,128]{2,1,0:T(8,128)S(1)}, f32[16,16,128]{2,1,0:T(8,128)S(1)}, u32[]{:S(2)}, u32[]{:S(2)}) collective-permute-start(f32[16,16,128]{2,1,0:T(8,128)S(1)} %bitcast.210), channel_id=1, source_target_pairs={{0,2},{2,4},{4,6},{6,8},{8,10},{10,12},{12,14},{14,16},{16,18},{18... | collective-permute-start | bytes 393224 | tf_op jit(solution)/shard_map/ppermute | solution.py:14
  52.6 2.0 %copy-start.6 = (bf16[16,16,16,128]{3,2,1,0:T(8,128)(2,1)}, bf16[16,16,16,128]{3,2,1,0:T(8,128)(2,1)S(1)}, u32[]{:S(2)}) copy-start(bf16[16,16,16,128]{3,2,1,0:T(8,128)(2,1)S(1)} %fusion) | copy-start | bytes 3145732
  68.7 2.2 %copy-start.17 = (bf16[1,16,16,128]{3,2,1,0:T(8,128)(2,1)S(1)}, bf16[1,16,16,128]{3,2,1,0:T(8,128)(2,1)}, u32[]{:S(2)}) copy-start(bf16[1,16,16,128]{3,2,1,0:T(8,128)(2,1)} %slice.448) | copy-start | bytes 196612
  68.7 2.4 %copy-start.7 = (bf16[16,16,16,128]{3,2,1,0:T(8,128)(2,1)S(1)}, bf16[16,16,16,128]{3,2,1,0:T(8,128)(2,1)}, u32[]{:S(2)}) copy-start(bf16[16,16,16,128]{3,2,1,0:T(8,128)(2,1)} %copy-done.6) | copy-start | bytes 3145732
  70.9 1.9 %collective-permute-start.4 = (bf16[1,16,16,128]{3,2,1,0:T(8,128)(2,1)S(1)}, bf16[1,16,16,128]{3,2,1,0:T(8,128)(2,1)S(1)}, u32[]{:S(2)}, u32[]{:S(2)}) collective-permute-start(bf16[1,16,16,128]{3,2,1,0:T(8,128)(2,1)S(1)} %copy-done.17), channel_id=1, source_target_pairs={{0,30},{2,0},{4,2},{6,4},{8,6},{10,8},{12,10},{14,12},{16,14},{18,... | collective-permute-start | bytes 196616 | tf_op jit(solution)/shard_map/ppermute | solution.py:14
  71.2 15.7 %collective-permute-start.5 = (f32[1,32,128]{2,1,0:T(8,128)S(1)}, f32[1,32,128]{2,1,0:T(8,128)}, u32[]{:S(2)}, u32[]{:S(2)}) collective-permute-start(f32[1,32,128]{2,1,0:T(8,128)S(1)} %bitcast.217), channel_id=1, source_target_pairs={{0,30},{2,0},{4,2},{6,4},{8,6},{10,8},{12,10},{14,12},{16,14},{18,... | collective-permute-start | bytes 49160 | tf_op jit(solution)/shard_map/ppermute | solution.py:14
  84.7 2.2 %copy-start.21 = (f32[32]{0:T(128)S(1)}, f32[32]{0:T(128)}, u32[]{:S(2)}) copy-start(f32[32]{0:T(128)} %copy-done.20) | copy-start | bytes 388
  84.7 3.1 %copy-start.15 = (bf16[1,729,32]{1,2,0:T(8,128)(2,1)S(1)}, bf16[1,729,32]{1,2,0:T(8,128)(2,1)}, u32[]{:S(2)}) copy-start(bf16[1,729,32]{1,2,0:T(8,128)(2,1)} %param.16) | copy-start | bytes 139972
  84.7 3.1 %copy-start.25 = (bf16[4]{0:T(256)(128)(2,1)S(1)}, bf16[4]{0:T(256)(128)(2,1)}, u32[]{:S(2)}) copy-start(bf16[4]{0:T(256)(128)(2,1)} %copy-done.24) | copy-start | bytes 28
  84.7 3.1 %copy-start.29 = (f32[4]{0:T(128)S(1)}, f32[4]{0:T(128)}, u32[]{:S(2)}) copy-start(f32[4]{0:T(128)} %copy-done.28) | copy-start | bytes 52
  86.6 7.0 %copy-start.8 = (f32[4,128,729]{1,2,0:T(8,128)S(1)}, f32[4,128,729]{1,2,0:T(8,128)}, u32[]{:S(2)}) copy-start(f32[4,128,729]{1,2,0:T(8,128)} %fusion.10) | copy-start | bytes 4478980
  86.6 7.0 %copy-start.23 = (f32[4]{0:T(128)S(1)}, f32[4]{0:T(128)}, u32[]{:S(2)}) copy-start(f32[4]{0:T(128)} %copy-done.22) | copy-start | bytes 52
  86.6 7.0 %copy-start.27 = (bf16[4]{0:T(256)(128)(2,1)S(1)}, bf16[4]{0:T(256)(128)(2,1)}, u32[]{:S(2)}) copy-start(bf16[4]{0:T(256)(128)(2,1)} %copy-done.26) | copy-start | bytes 28
  87.8 5.8 %collective-permute-start.6 = (bf16[1,32,128]{2,1,0:T(8,128)(2,1)S(1)}, bf16[1,32,128]{2,1,0:T(8,128)(2,1)S(1)}, u32[]{:S(2)}, u32[]{:S(2)}) collective-permute-start(bf16[1,32,128]{2,1,0:T(8,128)(2,1)S(1)} %multiply_convert_fusion), channel_id=1, source_target_pairs={{0,2},{2,4},{4,6},{6,8},{8,10},{10,12},{12,14},{14,16},{16,18},{18... | collective-permute-start | bytes 24584 | tf_op jit(solution)/shard_map/ppermute | solution.py:14
  100.8 7.2 %collective-permute-start.7 = (f32[16,16,128]{2,1,0:T(8,128)S(1)}, f32[16,16,128]{2,1,0:T(8,128)S(1)}, u32[]{:S(2)}, u32[]{:S(2)}) collective-permute-start(f32[16,16,128]{2,1,0:T(8,128)S(1)} %get-tuple-element.18), channel_id=1, source_target_pairs={{0,2},{2,4},{4,6},{6,8},{8,10},{10,12},{12,14},{14,16},{16,18},{18... | collective-permute-start | bytes 393224 | tf_op jit(solution)/shard_map/ppermute | solution.py:14
  101.1 7.0 %copy-start.4 = (f32[1,7,16,16,128]{4,0,3,2,1:T(1,128)S(1)}, f32[1,7,16,16,128]{4,0,3,2,1:T(1,128)}, u32[]{:S(2)}) copy-start(f32[1,7,16,16,128]{4,0,3,2,1:T(1,128)} %copy-done.3) | copy-start | bytes 2752516
  101.1 7.0 %copy-start.11 = (f32[16,16,16]{2,1,0:T(8,128)S(1)}, f32[16,16,16]{2,1,0:T(8,128)}, u32[]{:S(2)}) copy-start(f32[16,16,16]{2,1,0:T(8,128)} %mul.190) | copy-start | bytes 49156
  109.7 1.3 %copy-start.5 = (bf16[16,16,16,128]{3,2,1,0:T(8,128)(2,1)}, bf16[16,16,16,128]{3,2,1,0:T(8,128)(2,1)S(1)}, u32[]{:S(2)}) copy-start(bf16[16,16,16,128]{3,2,1,0:T(8,128)(2,1)S(1)} %fusion.5) | copy-start | bytes 3145732
  109.9 2.0 %collective-permute-start.8 = (bf16[1,16,16,128]{3,2,1,0:T(8,128)(2,1)S(1)}, bf16[1,16,16,128]{3,2,1,0:T(8,128)(2,1)S(1)}, u32[]{:S(2)}, u32[]{:S(2)}) collective-permute-start(bf16[1,16,16,128]{3,2,1,0:T(8,128)(2,1)S(1)} %slice.469), channel_id=1, source_target_pairs={{0,30},{2,0},{4,2},{6,4},{8,6},{10,8},{12,10},{14,12},{16,14},{18,... | collective-permute-start | bytes 196616 | tf_op jit(solution)/shard_map/ppermute | solution.py:14
  111.0 2.1 %collective-permute-start.9 = (f32[1,32,128]{2,1,0:T(8,128)S(1)}, f32[1,32,128]{2,1,0:T(8,128)S(1)}, u32[]{:S(2)}, u32[]{:S(2)}) collective-permute-start(f32[1,32,128]{2,1,0:T(8,128)S(1)} %bitcast.218), channel_id=1, source_target_pairs={{0,30},{2,0},{4,2},{6,4},{8,6},{10,8},{12,10},{14,12},{16,14},{18,... | collective-permute-start | bytes 49160 | tf_op jit(solution)/shard_map/ppermute | solution.py:14
  111.8 0.8 copy-start.16
  112.2 1.5 %copy-start.1 = (bf16[729,729]{1,0:T(8,128)(2,1)S(1)}, bf16[729,729]{1,0:T(8,128)(2,1)}, u32[]{:S(2)}) copy-start(bf16[729,729]{1,0:T(8,128)(2,1)} %param.15) | copy-start | bytes 3188650
where the time goes:
time: 116 us; the launch traced here: 114 us
  local copies, waits for them, and re-layouts  46.1 us (40%)
  waiting for transfers between devices  26.3 us (23%)
  other arithmetic  19 us (16%)
  matrix products  11.7 us (10%)
  starting transfers between devices  6.82 us (6%)
  between operations  3.73 us (3%)
    ppermute x10, waiting for transfers between devices, shifted(): return lax.ppermute(value, axis, pairs)  26.3 us
    another operation x28, local copies, waits for them, and re-layouts, layer_blocks(): return jnp.stack(gathered)  19.2 us
    ppermute x10, starting transfers between devices, shifted(): return lax.ppermute(value, axis, pairs)  6.82 us
    unnamed x74, local copies, waits for them, and re-layouts  6.52 us
    concatenate x4, other arithmetic, wrap_sides(): return jnp.concatenate([planes, planes[:, :, :1]], axis=2)  5.59 us
    dot_general x2, matrix products, operator(): jnp.einsum('ij,ejb->eib', stiffness, bottom_blocks, preferred_element_typ...  4.93 us
    slice x2, local copies, waits for them, and re-layouts, assemble_blocks(): grouped[:, :, 0]  4.61 us
    concatenate x4, other arithmetic, join_pair(): return jnp.concatenate(pieces, axis=axis)  3.77 us
  transfers between devices with their start and end apart: 10, of which 6 were waited for; matrix products, arithmetic and copies ran while one was open for 26% of the time, Pallas kernels for 0%

commit v1 on v0

v1 whole, which is shorter than its diff:
```python
import functools

import jax
import jax.numpy as jnp
import numpy as np
from jax import lax
from jax.experimental import pallas as pl
from jax.experimental.pallas import tpu as pltpu
from jax.sharding import PartitionSpec as P

spectrum_center = 1.0
spectrum_half = 6.0
f32 = jnp.float32
bf16 = jnp.bfloat16
LANES = 128
FACE = 96
CONST_ROWS = 16


def shifted(value, axis, steps):
    count = lax.axis_size(axis)
    pairs = [(source, (source + steps) % count) for source in range(count)]
    return lax.ppermute(value, axis, pairs)


def row_order(degree):
    points = degree + 1

    def natural(i, j, l):
        return (i * points + j) * points + l

    inner = range(degree)
    order = [natural(degree, j, l) for j in inner for l in inner]
    order += [natural(degree, degree, l) for l in inner]
    order += [natural(degree, j, degree) for j in inner]
    order += [natural(degree, degree, degree)] + [-1] * (degree - 1)
    order += [natural(i, j, l) for i in inner for j in inner for l in inner]
    order += [natural(i, degree, l) for i in inner for l in inner]
    order += [natural(i, j, degree) for i in inner for j in inner]
    order += [natural(i, degree, degree) for i in inner]
    used = len(order)
    order += [-1] * (-used % 256)
    return np.asarray(order, np.int32), used


def dot(a, b):
    return jnp.dot(a, b, preferred_element_type=f32)


def dot_nt(a, b):
    return lax.dot_general(a, b, (((1,), (1,)), ((), ())), preferred_element_type=f32)


def onehot_rows(perm, count):
    return (perm == lax.broadcasted_iota(jnp.int32, (perm.shape[0], count), 1)).astype(bf16)


class Mesh1:
    def __init__(self, degree, channels, used, padded):
        self.d = degree
        self.e = 2 * degree
        self.plane = self.e * self.e
        self.nodes = self.e * self.plane
        self.ch = channels
        self.face_groups = degree + 3
        self.used = used
        self.padded = padded

    def far(self, index):
        return (1 - index) * self.d

    def aligned(self, value):
        return value if isinstance(value, int) else pl.multiple_of(value, self.d)

    def face_places(self, base, a, b):
        d, e = self.d, self.e
        near = base + a * d * e + b * d
        places = [(self.aligned(near + j * e), 1) for j in range(d)]
        places.append((self.aligned(base + self.far(a) * e + b * d), 1))
        places.append((base + a * d * e + self.far(b), e))
        places.append((self.aligned(base + self.far(a) * e + self.far(b)), 0))
        return places

    def layer_places(self, base, a, b):
        d, e, plane = self.d, self.e, self.plane
        near = base + a * d * e + b * d
        places = [(self.aligned(near + i * plane + j * e), 1) for i in range(d) for j in range(d)]
        places += [
            (self.aligned(base + i * plane + self.far(a) * e + b * d), 1) for i in range(d)
        ]
        places += [(base + i * plane + a * d * e + self.far(b), e) for i in range(d)]
        places.append((base + self.far(a) * e + self.far(b), plane))
        return places

    def take(self, ref, place):
        start, stride = place
        if stride > 1:
            return ref[pl.ds(start, self.d, stride=stride), :]
        value = ref[pl.ds(start, self.d), :]
        if stride == 0:
            first = lax.broadcasted_iota(jnp.int32, value.shape, 0) == 0
            value = jnp.where(first, value, 0.0)
        return value

    def put_add(self, ref, place, value):
        start, stride = place
        if stride > 1:
            rows = pl.ds(start, self.d, stride=stride)
        else:
            rows = pl.ds(start, self.d)
            if stride == 0:
                first = lax.broadcasted_iota(jnp.int32, value.shape, 0) == 0
                value = jnp.where(first, value, 0.0)
        ref[rows, :] = ref[rows, :] + value

    def pack(self, ref, lane, groups, first_row=0):
        lanes = pl.ds(lane, LANES)
        for at in range(0, len(groups), 2):
            pair = jnp.concatenate([groups[at], groups[at + 1]], axis=0).astype(bf16)
            ref[pl.ds(first_row + at * self.d, 2 * self.d), lanes] = pair

    def gather_element(self, slab, ref, lane, base, a, b, with_face):
        d = self.d
        zero = jnp.zeros((d, LANES), f32)
        if with_face:
            groups = [self.take(slab, p) for p in self.face_places(base + d * self.plane, a, b)]
        else:
            groups = [zero] * self.face_groups
        groups += [self.take(slab, p) for p in self.layer_places(base, a, b)]
        groups += [zero] * ((self.padded - self.used) // d)
        self.pack(ref, lane, groups)

    def gather_face(self, slab, ref, lane, base, a, b):
        zero = jnp.zeros((self.d, LANES), f32)
        groups = [self.take(slab, p) for p in self.face_places(base, a, b)]
        groups += [zero] * (LANES // self.d - len(groups))
        self.pack(ref, lane, groups)

    def add_face(self, ref, base, a, b, load):
        for g, place in enumerate(self.face_places(base, a, b)):
            self.put_add(ref, place, load(g))

    def add_layer(self, ref, base, a, b, load, start=0):
        for g, place in enumerate(self.layer_places(base, a, b)):
            if g >= start:
                self.put_add(ref, place, load(self.face_groups + g))


def live_weights(kb, count):
    lane = lax.broadcasted_iota(jnp.int32, kb.shape, 1)
    return kb * jnp.where(lane < count, 1.0, 0.0)


def as_column(row):
    size = row.shape[1]
    shape = (size, size)
    eye = lax.broadcasted_iota(jnp.int32, shape, 0) == lax.broadcasted_iota(jnp.int32, shape, 1)
    return jnp.sum(jnp.where(eye, jnp.broadcast_to(row, shape), 0.0), axis=1, keepdims=True)


def split_element(column):
    return column // 2, column % 2


def outgoing(g, acol, ucol, scale, slab, x, kface, both_t, face_sums, up, down, own_out, held_out):
    d, ch = g.d, g.ch
    half = 4 * LANES
    own = dot(both_t[ch:, :], x[:, pl.ds(pl.multiple_of(half + acol * LANES, LANES), LANES)])
    held = dot(both_t[:ch, :], x[:, pl.ds(pl.multiple_of(ucol * LANES, LANES), LANES)])
    own_out[...] = own
    held_out[...] = held
    sums = dot(kface, x[:, half:])
    face_sums[...] = jnp.zeros_like(face_sums)
    for a in range(2):
        for b in range(2):
            lane = (a * 2 + b) * LANES
            part = sums[:, lane : lane + LANES] * scale[1, a, b]
            g.add_face(face_sums, 0, a, b, lambda k: part[k * d : (k + 1) * d])
    up[: g.plane, :] = face_sums[...].astype(bf16)
    up[g.plane : g.plane + ch, :] = own.astype(bf16)
    down[: g.plane, :] = slab[: g.plane, :].astype(bf16)
    down[g.plane :, :] = held.astype(bf16)


def gather_all(g, slab, x):
    for a in range(2):
        for b in range(2):
            lane = (a * 2 + b) * LANES
            g.gather_element(slab, x, lane, 0, a, b, True)
            g.gather_element(slab, x, 4 * LANES + lane, g.d * g.plane, a, b, False)


def start_kernel(
    g, acol, ucol, count, scale, wave, mass, perm, stiff, plow, pup, kb,
    slab, x, mass_wide, both, both_t, own_out, held_out, up, down, face_sums,
):
    ch = g.ch
    mass_t = mass[...].T
    for p in range(g.e):
        wide = jnp.broadcast_to(mass_t[:, p : p + 1], (g.plane, LANES))
        rows = pl.ds(p * g.plane, g.plane)
        mass_wide[rows, :] = wide
        start = wave[p].astype(f32).reshape(g.plane, LANES)
        slab[rows, :] = (wide * start).astype(bf16).astype(f32)
    pick = onehot_rows(perm[...], stiff.shape[0])
    pair = jnp.concatenate([pup[0], plow[0]], axis=1)
    ordered = dot(pick, pair).astype(bf16)
    both[...] = ordered
    turned = ordered.astype(f32).T.astype(bf16)
    both_t[...] = turned
    kface = dot_nt(dot(pick[:FACE], stiff[...]).astype(bf16), pick).astype(bf16)
    gather_all(g, slab, x)
    outgoing(g, acol[0], ucol[0], scale, slab, x, kface, both_t, face_sums, up, down, own_out, held_out)
    at = g.plane + ch
    up[at : at + FACE, :] = jnp.zeros((FACE, LANES), bf16)
    up[at : at + FACE, :ch] = ordered[:FACE, ch:]
    shape = (CONST_ROWS, LANES)
    row = lax.broadcasted_iota(jnp.int32, shape, 0)
    values = jnp.zeros(shape, f32)
    for k in range(4):
        chosen = jnp.where(acol[0] == k, 1.0, 0.0)
        values = jnp.where(row == k, chosen, values)
        full = jnp.full(shape, scale[1, k // 2, k % 2], f32)
        high = full.astype(bf16).astype(f32)
        values = jnp.where(row == 4 + k, high, values)
        values = jnp.where(row == 8 + k, full - high, values)
    weights = live_weights(kb[...], count[0])
    weights = jnp.concatenate([weights, jnp.zeros((1, LANES - ch), f32)], axis=1)
    full = jnp.broadcast_to(weights, shape)
    high = full.astype(bf16).astype(f32)
    values = jnp.where(row == 12, high, values)
    values = jnp.where(row == 13, full - high, values)
    up[at + FACE :, :] = values.astype(bf16)


def order_kernel(stiff, perm, ordered):
    pick = onehot_rows(perm[...], stiff.shape[0])
    part = perm.shape[0] // 3
    for k in range(3):
        rows = slice(k * part, (k + 1) * part)
        half = dot(pick[rows], stiff[...]).astype(bf16)
        ordered[rows, :] = dot_nt(half, pick).astype(bf16)


def bulk_kernel(g, scale, ordered, x, slab, potential, total, face_own, x_face, z):
    d = g.d
    pot_t = potential[...].T
    for p in range(g.e):
        wide = jnp.broadcast_to(pot_t[:, p : p + 1], (g.plane, LANES))
        rows = pl.ds(p * g.plane, g.plane)
        total[rows, :] = wide * slab[rows, :]
    for layer in range(2):
        for a in range(2):
            lane = (layer * 2 + a) * 2 * LANES
            z[...] = dot(ordered[: g.used, :], x[:, lane : lane + 2 * LANES])
            for b in range(2):
                factor = scale[layer, a, b]

                def load(k):
                    return z[k * d : (k + 1) * d, b * LANES : (b + 1) * LANES] * factor

                base = layer * d * g.plane
                if layer == 0:
                    g.add_face(total, d * g.plane, a, b, load)
                g.add_layer(total, base, a, b, load)
    for a in range(2):
        for b in range(2):
            g.gather_face(slab, x_face, (a * 2 + b) * LANES, 0, a, b)
    face_own[...] = dot(ordered[:FACE, :LANES], x_face[...])


def complete(
    g, acol, ucol, count, scale, total, face_own, x_face, ordered, both, both_t, own, held, kb,
    face_low, consts, up, down, sums, next_plane, x_next,
):
    d, ch = g.d, g.ch
    next_plane[...] = down[: g.plane, :].astype(f32)
    for a in range(2):
        for b in range(2):
            g.gather_face(next_plane, x_next, (a * 2 + b) * LANES, 0, a, b)
    mine = own[...] + down[g.plane :, :].astype(f32)
    column = pl.ds(pl.multiple_of(acol * LANES, LANES), LANES)
    mine = mine + dot(both_t[ch:, :LANES], x_next[:, column])
    mine = (as_column(live_weights(kb[...], count)) * mine).astype(bf16)
    const = consts.astype(f32)
    one_hot = [const[k : k + 1, :] for k in range(4)]
    scale_low = [const[4 + k : 5 + k, :] + const[8 + k : 9 + k, :] for k in range(4)]
    weights_low = as_column(const[12:13, :ch] + const[13:14, :ch])
    low = up[g.plane : g.plane + ch, :].astype(f32) + held[...]
    low = low + dot_chosen(face_low, x_face, one_hot)
    low = (weights_low * low).astype(bf16)
    lifted_low = dot(face_low, low)
    upper = dot(ordered[: g.used, :LANES], x_next[...])
    lifted = dot(both[: g.used, ch:], mine)
    half = d * g.plane
    sums[:half, :] = total[:half, :]
    for a in range(2):
        for b in range(2):
            lane = (a * 2 + b) * LANES
            here = jnp.where(acol == a * 2 + b, 1.0, 0.0)
            factor = scale[1, a, b]

            def load(k):
                rows = slice(k * d, (k + 1) * d)
                return upper[rows, lane : lane + LANES] * factor + lifted[rows] * here

            near = half + a * d * g.e + b * d
            for i in range(d):
                for j in range(d):
                    rows = pl.ds(near + i * g.plane + j * g.e, d)
                    sums[rows, :] = total[rows, :] + load(g.face_groups + i * d + j)
    for a in range(2):
        for b in range(2):
            lane = (a * 2 + b) * LANES
            here = jnp.where(acol == a * 2 + b, 1.0, 0.0)
            factor = scale[1, a, b]

            def load(k):
                rows = slice(k * d, (k + 1) * d)
                return upper[rows, lane : lane + LANES] * factor + lifted[rows] * here

            g.add_layer(sums, half, a, b, load, start=d * d)
    sums[: g.plane, :] = sums[: g.plane, :] + up[: g.plane, :].astype(f32)
    for a in range(2):
        for b in range(2):
            k4 = a * 2 + b
            part = face_own[:, k4 * LANES : (k4 + 1) * LANES] * scale_low[k4]
            part = part + lifted_low * one_hot[k4]
            g.add_face(sums, 0, a, b, lambda k: part[k * d : (k + 1) * d])
    lifted_up = dot(both[: g.used, :ch], low)
    a, b = split_element(ucol)

    def load_up(k):
        return lifted_up[k * d : (k + 1) * d]

    g.add_face(sums, half, a, b, load_up)
    g.add_layer(sums, 0, a, b, load_up)


def dot_chosen(face, x_face, one_hot):
    rows = face.shape[0]
    chosen = jnp.zeros((rows, LANES), f32)
    for k in range(4):
        chosen = chosen + x_face[:rows, k * LANES : (k + 1) * LANES].astype(f32) * one_hot[k]
    face_t = face.astype(f32).T.astype(bf16)
    return dot(face_t, chosen.astype(bf16))


def middle_kernel(
    g, acol, ucol, count, scale, wave, mass_wide, total, face_own, x_face, ordered, both, both_t,
    own, held, kb, up, down,
    slab, x, step, own_out, held_out, up_out, down_out,
    sums, next_plane, x_next, face_sums,
):
    at = g.plane + g.ch
    complete(
        g, acol[0], ucol[0], count[0], scale, total, face_own, x_face, ordered, both, both_t, own, held, kb,
        up[at : at + FACE, : g.ch], up[at + FACE :, :], up, down, sums, next_plane, x_next,
    )
    for p in range(g.e):
        rows = pl.ds(p * g.plane, g.plane)
        wide = mass_wide[rows, :]
        before = wave[p].astype(f32).reshape(g.plane, LANES)
        image = wide * sums[rows, :]
        one = ((image - spectrum_center * before) * (1.0 / spectrum_half)).astype(bf16)
        step[rows, :] = one
        slab[rows, :] = (wide * one.astype(f32)).astype(bf16).astype(f32)
    gather_all(g, slab, x)
    outgoing(
        g, acol[0], ucol[0], scale, slab, x, ordered[:FACE, :], both_t, face_sums, up_out, down_out,
        own_out, held_out,
    )


def last_kernel(
    g, acol, ucol, count, scale, wave, mass_wide, total, face_own, x_face, ordered, both, both_t,
    own, held, kb, up_first, up, down, step,
    filtered, own_out, held_out,
    sums, next_plane, x_next, x_pair,
):
    at = g.plane + g.ch
    d, ch = g.d, g.ch
    face_low = up_first[at : at + FACE, :ch]
    consts = up_first[at + FACE :, :]
    complete(
        g, acol[0], ucol[0], count[0], scale, total, face_own, x_face, ordered, both, both_t, own, held, kb,
        face_low, consts, up, down, sums, next_plane, x_next,
    )
    for p in range(g.e):
        rows = pl.ds(p * g.plane, g.plane)
        before = wave[p].astype(f32).reshape(g.plane, LANES)
        image = mass_wide[rows, :] * sums[rows, :]
        one = step[rows, :].astype(f32)
        new = (image - spectrum_center * one) * (2.0 / spectrum_half) - before
        new = new.astype(bf16)
        filtered[p] = new.reshape(g.e, g.e, LANES)
        sums[rows, :] = new.astype(f32)
    a, b = split_element(acol[0])
    g.gather_element(sums, x_pair, 0, d * g.plane, a, b, False)
    own_out[...] = dot(both_t[ch:, :], x_pair[:, :LANES])
    a, b = split_element(ucol[0])
    g.gather_element(sums, x_pair, LANES, 0, a, b, True)
    for a in range(2):
        for b in range(2):
            g.gather_face(sums, x_next, (a * 2 + b) * LANES, 0, a, b)
    const = consts.astype(f32)
    one_hot = [const[k : k + 1, :] for k in range(4)]
    held_out[...] = dot(both_t[:ch, :], x_pair[:, LANES:]) + dot_chosen(face_low, x_next, one_hot)


def call(kernel, name, operands, outs, scratch, flops, limit=24 << 20):
    smem = pl.BlockSpec(memory_space=pltpu.SMEM)
    vmem = pl.BlockSpec(memory_space=pltpu.VMEM)
    specs = [smem if value.ndim == 1 or value.shape == (2, 2, 2) else vmem for value in operands]
    moved = sum(v.size * v.dtype.itemsize for v in operands)
    return pl.pallas_call(
        kernel,
        name=name,
        out_shape=[jax.ShapeDtypeStruct(s, t) for s, t in outs],
        in_specs=specs,
        out_specs=[vmem] * len(outs),
        scratch_shapes=[pltpu.VMEM(s, t) for s, t in scratch],
        compiler_params=pltpu.CompilerParams(vmem_limit_bytes=limit),
        cost_estimate=pl.CostEstimate(flops=flops, bytes_accessed=moved, transcendentals=0),
    )(*operands)


def per_device(
    wave_in, mass_scale, potential, elem_scale, stiffness, proj_lower, proj_upper, kb_coef,
    atom_column, chan_count, upper_column,
):
    extent = wave_in.shape[0]
    degree = extent // 2
    ch = kb_coef.shape[-1]
    order, used = row_order(degree)
    padded = order.shape[0]
    perm = jnp.asarray(order)[:, None]
    g = Mesh1(degree, ch, used, padded)
    plane, nodes = g.plane, g.nodes
    scalars = (atom_column, upper_column, chan_count, elem_scale)
    part = ((ch, LANES), f32)
    slab_s, x_s = ((nodes, LANES), f32), ((padded, 8 * LANES), bf16)
    down_s, up_s = ((plane + ch, LANES), bf16), ((plane + ch, LANES), bf16)
    up_first_s = ((plane + ch + FACE + CONST_ROWS, LANES), bf16)
    plane_s, face_s = ((plane, LANES), f32), ((LANES, 4 * LANES), bf16)

    slab, x, mass_wide, both, both_t, own, held, up, down = call(
        functools.partial(start_kernel, g), "start",
        (*scalars, wave_in, mass_scale, perm, stiffness, proj_lower, proj_upper, kb_coef),
        [slab_s, x_s, slab_s, ((padded, 2 * ch), bf16), ((2 * ch, padded), bf16), part, part, up_first_s, down_s],
        [plane_s], 10**8,
    )
    up_first = shifted(up, "space", 1)
    down = shifted(down, "space", -1)
    (ordered,) = call(order_kernel, "order", (stiffness, perm), [((padded, padded), bf16)], [], 2 * 10**9)

    def bulk(slab, x):
        return call(
            functools.partial(bulk_kernel, g), "bulk", (elem_scale, ordered, x, slab, potential),
            [slab_s, ((FACE, 4 * LANES), f32), face_s], [((used, 2 * LANES), f32)], 2 * 10**9,
        )

    total, face_own, x_face = bulk(slab, x)
    shared = (ordered, both, both_t)
    slab, x, step, own, held, up, down = call(
        functools.partial(middle_kernel, g), "middle",
        (*scalars, wave_in, mass_wide, total, face_own, x_face, *shared, own, held, kb_coef, up_first, down),
        [slab_s, x_s, ((nodes, LANES), bf16), part, part, up_s, down_s],
        [slab_s, plane_s, face_s, plane_s], 10**8,
    )
    up = shifted(up, "space", 1)
    down = shifted(down, "space", -1)
    total, face_own, x_face = bulk(slab, x)
    filtered, own, held = call(
        functools.partial(last_kernel, g), "last",
        (*scalars, wave_in, mass_wide, total, face_own, x_face, *shared, own, held, kb_coef, up_first, up, down, step),
        [(wave_in.shape, bf16), part, part],
        [slab_s, plane_s, face_s, ((padded, 2 * LANES), bf16)], 10**8,
    )
    return filtered, (own + shifted(held, "space", -1))[None]


def solution(mesh):
    in_specs = (
        P("space", None, None, "band"),
        P("space", None),
        P("space", None),
        P("space", None, None),
        P(),
        P("space", None, None),
        P("space", None, None),
        P("space", None),
        P("space"),
        P("space"),
        P("space"),
    )
    out_specs = (P("space", None, None, "band"), P("space", None, "band"))
    return jax.shard_map(
        per_device, mesh=mesh, in_specs=in_specs, out_specs=out_specs, check_vma=False
    )
```

time: 116 us -> 44.6 us (0.38); the launches traced: 114 us -> 44.1 us
  local copies, waits for them, and re-layouts: 46.1 us -> 7.47 us
  waiting for transfers between devices: 26.3 us -> 3.61 us
  other arithmetic: 19 us -> 0.61 us
  Pallas kernels: 0 us -> 15.7 us
  matrix products: 11.7 us -> 0 us
  starting transfers between devices: 6.82 us -> 14.1 us
    ppermute x10 -> x5, waiting for transfers between devices: 26.3 us -> 3.61 us  [shifted(): return lax.ppermute(value, axis, pairs)]
    another operation x28 -> x0, local copies, waits for them, and re-layouts: 19.2 us -> none  [layer_blocks(): return jnp.stack(gathered)]
    pallas_call x0 -> x6, Pallas kernels: none -> 15.7 us  [call(): pl.pallas_call(kernel, name=name, out_shape=[jax.ShapeDtypeStruct(s, t) f...]
    slice x29 -> x0, local copies, waits for them, and re-layouts: 14.3 us -> none  [the longest x2 4.61 us: assemble_blocks(): grouped[:, :, 0]]
    dot_general x20 -> x0, matrix products: 11.7 us -> none  [the longest x2 4.93 us: operator(): jnp.einsum('ij,ejb->eib', stiffness, bottom_blocks, preferred_element_typ...]
    concatenate x13 -> x0, other arithmetic: 9.78 us -> none  [the longest x4 5.59 us: wrap_sides(): return jnp.concatenate([planes, planes[:, :, :1]], axis=2)]
    ppermute x10 -> x5, starting transfers between devices: 6.82 us -> 14.1 us  [shifted(): return lax.ppermute(value, axis, pairs)]
    convert_element_type x7 -> x0, other arithmetic: 5.78 us -> none  [the longest x1 1.75 us: per_device(): scaled_start = (mass_nodes * initial).astype(jnp.bfloat16)]
  transfers between devices with their start and end apart: 10 -> 5, of which waited for: 6 -> 2; matrix products, arithmetic and copies ran while one was open for 26% -> 0% of each run, Pallas kernels for 0% -> 16%
where the time goes in v1:
time: 44.6 us; the launch traced here: 44.1 us
  Pallas kernels  15.7 us (35%)
  starting transfers between devices  14.1 us (32%)
  local copies, waits for them, and re-layouts  7.47 us (17%)
  waiting for transfers between devices  3.61 us (8%)
  between operations  2.68 us (6%)
  other arithmetic  0.61 us (1%)
    pallas_call x6, Pallas kernels, call(): pl.pallas_call(kernel, name=name, out_shape=[jax.ShapeDtypeStruct(s, t) f...  15.7 us
    ppermute x5, starting transfers between devices, shifted(): return lax.ppermute(value, axis, pairs)  14.1 us
    unnamed x20, local copies, waits for them, and re-layouts  7.47 us
    ppermute x5, waiting for transfers between devices, shifted(): return lax.ppermute(value, axis, pairs)  3.61 us
  transfers between devices with their start and end apart: 5, of which 2 were waited for; matrix products, arithmetic and copies ran while one was open for 0% of the time, Pallas kernels for 16%

profile of v1, /device:TPU:0, one launch (start us, length us, event | category | flops | bytes accessed | tf_op | source)
XLA Modules:
  0.0 44.1 jit_solution(6000988791297459745)
XLA Ops:
  2.6 1.0 %copy.14.plow = bf16[1,729,32]{2,1,0:T(8,128)(2,1)S(1)} copy(bf16[1,729,32]{1,2,0:T(8,128)(2,1)} %param.17) | data formatting | bytes 93312 | tf_op args[5]
  3.5 1.0 %copy.15.pup = bf16[1,729,32]{2,1,0:T(8,128)(2,1)S(1)} copy(bf16[1,729,32]{1,2,0:T(8,128)(2,1)} %param.18) | data formatting | bytes 93312 | tf_op args[6]
  4.5 0.0 copy-start
  4.5 1.2 %copy-done = bf16[16,16,16,128]{3,2,1,0:T(8,128)(2,1)S(1)} copy-done((bf16[16,16,16,128]{3,2,1,0:T(8,128)(2,1)S(1)}, bf16[16,16,16,128]{3,2,1,0:T(8,128)(2,1)}, u32[]{:S(2)}) %copy-start) | copy-done | bytes 1048600
  5.7 0.0 copy-start.2
  5.7 1.3 %copy-done.2 = bf16[729,729]{1,0:T(8,128)(2,1)S(1)} copy-done((bf16[729,729]{1,0:T(8,128)(2,1)S(1)}, bf16[729,729]{1,0:T(8,128)(2,1)}, u32[]{:S(2)}) %copy-start.2) | copy-done | bytes 1062906
  7.0 0.0 copy-start.3
  7.0 1.0 %copy-done.3 = s32[768,1]{1,0:T(8,128)S(1)} copy-done((s32[768,1]{1,0:T(8,128)S(1)}, s32[768,1]{1,0:T(8,128)}, u32[]{:S(2)}) %copy-start.3) | copy-done | bytes 3096
  8.0 0.0 copy-start.4
  8.0 0.7 %copy-done.4 = f32[2,2,2]{2,1,0:T(2,128)S(1)} copy-done((f32[2,2,2]{2,1,0:T(2,128)S(1)}, f32[2,2,2]{2,1,0:T(2,128)}, u32[]{:S(2)}) %copy-start.4) | copy-done | bytes 56
  8.7 0.0 copy-start.5
  8.7 0.7 %copy-done.5 = f32[16,256]{1,0:T(8,128)S(1)} copy-done((f32[16,256]{1,0:T(8,128)S(1)}, f32[16,256]{1,0:T(8,128)}, u32[]{:S(2)}) %copy-start.5) | copy-done | bytes 16408
  9.4 0.0 copy-start.6
  9.4 0.7 %copy-done.6 = f32[1,32]{1,0:T(1,128)S(1)} copy-done((f32[1,32]{1,0:T(1,128)S(1)}, f32[1,32]{1,0:T(1,128)}, u32[]{:S(2)}) %copy-start.6) | copy-done | bytes 152
  10.0 2.3 %start.1 = (f32[4096,128]{1,0:T(8,128)S(1)}, bf16[768,1024]{1,0:T(8,128)(2,1)S(1)}, f32[4096,128]{1,0:T(8,128)S(1)}, bf16[768,64]{1,0:T(8,128)(2,1)S(1)}, bf16[6...) custom-call(s32[1]{0:T(128)S(6)} %copy.16.acol, ...), custom_call_target="tpu_custom_call" | custom-call | flops 100000000 | bytes 2224398 | tf_op jit(solution)/shard_map/start/pallas_call | solution.py:416
  12.3 5.5 %collective-permute-start.1 = (bf16[288,128]{1,0:T(8,128)(2,1)S(1)}, bf16[288,128]{1,0:T(8,128)(2,1)S(1)}, u32[]{:S(2)}, u32[]{:S(2)}) collective-permute-start(bf16[288,128]{1,0:T(8,128)(2,1)S(1)} %get-tuple-element.38), channel_id=1, source_target_pairs={{0,30},{2,0},{4,2},{6,4},{8,6},{10,8},{12,10},{14,12},{16,14},{18,... | collective-permute-start | bytes 221192 | tf_op jit(solution)/shard_map/ppermute | solution.py:23
  17.8 0.0 copy-start.8
  17.8 0.0 collective-permute-start
  17.8 2.2 %order.1.ordered = bf16[768,768]{1,0:T(8,128)(2,1)S(1)} custom-call(bf16[729,729]{1,0:T(8,128)(2,1)S(1)} %copy-done.2, s32[768,1]{1,0:T(8,128)S(1)} %copy-done.3), custom_call_target="tpu_custom_call" | custom-call | flops 2000000000 | bytes 1065954 | tf_op jit(solution)/shard_map/order/pallas_call | solution.py:416
  20.1 0.0 copy-done.8
  20.1 0.0 copy-start.1
  20.1 0.0 copy-start.7
  20.1 2.3 %bulk.2 = (f32[4096,128]{1,0:T(8,128)S(1)}, f32[96,512]{1,0:T(8,128)S(1)}, bf16[128,512]{1,0:T(8,128)(2,1)S(1)}) custom-call(f32[2,2,2]{2,1,0:T(2,128)S(1)} %copy-done.4, bf16[768,768]{1,0:T(8,128)(2,1)S(1)} %order.1.ordered, bf16[768,1024]{1,0:T(8,128)(2,1)S(1)} %get-tuple-element.28.x, f32[4096,128]{1,0:T(8,128)S(1)} %get-tuple-element.29.slab, ...), custom_call_target="tpu_custom_call" | custom-call | flops 2000000000 | bytes 4866080 | tf_op jit(solution)/shard_map/bulk/pallas_call | solution.py:416
  22.4 0.0 collective-permute-done.1.down
  22.4 2.2 %collective-permute-done.up.up_first = bf16[400,128]{1,0:T(8,128)(2,1)S(1)} collective-permute-done((bf16[400,128]{1,0:T(8,128)(2,1)S(1)}, bf16[400,128]{1,0:T(8,128)(2,1)S(1)}, u32[]{:S(2)}, u32[]{:S(2)}) %collective-permute-start) | collective-permute-done | bytes 102432 | tf_op jit(solution)/shard_map/ppermute | solution.py:23
  24.6 0.0 copy-done.1
  24.6 0.0 copy-done.7
  24.6 3.0 %middle.1 = (f32[4096,128]{1,0:T(8,128)S(1)}, bf16[768,1024]{1,0:T(8,128)(2,1)S(1)}, bf16[4096,128]{1,0:T(8,128)(2,1)S(1)}, f32[32,128]{1,0:T(8,128)S(1)}, f32[3...) custom-call(s32[1]{0:T(128)S(6)} %copy.16.acol, s32[1]{0:T(128)S(6)} %copy.18.ucol, ...), custom_call_target="tpu_custom_call" | custom-call | flops 100000000 | bytes 7155884 | tf_op jit(solution)/shard_map/middle/pallas_call | solution.py:416
  27.6 0.1 collective-permute-start.2
  27.7 4.4 %collective-permute-start.3 = (bf16[288,128]{1,0:T(8,128)(2,1)S(1)}, bf16[288,128]{1,0:T(8,128)(2,1)S(1)}, u32[]{:S(2)}, u32[]{:S(2)}) collective-permute-start(bf16[288,128]{1,0:T(8,128)(2,1)S(1)} %get-tuple-element.47), channel_id=1, source_target_pairs={{0,30},{2,0},{4,2},{6,4},{8,6},{10,8},{12,10},{14,12},{16,14},{18,... | collective-permute-start | bytes 221192 | tf_op jit(solution)/shard_map/ppermute | solution.py:23
  32.1 2.3 %bulk.3 = (f32[4096,128]{1,0:T(8,128)S(1)}, f32[96,512]{1,0:T(8,128)S(1)}, bf16[128,512]{1,0:T(8,128)(2,1)S(1)}) custom-call(f32[2,2,2]{2,1,0:T(2,128)S(1)} %copy-done.4, bf16[768,768]{1,0:T(8,128)(2,1)S(1)} %order.1.ordered, bf16[768,1024]{1,0:T(8,128)(2,1)S(1)} %get-tuple-element.39.x, f32[4096,128]{1,0:T(8,128)S(1)} %get-tuple-element.40.slab, ...), custom_call_target="tpu_custom_call" | custom-call | flops 2000000000 | bytes 4866080 | tf_op jit(solution)/shard_map/bulk/pallas_call | solution.py:416
  34.4 0.0 collective-permute-done.2.up
  34.5 0.0 collective-permute-done.3.down
  34.5 3.5 %last.1 = (bf16[16,16,16,128]{3,2,1,0:T(8,128)(2,1)}, f32[32,128]{1,0:T(8,128)S(1)}, f32[32,128]{1,0:T(8,128)S(1)}) custom-call(s32[1]{0:T(128)S(6)} %copy.16.acol, s32[1]{0:T(128)S(6)} %copy.18.ucol, s32[1]{0:T(128)S(6)} %copy.17.count, f32[2,2,2]{2,1,0:T(2,128)S(1)} %copy-done.4, bf16[16,16,16,128]{3,2,1,0:T(8,128)(2,1)S(1)} %copy-done.1, ...), custom_call_target="tpu_custom_call" | custom-call | flops 100000000 | bytes 8278188 | tf_op jit(solution)/shard_map/last/pallas_call | solution.py:416
  38.0 4.1 %collective-permute-start.4 = (f32[32,128]{1,0:T(8,128)S(1)}, f32[32,128]{1,0:T(8,128)S(1)}, u32[]{:S(2)}, u32[]{:S(2)}) collective-permute-start(f32[32,128]{1,0:T(8,128)S(1)} %get-tuple-element.51), channel_id=1, source_target_pairs={{0,30},{2,0},{4,2},{6,4},{8,6},{10,8},{12,10},{14,12},{16,14},{18,... | collective-permute-start | bytes 49160 | tf_op jit(solution)/shard_map/ppermute | solution.py:23
  42.1 1.4 %collective-permute-done.4 = f32[32,128]{1,0:T(8,128)S(1)} collective-permute-done((f32[32,128]{1,0:T(8,128)S(1)}, f32[32,128]{1,0:T(8,128)S(1)}, u32[]{:S(2)}, u32[]{:S(2)}) %collective-permute-start.4) | collective-permute-done | bytes 16416 | tf_op jit(solution)/shard_map/ppermute | solution.py:23
  43.5 0.6 %add_bitcast_fusion = f32[1,32,128]{2,1,0:T(8,128)} fusion(f32[32,128]{1,0:T(8,128)S(1)} %get-tuple-element.50, f32[32,128]{1,0:T(8,128)S(1)} %collective-permute-done.4), kind=kLoop, calls=%fused_computation | loop fusion | flops 4096 | bytes 49152 | tf_op jit(solution)/shard_map/broadcast_in_dim | solution.py:480
Async XLA Ops:
  4.5 1.2 %copy-start = (bf16[16,16,16,128]{3,2,1,0:T(8,128)(2,1)S(1)}, bf16[16,16,16,128]{3,2,1,0:T(8,128)(2,1)}, u32[]{:S(2)}) copy-start(bf16[16,16,16,128]{3,2,1,0:T(8,128)(2,1)} %wave.5) | copy-start | bytes 3145732
  5.7 1.3 %copy-start.2 = (bf16[729,729]{1,0:T(8,128)(2,1)S(1)}, bf16[729,729]{1,0:T(8,128)(2,1)}, u32[]{:S(2)}) copy-start(bf16[729,729]{1,0:T(8,128)(2,1)} %stiff.3) | copy-start | bytes 3188650
  7.0 1.0 %copy-start.3 = (s32[768,1]{1,0:T(8,128)S(1)}, s32[768,1]{1,0:T(8,128)}, u32[]{:S(2)}) copy-start(s32[768,1]{1,0:T(8,128)} %constant.10.perm) | copy-start | bytes 9220
  8.0 0.7 %copy-start.4 = (f32[2,2,2]{2,1,0:T(2,128)S(1)}, f32[2,2,2]{2,1,0:T(2,128)}, u32[]{:S(2)}) copy-start(f32[2,2,2]{2,1,0:T(2,128)} %scale.9) | copy-start | bytes 100
  8.7 0.7 %copy-start.5 = (f32[16,256]{1,0:T(8,128)S(1)}, f32[16,256]{1,0:T(8,128)}, u32[]{:S(2)}) copy-start(f32[16,256]{1,0:T(8,128)} %mass.1) | copy-start | bytes 49156
  9.4 0.7 %copy-start.6 = (f32[1,32]{1,0:T(1,128)S(1)}, f32[1,32]{1,0:T(1,128)}, u32[]{:S(2)}) copy-start(f32[1,32]{1,0:T(1,128)} %kb.5) | copy-start | bytes 388
  12.3 10.1 %collective-permute-start.1 = (bf16[288,128]{1,0:T(8,128)(2,1)S(1)}, bf16[288,128]{1,0:T(8,128)(2,1)S(1)}, u32[]{:S(2)}, u32[]{:S(2)}) collective-permute-start(bf16[288,128]{1,0:T(8,128)(2,1)S(1)} %get-tuple-element.38), channel_id=1, source_target_pairs={{0,30},{2,0},{4,2},{6,4},{8,6},{10,8},{12,10},{14,12},{16,14},{18,... | collective-permute-start | bytes 221192 | tf_op jit(solution)/shard_map/ppermute | solution.py:23
  17.8 2.3 %copy-start.8 = (f32[16,256]{1,0:T(8,128)S(1)}, f32[16,256]{1,0:T(8,128)}, u32[]{:S(2)}) copy-start(f32[16,256]{1,0:T(8,128)} %potential.3) | copy-start | bytes 49156
  17.8 6.8 %collective-permute-start = (bf16[400,128]{1,0:T(8,128)(2,1)S(1)}, bf16[400,128]{1,0:T(8,128)(2,1)S(1)}, u32[]{:S(2)}, u32[]{:S(2)}) collective-permute-start(bf16[400,128]{1,0:T(8,128)(2,1)S(1)} %get-tuple-element.37), channel_id=1, source_target_pairs={{0,2},{2,4},{4,6},{6,8},{8,10},{10,12},{12,14},{14,16},{16,18},{18... | collective-permute-start | bytes 307208 | tf_op jit(solution)/shard_map/ppermute | solution.py:23
  20.1 4.5 %copy-start.1 = (bf16[16,16,16,128]{3,2,1,0:T(8,128)(2,1)S(1)}, bf16[16,16,16,128]{3,2,1,0:T(8,128)(2,1)}, u32[]{:S(2)}) copy-start(bf16[16,16,16,128]{3,2,1,0:T(8,128)(2,1)} %wave.5) | copy-start | bytes 3145732
  20.1 4.5 %copy-start.7 = (f32[1,32]{1,0:T(1,128)S(1)}, f32[1,32]{1,0:T(1,128)}, u32[]{:S(2)}) copy-start(f32[1,32]{1,0:T(1,128)} %kb.5) | copy-start | bytes 388
  27.6 6.8 %collective-permute-start.2 = (bf16[288,128]{1,0:T(8,128)(2,1)S(1)}, bf16[288,128]{1,0:T(8,128)(2,1)S(1)}, u32[]{:S(2)}, u32[]{:S(2)}) collective-permute-start(bf16[288,128]{1,0:T(8,128)(2,1)S(1)} %get-tuple-element.46), channel_id=1, source_target_pairs={{0,2},{2,4},{4,6},{6,8},{8,10},{10,12},{12,14},{14,16},{16,18},{18... | collective-permute-start | bytes 221192 | tf_op jit(solution)/shard_map/ppermute | solution.py:23
  27.7 6.8 %collective-permute-start.3 = (bf16[288,128]{1,0:T(8,128)(2,1)S(1)}, bf16[288,128]{1,0:T(8,128)(2,1)S(1)}, u32[]{:S(2)}, u32[]{:S(2)}) collective-permute-start(bf16[288,128]{1,0:T(8,128)(2,1)S(1)} %get-tuple-element.47), channel_id=1, source_target_pairs={{0,30},{2,0},{4,2},{6,4},{8,6},{10,8},{12,10},{14,12},{16,14},{18,... | collective-permute-start | bytes 221192 | tf_op jit(solution)/shard_map/ppermute | solution.py:23
  38.0 5.5 %collective-permute-start.4 = (f32[32,128]{1,0:T(8,128)S(1)}, f32[32,128]{1,0:T(8,128)S(1)}, u32[]{:S(2)}, u32[]{:S(2)}) collective-permute-start(f32[32,128]{1,0:T(8,128)S(1)} %get-tuple-element.51), channel_id=1, source_target_pairs={{0,30},{2,0},{4,2},{6,4},{8,6},{10,8},{12,10},{14,12},{16,14},{18,... | collective-permute-start | bytes 49160 | tf_op jit(solution)/shard_map/ppermute | solution.py:23

commit v2 on v1

--- a/solution.py
+++ b/solution.py
@@ -21,6 +21,41 @@
     count = lax.axis_size(axis)
     pairs = [(source, (source + steps) % count) for source in range(count)]
     return lax.ppermute(value, axis, pairs)
+
+
+def swapped(inner, outer, axis):
+    count = lax.axis_size(axis)
+    within = [(source, source ^ 1) for source in range(count)]
+    across = [(source, (source + (1 if source % 2 else -1)) % count) for source in range(count)]
+    return lax.ppermute(inner, axis, within), lax.ppermute(outer, axis, across)
+
+
+def is_odd():
+    return lax.rem(lax.axis_index("space"), 2) == 1
+
+
+def post(up, down, inner, outer):
+    @pl.when(is_odd())
+    def _():
+        inner[: down.shape[0], :] = down[...]
+        outer[: up.shape[0], :] = up[...]
+
+    @pl.when(jnp.logical_not(is_odd()))
+    def _():
+        inner[: up.shape[0], :] = up[...]
+        outer[: down.shape[0], :] = down[...]
+
+
+def collect(inner, outer, up, down):
+    @pl.when(is_odd())
+    def _():
+        up[...] = inner[: up.shape[0], :]
+        down[...] = outer[: down.shape[0], :]
+
+    @pl.when(jnp.logical_not(is_odd()))
+    def _():
+        up[...] = outer[: up.shape[0], :]
+        down[...] = inner[: down.shape[0], :]
 
 
 def row_order(degree):
@@ -52,7 +87,10 @@
 
 
 def onehot_rows(perm, count):
-    return (perm == lax.broadcasted_iota(jnp.int32, (perm.shape[0], count), 1)).astype(bf16)
+    rows = perm.shape[1]
+    column = jnp.broadcast_to(perm, (8, rows)).T[:, :1]
+    lane = lax.broadcasted_iota(jnp.int32, (rows, count), 1).astype(f32)
+    return (column == lane).astype(bf16)
 
 
 class Mesh1:
@@ -174,7 +212,7 @@
     for a in range(2):
         for b in range(2):
             lane = (a * 2 + b) * LANES
-            part = sums[:, lane : lane + LANES] * scale[1, a, b]
+            part = sums[:, lane : lane + LANES] * scale[4 + a * 2 + b : 5 + a * 2 + b, :]
             g.add_face(face_sums, 0, a, b, lambda k: part[k * d : (k + 1) * d])
     up[: g.plane, :] = face_sums[...].astype(bf16)
     up[g.plane : g.plane + ch, :] = own.astype(bf16)
@@ -191,10 +229,22 @@
 
 
 def start_kernel(
-    g, acol, ucol, count, scale, wave, mass, perm, stiff, plow, pup, kb,
-    slab, x, mass_wide, both, both_t, own_out, held_out, up, down, face_sums,
+    g, acol, ucol, count, wave_hbm, mass_hbm, scale_hbm, stiff_hbm, low_hbm, up_hbm, kb_hbm, perm_hbm, pot_hbm,
+    slab, x, mass_wide, wave, stiff, scale, perm, pot, kb, both, both_t, own_out, held_out, inner, outer,
+    face_sums, up, down, mass, scale_in, proj, sems,
 ):
     ch = g.ch
+    copies = [
+        pltpu.make_async_copy(source, target, sems.at[k])
+        for k, (source, target) in enumerate((
+            (mass_hbm, mass), (wave_hbm, wave), (up_hbm.at[0], proj.at[:ch]), (low_hbm.at[0], proj.at[ch:]),
+            (perm_hbm, perm), (stiff_hbm, stiff), (scale_hbm, scale_in), (kb_hbm, kb), (pot_hbm, pot),
+        ))
+    ]
+    for copy in copies:
+        copy.start()
+    copies[0].wait()
+    copies[1].wait()
     mass_t = mass[...].T
     for p in range(g.e):
         wide = jnp.broadcast_to(mass_t[:, p : p + 1], (g.plane, LANES))
@@ -202,14 +252,18 @@
         mass_wide[rows, :] = wide
         start = wave[p].astype(f32).reshape(g.plane, LANES)
         slab[rows, :] = (wide * start).astype(bf16).astype(f32)
+    gather_all(g, slab, x)
+    for copy in copies[2:]:
+        copy.wait()
+    for k in range(8):
+        one = scale_in[k // 4, k % 4 // 2 : k % 4 // 2 + 1, k % 2 : k % 2 + 1]
+        scale[k : k + 1, :] = jnp.broadcast_to(one, (1, LANES))
     pick = onehot_rows(perm[...], stiff.shape[0])
-    pair = jnp.concatenate([pup[0], plow[0]], axis=1)
-    ordered = dot(pick, pair).astype(bf16)
+    ordered = dot_nt(proj[...], pick)
+    both_t[...] = ordered.astype(bf16)
+    ordered = ordered.T.astype(bf16)
     both[...] = ordered
-    turned = ordered.astype(f32).T.astype(bf16)
-    both_t[...] = turned
     kface = dot_nt(dot(pick[:FACE], stiff[...]).astype(bf16), pick).astype(bf16)
-    gather_all(g, slab, x)
     outgoing(g, acol[0], ucol[0], scale, slab, x, kface, both_t, face_sums, up, down, own_out, held_out)
     at = g.plane + ch
     up[at : at + FACE, :] = jnp.zeros((FACE, LANES), bf16)
@@ -220,7 +274,7 @@
     for k in range(4):
         chosen = jnp.where(acol[0] == k, 1.0, 0.0)
         values = jnp.where(row == k, chosen, values)
-        full = jnp.full(shape, scale[1, k // 2, k % 2], f32)
+        full = jnp.broadcast_to(scale[4 + k : 5 + k, :], shape)
         high = full.astype(bf16).astype(f32)
         values = jnp.where(row == 4 + k, high, values)
         values = jnp.where(row == 8 + k, full - high, values)
@@ -231,11 +285,12 @@
     values = jnp.where(row == 12, high, values)
     values = jnp.where(row == 13, full - high, values)
     up[at + FACE :, :] = values.astype(bf16)
+    post(up, down, inner, outer)
 
 
 def order_kernel(stiff, perm, ordered):
     pick = onehot_rows(perm[...], stiff.shape[0])
-    part = perm.shape[0] // 3
+    part = perm.shape[1] // 3
     for k in range(3):
         rows = slice(k * part, (k + 1) * part)
         half = dot(pick[rows], stiff[...]).astype(bf16)
@@ -254,7 +309,7 @@
             lane = (layer * 2 + a) * 2 * LANES
             z[...] = dot(ordered[: g.used, :], x[:, lane : lane + 2 * LANES])
             for b in range(2):
-                factor = scale[layer, a, b]
+                factor = scale[layer * 4 + a * 2 + b : layer * 4 + a * 2 + b + 1, :]
 
                 def load(k):
                     return z[k * d : (k + 1) * d, b * LANES : (b + 1) * LANES] * factor
@@ -298,7 +353,7 @@
         for b in range(2):
             lane = (a * 2 + b) * LANES
             here = jnp.where(acol == a * 2 + b, 1.0, 0.0)
-            factor = scale[1, a, b]
+            factor = scale[4 + a * 2 + b : 5 + a * 2 + b, :]
 
             def load(k):
                 rows = slice(k * d, (k + 1) * d)
@@ -313,7 +368,7 @@
         for b in range(2):
             lane = (a * 2 + b) * LANES
             here = jnp.where(acol == a * 2 + b, 1.0, 0.0)
-            factor = scale[1, a, b]
+            factor = scale[4 + a * 2 + b : 5 + a * 2 + b, :]
 
             def load(k):
                 rows = slice(k * d, (k + 1) * d)
@@ -348,11 +403,13 @@
 
 def middle_kernel(
     g, acol, ucol, count, scale, wave, mass_wide, total, face_own, x_face, ordered, both, both_t,
-    own, held, kb, up, down,
-    slab, x, step, own_out, held_out, up_out, down_out,
-    sums, next_plane, x_next, face_sums,
+    own, held, kb, inner, outer,
+    slab, x, step, own_out, held_out, inner_out, outer_out, kept,
+    sums, next_plane, x_next, face_sums, up, down, up_out, down_out,
 ):
     at = g.plane + g.ch
+    collect(inner, outer, up, down)
+    kept[...] = up[at:, :]
     complete(
         g, acol[0], ucol[0], count[0], scale, total, face_own, x_face, ordered, both, both_t, own, held, kb,
         up[at : at + FACE, : g.ch], up[at + FACE :, :], up, down, sums, next_plane, x_next,
@@ -370,18 +427,19 @@
         g, acol[0], ucol[0], scale, slab, x, ordered[:FACE, :], both_t, face_sums, up_out, down_out,
         own_out, held_out,
     )
+    post(up_out, down_out, inner_out, outer_out)
 
 
 def last_kernel(
     g, acol, ucol, count, scale, wave, mass_wide, total, face_own, x_face, ordered, both, both_t,
-    own, held, kb, up_first, up, down, step,
+    own, held, kb, kept, inner, outer, step,
     filtered, own_out, held_out,
-    sums, next_plane, x_next, x_pair,
+    sums, next_plane, x_next, x_pair, up, down,
 ):
-    at = g.plane + g.ch
     d, ch = g.d, g.ch
-    face_low = up_first[at : at + FACE, :ch]
-    consts = up_first[at + FACE :, :]
+    collect(inner, outer, up, down)
+    face_low = kept[:FACE, :ch]
+    consts = kept[FACE:, :]
     complete(
         g, acol[0], ucol[0], count[0], scale, total, face_own, x_face, ordered, both, both_t, own, held, kb,
         face_low, consts, up, down, sums, next_plane, x_next,
@@ -408,21 +466,23 @@
     held_out[...] = dot(both_t[:ch, :], x_pair[:, LANES:]) + dot_chosen(face_low, x_next, one_hot)
 
 
-def call(kernel, name, operands, outs, scratch, flops, limit=24 << 20):
+def call(kernel, name, scalars, operands, outs, scratch, flops, limit=24 << 20, hbm=False):
     smem = pl.BlockSpec(memory_space=pltpu.SMEM)
     vmem = pl.BlockSpec(memory_space=pltpu.VMEM)
-    specs = [smem if value.ndim == 1 or value.shape == (2, 2, 2) else vmem for value in operands]
+    far = pl.BlockSpec(memory_space=pltpu.MemorySpace.HBM)
     moved = sum(v.size * v.dtype.itemsize for v in operands)
+    if hbm:
+        operands = [pltpu.with_memory_space_constraint(v, pltpu.MemorySpace.HBM) for v in operands]
     return pl.pallas_call(
         kernel,
         name=name,
         out_shape=[jax.ShapeDtypeStruct(s, t) for s, t in outs],
-        in_specs=specs,
+        in_specs=[smem] * len(scalars) + [far if hbm else vmem] * len(operands),
         out_specs=[vmem] * len(outs),
-        scratch_shapes=[pltpu.VMEM(s, t) for s, t in scratch],
+        scratch_shapes=[s if isinstance(s, pltpu.SemaphoreType) or not isinstance(s, tuple) else pltpu.VMEM(*s) for s in scratch],
         compiler_params=pltpu.CompilerParams(vmem_limit_bytes=limit),
         cost_estimate=pl.CostEstimate(flops=flops, bytes_accessed=moved, transcendentals=0),
-    )(*operands)
+    )(*scalars, *operands)
 
 
 def per_device(
@@ -434,48 +494,50 @@
     ch = kb_coef.shape[-1]
     order, used = row_order(degree)
     padded = order.shape[0]
-    perm = jnp.asarray(order)[:, None]
+    perm = jnp.asarray(order, f32)[None, :]
     g = Mesh1(degree, ch, used, padded)
     plane, nodes = g.plane, g.nodes
-    scalars = (atom_column, upper_column, chan_count, elem_scale)
+    scalars = (atom_column, upper_column, chan_count)
     part = ((ch, LANES), f32)
     slab_s, x_s = ((nodes, LANES), f32), ((padded, 8 * LANES), bf16)
-    down_s, up_s = ((plane + ch, LANES), bf16), ((plane + ch, LANES), bf16)
-    up_first_s = ((plane + ch + FACE + CONST_ROWS, LANES), bf16)
+    wire_s = ((plane + ch, LANES), bf16)
+    wire_first_s = ((plane + ch + FACE + CONST_ROWS, LANES), bf16)
     plane_s, face_s = ((plane, LANES), f32), ((LANES, 4 * LANES), bf16)
 
-    slab, x, mass_wide, both, both_t, own, held, up, down = call(
-        functools.partial(start_kernel, g), "start",
-        (*scalars, wave_in, mass_scale, perm, stiffness, proj_lower, proj_upper, kb_coef),
-        [slab_s, x_s, slab_s, ((padded, 2 * ch), bf16), ((2 * ch, padded), bf16), part, part, up_first_s, down_s],
-        [plane_s], 10**8,
-    )
-    up_first = shifted(up, "space", 1)
-    down = shifted(down, "space", -1)
-    (ordered,) = call(order_kernel, "order", (stiffness, perm), [((padded, padded), bf16)], [], 2 * 10**9)
+    slab, x, mass_wide, wave, stiff, scale, order_row, pot, kb, both, both_t, own, held, inner, outer = call(
+        functools.partial(start_kernel, g), "start", scalars,
+        (wave_in, mass_scale, elem_scale, stiffness, jnp.swapaxes(proj_lower, 1, 2), jnp.swapaxes(proj_upper, 1, 2),
+         kb_coef, perm, potential),
+        [slab_s, x_s, slab_s, (wave_in.shape, bf16), (stiffness.shape, bf16), ((8, LANES), f32), (perm.shape, f32),
+         (potential.shape, f32), (kb_coef.shape, f32), ((padded, 2 * ch), bf16), ((2 * ch, padded), bf16), part, part,
+         wire_first_s, wire_first_s],
+        [plane_s, wire_first_s, wire_s, (mass_scale.shape, f32), (elem_scale.shape, f32),
+         ((2 * ch, stiffness.shape[0]), bf16), pltpu.SemaphoreType.DMA((9,))], 10**8, hbm=True,
+    )
+    inner, outer = swapped(inner, outer, "space")
+    (ordered,) = call(order_kernel, "order", (), (stiff, order_row), [((padded, padded), bf16)], [], 2 * 10**9)
 
     def bulk(slab, x):
         return call(
-            functools.partial(bulk_kernel, g), "bulk", (elem_scale, ordered, x, slab, potential),
+            functools.partial(bulk_kernel, g), "bulk", (), (scale, ordered, x, slab, pot),
             [slab_s, ((FACE, 4 * LANES), f32), face_s], [((used, 2 * LANES), f32)], 2 * 10**9,
         )
 
     total, face_own, x_face = bulk(slab, x)
     shared = (ordered, both, both_t)
-    slab, x, step, own, held, up, down = call(
-        functools.partial(middle_kernel, g), "middle",
-        (*scalars, wave_in, mass_wide, total, face_own, x_face, *shared, own, held, kb_coef, up_first, down),
-        [slab_s, x_s, ((nodes, LANES), bf16), part, part, up_s, down_s],
-        [slab_s, plane_s, face_s, plane_s], 10**8,
-    )
-    up = shifted(up, "space", 1)
-    down = shifted(down, "space", -1)
+    slab, x, step, own, held, inner, outer, kept = call(
+        functools.partial(middle_kernel, g), "middle", scalars,
+        (scale, wave, mass_wide, total, face_own, x_face, *shared, own, held, kb, inner, outer),
+        [slab_s, x_s, ((nodes, LANES), bf16), part, part, wire_s, wire_s, ((FACE + CONST_ROWS, LANES), bf16)],
+        [slab_s, plane_s, face_s, plane_s, wire_first_s, wire_s, wire_s, wire_s], 10**8,
+    )
+    inner, outer = swapped(inner, outer, "space")
     total, face_own, x_face = bulk(slab, x)
     filtered, own, held = call(
-        functools.partial(last_kernel, g), "last",
-        (*scalars, wave_in, mass_wide, total, face_own, x_face, *shared, own, held, kb_coef, up_first, up, down, step),
+        functools.partial(last_kernel, g), "last", scalars,
+        (scale, wave, mass_wide, total, face_own, x_face, *shared, own, held, kb, kept, inner, outer, step),
         [(wave_in.shape, bf16), part, part],
-        [slab_s, plane_s, face_s, ((padded, 2 * LANES), bf16)], 10**8,
+        [slab_s, plane_s, face_s, ((padded, 2 * LANES), bf16), wire_s, wire_s], 10**8,
     )
     return filtered, (own + shifted(held, "space", -1))[None]
 

time: 44.6 us -> 33.6 us (0.75)
  local copies, waits for them, and re-layouts: 7.47 us -> 0 us
  starting transfers between devices: 14.1 us -> 11.5 us
  Pallas kernels: 15.7 us -> 15.1 us
    ppermute x5 -> x1, starting transfers between devices: 14.1 us -> 2.57 us  [shifted(): return lax.ppermute(value, axis, pairs)]
    ppermute x0 -> x4, starting transfers between devices: none -> 8.89 us  [the longest x2 8.27 us: swapped(): lax.ppermute(outer, axis, across)]
    unnamed x20 -> x0, local copies, waits for them, and re-layouts: 7.47 us -> none
    ppermute x5 -> x1, waiting for transfers between devices: 3.61 us -> 1.44 us  [shifted(): return lax.ppermute(value, axis, pairs)]
    ppermute x0 -> x4, waiting for transfers between devices: none -> 2.09 us  [the longest x2 2.08 us: swapped(): lax.ppermute(outer, axis, across)]
    pallas_call x6, Pallas kernels: 15.7 us -> 15.1 us  [call(): pl.pallas_call(kernel, name=name, out_shape=[jax.ShapeDtypeStruct(s, t) f...]
  transfers between devices with their start and end apart: 5 -> 5, of which waited for: 2 -> 2; matrix products, arithmetic and copies ran while one was open for 0% -> 0% of each run, Pallas kernels for 16% -> 18%
where the time goes in v2:
time: 33.6 us; the launch traced here: 33.3 us
  Pallas kernels  15.1 us (45%)
  starting transfers between devices  11.5 us (34%)
  waiting for transfers between devices  3.53 us (11%)
  between operations  2.64 us (8%)
  other arithmetic  0.61 us (2%)
    pallas_call x6, Pallas kernels, call(): pl.pallas_call(kernel, name=name, out_shape=[jax.ShapeDtypeStruct(s, t) f...  15.1 us
    ppermute x2, starting transfers between devices, swapped(): lax.ppermute(outer, axis, across)  8.27 us
    ppermute x1, starting transfers between devices, shifted(): return lax.ppermute(value, axis, pairs)  2.57 us
    ppermute x2, waiting for transfers between devices, swapped(): lax.ppermute(outer, axis, across)  2.08 us
    ppermute x1, waiting for transfers between devices, shifted(): return lax.ppermute(value, axis, pairs)  1.44 us
  transfers between devices with their start and end apart: 5, of which 2 were waited for; matrix products, arithmetic and copies ran while one was open for 0% of the time, Pallas kernels for 18%

profile of v2, /device:TPU:0, one launch (start us, length us, event | category | flops | bytes accessed | tf_op | source)
XLA Modules:
  0.0 33.3 jit_solution(17413400431675827194)
XLA Ops:
  2.6 3.7 %start.1 = (f32[4096,128]{1,0:T(8,128)S(1)}, bf16[768,1024]{1,0:T(8,128)(2,1)S(1)}, f32[4096,128]{1,0:T(8,128)S(1)}, bf16[16,16,16,128]{3,2,1,0:T(8,128)(2,1)S(1...) custom-call(s32[1]{0:T(128)S(6)} %copy.14.acol, ...), custom_call_target="tpu_custom_call" | custom-call | flops 100000000 | bytes 2240770 | tf_op jit(solution)/shard_map/start/pallas_call | solution.py:476
  6.3 0.6 %collective-permute-start = (bf16[400,128]{1,0:T(8,128)(2,1)S(1)}, bf16[400,128]{1,0:T(8,128)(2,1)S(1)}, u32[]{:S(2)}, u32[]{:S(2)}) collective-permute-start(bf16[400,128]{1,0:T(8,128)(2,1)S(1)} %get-tuple-element.50), channel_id=1, source_target_pairs={{0,2},{2,0},{4,6},{6,4},{8,10},{10,8},{12,14},{14,12},{16,18},{18,... | collective-permute-start | bytes 307208 | tf_op jit(solution)/shard_map/ppermute | solution.py:30
  6.8 5.6 %collective-permute-start.1 = (bf16[400,128]{1,0:T(8,128)(2,1)S(1)}, bf16[400,128]{1,0:T(8,128)(2,1)S(1)}, u32[]{:S(2)}, u32[]{:S(2)}) collective-permute-start(bf16[400,128]{1,0:T(8,128)(2,1)S(1)} %get-tuple-element.51), channel_id=1, source_target_pairs={{0,30},{2,4},{4,2},{6,8},{8,6},{10,12},{12,10},{14,16},{16,14},{18... | collective-permute-start | bytes 307208 | tf_op jit(solution)/shard_map/ppermute | solution.py:30
  12.5 2.3 %order.1.ordered = bf16[768,768]{1,0:T(8,128)(2,1)S(1)} custom-call(bf16[729,729]{1,0:T(8,128)(2,1)S(1)} %get-tuple-element.37.stiff, f32[1,768]{1,0:T(1,128)S(1)} %get-tuple-element.38.perm), custom_call_target="tpu_custom_call" | custom-call | flops 2000000000 | bytes 1065954 | tf_op jit(solution)/shard_map/order/pallas_call | solution.py:476
  14.8 1.8 %bulk.2 = (f32[4096,128]{1,0:T(8,128)S(1)}, f32[96,512]{1,0:T(8,128)S(1)}, bf16[128,512]{1,0:T(8,128)(2,1)S(1)}) custom-call(f32[8,128]{1,0:T(8,128)S(1)} %get-tuple-element.34.scale, bf16[768,768]{1,0:T(8,128)(2,1)S(1)} %order.1.ordered, bf16[768,1024]{1,0:T(8,128)(2,1)S(1)} %get-tuple-element.39.x, f32[4096,128]{1,0:T(8,128)S(1)} %get-tuple-element.40.slab, ...), custom_call_target="tpu_custom_call" | custom-call | flops 2000000000 | bytes 4870144 | tf_op jit(solution)/shard_map/bulk/pallas_call | solution.py:476
  16.6 0.0 collective-permute-done.inner
  16.6 0.0 collective-permute-done.1.outer
  16.6 2.5 %middle.1 = (f32[4096,128]{1,0:T(8,128)S(1)}, bf16[768,1024]{1,0:T(8,128)(2,1)S(1)}, bf16[4096,128]{1,0:T(8,128)(2,1)S(1)}, f32[32,128]{1,0:T(8,128)S(1)}, f32[3...) custom-call(s32[1]{0:T(128)S(6)} %copy.14.acol, ...), custom_call_target="tpu_custom_call" | custom-call | flops 100000000 | bytes 7188608 | tf_op jit(solution)/shard_map/middle/pallas_call | solution.py:476
  19.2 0.1 collective-permute-start.2
  19.2 2.6 %collective-permute-start.3 = (bf16[288,128]{1,0:T(8,128)(2,1)S(1)}, bf16[288,128]{1,0:T(8,128)(2,1)S(1)}, u32[]{:S(2)}, u32[]{:S(2)}) collective-permute-start(bf16[288,128]{1,0:T(8,128)(2,1)S(1)} %get-tuple-element.61), channel_id=1, source_target_pairs={{0,30},{2,4},{4,2},{6,8},{8,6},{10,12},{12,10},{14,16},{16,14},{18... | collective-permute-start | bytes 221192 | tf_op jit(solution)/shard_map/ppermute | solution.py:30
  21.9 1.8 %bulk.3 = (f32[4096,128]{1,0:T(8,128)S(1)}, f32[96,512]{1,0:T(8,128)S(1)}, bf16[128,512]{1,0:T(8,128)(2,1)S(1)}) custom-call(f32[8,128]{1,0:T(8,128)S(1)} %get-tuple-element.34.scale, bf16[768,768]{1,0:T(8,128)(2,1)S(1)} %order.1.ordered, bf16[768,1024]{1,0:T(8,128)(2,1)S(1)} %get-tuple-element.52.x, f32[4096,128]{1,0:T(8,128)S(1)} %get-tuple-element.53.slab, ...), custom_call_target="tpu_custom_call" | custom-call | flops 2000000000 | bytes 4870144 | tf_op jit(solution)/shard_map/bulk/pallas_call | solution.py:476
  23.7 0.0 collective-permute-done.2.inner
  23.7 2.1 %collective-permute-done.3.outer = bf16[288,128]{1,0:T(8,128)(2,1)S(1)} collective-permute-done((bf16[288,128]{1,0:T(8,128)(2,1)S(1)}, bf16[288,128]{1,0:T(8,128)(2,1)S(1)}, u32[]{:S(2)}, u32[]{:S(2)}) %collective-permute-start.3) | collective-permute-done | bytes 73760 | tf_op jit(solution)/shard_map/ppermute | solution.py:30
  25.8 2.9 %last.1 = (bf16[16,16,16,128]{3,2,1,0:T(8,128)(2,1)}, f32[32,128]{1,0:T(8,128)S(1)}, f32[32,128]{1,0:T(8,128)S(1)}) custom-call(s32[1]{0:T(128)S(6)} %copy.14.acol, s32[1]{0:T(128)S(6)} %copy.16.ucol, s32[1]{0:T(128)S(6)} %copy.15.count, f32[8,128]{1,0:T(8,128)S(1)} %get-tuple-element.34.scale, bf16[16,16,16,128]{3,2,1,0:T(8,128)(2,1)S(1)} %get-tuple-element.35.wave, ...), custom_call_target="tpu_custom_call" | custom-call | flops 100000000 | bytes 8208512 | tf_op jit(solution)/shard_map/last/pallas_call | solution.py:476
  28.7 2.6 %collective-permute-start.4 = (f32[32,128]{1,0:T(8,128)S(1)}, f32[32,128]{1,0:T(8,128)S(1)}, u32[]{:S(2)}, u32[]{:S(2)}) collective-permute-start(f32[32,128]{1,0:T(8,128)S(1)} %get-tuple-element.65), channel_id=1, source_target_pairs={{0,30},{2,0},{4,2},{6,4},{8,6},{10,8},{12,10},{14,12},{16,14},{18,... | collective-permute-start | bytes 49160 | tf_op jit(solution)/shard_map/ppermute | solution.py:23
  31.3 1.4 %collective-permute-done.4 = f32[32,128]{1,0:T(8,128)S(1)} collective-permute-done((f32[32,128]{1,0:T(8,128)S(1)}, f32[32,128]{1,0:T(8,128)S(1)}, u32[]{:S(2)}, u32[]{:S(2)}) %collective-permute-start.4) | collective-permute-done | bytes 16416 | tf_op jit(solution)/shard_map/ppermute | solution.py:23
  32.7 0.6 %add_bitcast_fusion = f32[1,32,128]{2,1,0:T(8,128)} fusion(f32[32,128]{1,0:T(8,128)S(1)} %get-tuple-element.64, f32[32,128]{1,0:T(8,128)S(1)} %collective-permute-done.4), kind=kLoop, calls=%fused_computation | loop fusion | flops 4096 | bytes 49152 | tf_op jit(solution)/shard_map/broadcast_in_dim | solution.py:542
Async XLA Ops:
  6.3 10.3 %collective-permute-start = (bf16[400,128]{1,0:T(8,128)(2,1)S(1)}, bf16[400,128]{1,0:T(8,128)(2,1)S(1)}, u32[]{:S(2)}, u32[]{:S(2)}) collective-permute-start(bf16[400,128]{1,0:T(8,128)(2,1)S(1)} %get-tuple-element.50), channel_id=1, source_target_pairs={{0,2},{2,0},{4,6},{6,4},{8,10},{10,8},{12,14},{14,12},{16,18},{18,... | collective-permute-start | bytes 307208 | tf_op jit(solution)/shard_map/ppermute | solution.py:30
  6.8 9.8 %collective-permute-start.1 = (bf16[400,128]{1,0:T(8,128)(2,1)S(1)}, bf16[400,128]{1,0:T(8,128)(2,1)S(1)}, u32[]{:S(2)}, u32[]{:S(2)}) collective-permute-start(bf16[400,128]{1,0:T(8,128)(2,1)S(1)} %get-tuple-element.51), channel_id=1, source_target_pairs={{0,30},{2,4},{4,2},{6,8},{8,6},{10,12},{12,10},{14,16},{16,14},{18... | collective-permute-start | bytes 307208 | tf_op jit(solution)/shard_map/ppermute | solution.py:30
  19.2 4.5 %collective-permute-start.2 = (bf16[288,128]{1,0:T(8,128)(2,1)S(1)}, bf16[288,128]{1,0:T(8,128)(2,1)S(1)}, u32[]{:S(2)}, u32[]{:S(2)}) collective-permute-start(bf16[288,128]{1,0:T(8,128)(2,1)S(1)} %get-tuple-element.60), channel_id=1, source_target_pairs={{0,2},{2,0},{4,6},{6,4},{8,10},{10,8},{12,14},{14,12},{16,18},{18,... | collective-permute-start | bytes 221192 | tf_op jit(solution)/shard_map/ppermute | solution.py:30
  19.2 6.5 %collective-permute-start.3 = (bf16[288,128]{1,0:T(8,128)(2,1)S(1)}, bf16[288,128]{1,0:T(8,128)(2,1)S(1)}, u32[]{:S(2)}, u32[]{:S(2)}) collective-permute-start(bf16[288,128]{1,0:T(8,128)(2,1)S(1)} %get-tuple-element.61), channel_id=1, source_target_pairs={{0,30},{2,4},{4,2},{6,8},{8,6},{10,12},{12,10},{14,16},{16,14},{18... | collective-permute-start | bytes 221192 | tf_op jit(solution)/shard_map/ppermute | solution.py:30
  28.7 4.0 %collective-permute-start.4 = (f32[32,128]{1,0:T(8,128)S(1)}, f32[32,128]{1,0:T(8,128)S(1)}, u32[]{:S(2)}, u32[]{:S(2)}) collective-permute-start(f32[32,128]{1,0:T(8,128)S(1)} %get-tuple-element.65), channel_id=1, source_target_pairs={{0,30},{2,0},{4,2},{6,4},{8,6},{10,8},{12,10},{14,12},{16,14},{18,... | collective-permute-start | bytes 49160 | tf_op jit(solution)/shard_map/ppermute | solution.py:23

commit v3 on v2

v3 whole, which is shorter than its diff:
```python
import functools

import jax
import jax.numpy as jnp
import numpy as np
from jax import lax
from jax.experimental import pallas as pl
from jax.experimental.pallas import tpu as pltpu
from jax.sharding import PartitionSpec as P

spectrum_center = 1.0
spectrum_half = 6.0
f32 = jnp.float32
bf16 = jnp.bfloat16
LANES = 128
FACE = 96
CONST_ROWS = 16


def shifted(value, axis, steps):
    count = lax.axis_size(axis)
    pairs = [(source, (source + steps) % count) for source in range(count)]
    return lax.ppermute(value, axis, pairs)


def swapped(inner, outer, axis):
    count = lax.axis_size(axis)
    within = [(source, source ^ 1) for source in range(count)]
    across = [(source, (source + (1 if source % 2 else -1)) % count) for source in range(count)]
    return lax.ppermute(inner, axis, within), lax.ppermute(outer, axis, across)


def is_odd():
    return lax.rem(lax.axis_index("space"), 2) == 1


def post(up, down, inner, outer):
    @pl.when(is_odd())
    def _():
        inner[: down.shape[0], :] = down[...]
        outer[: up.shape[0], :] = up[...]

    @pl.when(jnp.logical_not(is_odd()))
    def _():
        inner[: up.shape[0], :] = up[...]
        outer[: down.shape[0], :] = down[...]


def collect(inner, outer, up, down):
    @pl.when(is_odd())
    def _():
        up[...] = inner[: up.shape[0], :]
        down[...] = outer[: down.shape[0], :]

    @pl.when(jnp.logical_not(is_odd()))
    def _():
        up[...] = outer[: up.shape[0], :]
        down[...] = inner[: down.shape[0], :]


def row_order(degree):
    points = degree + 1

    def natural(i, j, l):
        return (i * points + j) * points + l

    inner = range(degree)
    order = [natural(degree, j, l) for j in inner for l in inner]
    order += [natural(degree, degree, l) for l in inner]
    order += [natural(degree, j, degree) for j in inner]
    order += [natural(degree, degree, degree)] + [-1] * (degree - 1)
    order += [natural(i, j, l) for i in inner for j in inner for l in inner]
    order += [natural(i, degree, l) for i in inner for l in inner]
    order += [natural(i, j, degree) for i in inner for j in inner]
    order += [natural(i, degree, degree) for i in inner]
    used = len(order)
    order += [-1] * (-used % 256)
    return np.asarray(order, np.int32), used


def dot(a, b):
    return jnp.dot(a, b, preferred_element_type=f32)


def dot_nt(a, b):
    return lax.dot_general(a, b, (((1,), (1,)), ((), ())), preferred_element_type=f32)


def onehot_rows(perm, count):
    rows = perm.shape[1]
    column = jnp.broadcast_to(perm, (8, rows)).T[:, :1]
    lane = lax.broadcasted_iota(jnp.int32, (rows, count), 1).astype(f32)
    return (column == lane).astype(bf16)


class Mesh1:
    def __init__(self, degree, channels, used, padded):
        self.d = degree
        self.e = 2 * degree
        self.plane = self.e * self.e
        self.nodes = self.e * self.plane
        self.ch = channels
        self.face_groups = degree + 3
        self.used = used
        self.padded = padded
        self.columns = [(a, b) for a in range(2) for b in range(2)]
        self.face_rows = degree * (degree + 1) ** 2
        rest = self.face_groups * degree
        lines = rest + degree**3
        self.lower_face_rows = [rest + j * degree for j in range(degree)]
        self.lower_face_rows += [lines, lines + degree**2, lines + 2 * degree**2]

    def far(self, index):
        return (1 - index) * self.d

    def aligned(self, value):
        return value if isinstance(value, int) else pl.multiple_of(value, self.d)

    def face_places(self, base, a, b):
        d, e = self.d, self.e
        near = base + a * d * e + b * d
        places = [(self.aligned(near + j * e), 1) for j in range(d)]
        places.append((self.aligned(base + self.far(a) * e + b * d), 1))
        places.append((base + a * d * e + self.far(b), e))
        places.append((self.aligned(base + self.far(a) * e + self.far(b)), 0))
        return places

    def layer_places(self, base, a, b):
        d, e, plane = self.d, self.e, self.plane
        near = base + a * d * e + b * d
        places = [(self.aligned(near + i * plane + j * e), 1) for i in range(d) for j in range(d)]
        places += [
            (self.aligned(base + i * plane + self.far(a) * e + b * d), 1) for i in range(d)
        ]
        places += [(base + i * plane + a * d * e + self.far(b), e) for i in range(d)]
        places.append((base + self.far(a) * e + self.far(b), plane))
        return places

    def take(self, ref, place):
        start, stride = place
        if stride > 1:
            return ref[pl.ds(start, self.d, stride=stride), :]
        value = ref[pl.ds(start, self.d), :]
        if stride == 0:
            first = lax.broadcasted_iota(jnp.int32, value.shape, 0) == 0
            value = jnp.where(first, value, 0.0)
        return value

    def put_add(self, ref, place, value):
        start, stride = place
        if stride > 1:
            rows = pl.ds(start, self.d, stride=stride)
        else:
            rows = pl.ds(start, self.d)
            if stride == 0:
                first = lax.broadcasted_iota(jnp.int32, value.shape, 0) == 0
                value = jnp.where(first, value, 0.0)
        ref[rows, :] = ref[rows, :] + value

    def pack(self, ref, lane, groups, first_row=0):
        lanes = pl.ds(lane, LANES)
        for at in range(0, len(groups), 2):
            pair = jnp.concatenate([groups[at], groups[at + 1]], axis=0).astype(bf16)
            ref[pl.ds(first_row + at * self.d, 2 * self.d), lanes] = pair

    def gather_element(self, slab, ref, lane, base, a, b, with_face):
        d = self.d
        zero = jnp.zeros((d, LANES), f32)
        if with_face:
            groups = [self.take(slab, p) for p in self.face_places(base + d * self.plane, a, b)]
        else:
            groups = [zero] * self.face_groups
        groups += [self.take(slab, p) for p in self.layer_places(base, a, b)]
        groups += [zero] * ((self.padded - self.used) // d)
        self.pack(ref, lane, groups)

    def gather_face(self, slab, ref, lane, base, a, b):
        zero = jnp.zeros((self.d, LANES), f32)
        groups = [self.take(slab, p) for p in self.face_places(base, a, b)]
        groups += [zero] * (LANES // self.d - len(groups))
        self.pack(ref, lane, groups)

    def add_face(self, ref, base, a, b, load):
        for g, place in enumerate(self.face_places(base, a, b)):
            self.put_add(ref, place, load(g))

    def add_layer(self, ref, base, a, b, load, start=0):
        for g, place in enumerate(self.layer_places(base, a, b)):
            if g >= start:
                self.put_add(ref, place, load(self.face_groups + g))


def live_weights(kb, count):
    lane = lax.broadcasted_iota(jnp.int32, kb.shape, 1)
    return kb * jnp.where(lane < count, 1.0, 0.0)


def as_column(row):
    size = row.shape[1]
    shape = (size, size)
    eye = lax.broadcasted_iota(jnp.int32, shape, 0) == lax.broadcasted_iota(jnp.int32, shape, 1)
    return jnp.sum(jnp.where(eye, jnp.broadcast_to(row, shape), 0.0), axis=1, keepdims=True)


def split_element(column):
    return column // 2, column % 2


def outgoing(g, acol, scale, slab, x_top, x_held, kface, both_t, face_sums, up, down, own_out, held_out):
    d, ch = g.d, g.ch
    own = dot(both_t[ch:, :], x_top[:, pl.ds(pl.multiple_of(acol * LANES, LANES), LANES)])
    held = dot(both_t[:ch, :], x_held[...])
    own_out[...] = own
    held_out[...] = held
    sums = dot(kface, x_top[...])
    face_sums[...] = jnp.zeros_like(face_sums)
    for k, (a, b) in enumerate(g.columns):
        part = sums[:, k * LANES : (k + 1) * LANES] * scale[4 + k : 5 + k, :]
        g.add_face(face_sums, 0, a, b, lambda n: part[n * d : (n + 1) * d])
    up[: g.plane, :] = face_sums[...].astype(bf16)
    up[g.plane : g.plane + ch, :] = own.astype(bf16)
    down[: g.plane, :] = slab[: g.plane, :].astype(bf16)
    down[g.plane :, :] = held.astype(bf16)


def gather_out(g, slab, x_top, x_held, ucol):
    for k, (a, b) in enumerate(g.columns):
        g.gather_element(slab, x_top, k * LANES, g.d * g.plane, a, b, False)
    a, b = split_element(ucol)
    g.gather_element(slab, x_held, 0, 0, a, b, True)


def widen(g, source, target):
    value = source[...]
    high = value.astype(bf16).astype(f32)
    middle = (value - high).astype(bf16).astype(f32)
    parts = jnp.concatenate([high, middle, value - high - middle], axis=0).T.astype(bf16)
    shape = (3 * g.e, 2 * LANES)
    row = lax.rem(lax.broadcasted_iota(jnp.int32, shape, 0), g.e)
    second = (lax.broadcasted_iota(jnp.int32, shape, 1) >= LANES).astype(jnp.int32)
    for p in range(0, g.e, 2):
        wide = dot(parts, (row == p + second).astype(f32).astype(bf16))
        target[p * g.plane : (p + 1) * g.plane, :] = wide[:, :LANES]
        target[(p + 1) * g.plane : (p + 2) * g.plane, :] = wide[:, LANES:]


def start_kernel(
    g, acol, ucol, count, wave_hbm, mass_hbm, scale_hbm, stiff_hbm, low_hbm, up_hbm, kb_hbm, perm_hbm, pot_hbm,
    slab, x_top, mass_wide, wave, stiff, scale, perm, pot, kb, both, both_t, own_out, held_out, inner, outer,
    face_sums, up, down, mass, scale_in, proj, x_held, sems,
):
    ch = g.ch
    copies = [
        pltpu.make_async_copy(source, target, sems.at[k])
        for k, (source, target) in enumerate((
            (mass_hbm, mass), (wave_hbm, wave), (perm_hbm, perm), (up_hbm.at[0], proj.at[:ch]),
            (low_hbm.at[0], proj.at[ch:]), (stiff_hbm, stiff), (scale_hbm, scale_in), (kb_hbm, kb), (pot_hbm, pot),
        ))
    ]
    for copy in copies:
        copy.start()
    copies[0].wait()
    widen(g, mass, mass_wide)
    copies[1].wait()
    for p in range(g.e):
        rows = pl.ds(p * g.plane, g.plane)
        start = wave[p].astype(f32).reshape(g.plane, LANES)
        slab[rows, :] = (mass_wide[rows, :] * start).astype(bf16).astype(f32)
    gather_out(g, slab, x_top, x_held, ucol[0])
    for copy in copies[2:]:
        copy.wait()
    for k in range(8):
        one = scale_in[k // 4, k % 4 // 2 : k % 4 // 2 + 1, k % 2 : k % 2 + 1]
        scale[k : k + 1, :] = jnp.broadcast_to(one, (1, LANES))
    count_rows = stiff.shape[0]
    sublane = lax.broadcasted_iota(jnp.int32, (count_rows, g.padded), 0).astype(f32)
    pick_t = (perm[...] == sublane).astype(f32).astype(bf16)
    first = g.face_rows // 16 * 16
    left = jnp.concatenate([proj[...], stiff[first:, :]], axis=0)
    ordered = dot(left, pick_t)
    both_t[...] = ordered[: 2 * ch].astype(bf16)
    kface = dot(onehot_rows(perm[:, :LANES] - first, count_rows - first)[:FACE], ordered[2 * ch :].astype(bf16))
    kface = kface.astype(bf16)
    turned = ordered[: 2 * ch].T.astype(bf16)
    both[...] = turned
    outgoing(g, acol[0], scale, slab, x_top, x_held, kface, both_t, face_sums, up, down, own_out, held_out)
    at = g.plane + ch
    up[at : at + FACE, :] = jnp.zeros((FACE, LANES), bf16)
    up[at : at + FACE, :ch] = turned[:FACE, ch:]
    shape = (CONST_ROWS, LANES)
    row = lax.broadcasted_iota(jnp.int32, shape, 0)
    values = jnp.zeros(shape, f32)
    for k in range(4):
        chosen = jnp.where(acol[0] == k, 1.0, 0.0)
        values = jnp.where(row == k, chosen, values)
        full = jnp.broadcast_to(scale[4 + k : 5 + k, :], shape)
        high = full.astype(bf16).astype(f32)
        values = jnp.where(row == 4 + k, high, values)
        values = jnp.where(row == 8 + k, full - high, values)
    weights = live_weights(kb[...], count[0])
    weights = jnp.concatenate([weights, jnp.zeros((1, LANES - ch), f32)], axis=1)
    full = jnp.broadcast_to(weights, shape)
    high = full.astype(bf16).astype(f32)
    values = jnp.where(row == 12, high, values)
    values = jnp.where(row == 13, full - high, values)
    up[at + FACE :, :] = values.astype(bf16)
    post(up, down, inner, outer)


def order_kernel(g, stiff, perm, pot, ordered, pot_wide):
    widen(g, pot, pot_wide)
    pick = onehot_rows(perm[...], stiff.shape[0])
    part = perm.shape[1] // 3
    for k in range(3):
        rows = slice(k * part, (k + 1) * part)
        half = dot(pick[rows], stiff[...]).astype(bf16)
        ordered[rows, :] = dot_nt(half, pick).astype(bf16)


def bulk_sums(g, scale, ordered, x_top, slab, pot_wide, face_own, x_face, total, z, x_low):
    d = g.d
    for p in range(g.e):
        rows = pl.ds(p * g.plane, g.plane)
        total[rows, :] = pot_wide[rows, :] * slab[rows, :]
    for k, (a, b) in enumerate(g.columns):
        g.gather_element(slab, x_low, k * LANES, 0, a, b, True)
        g.gather_face(slab, x_face, k * LANES, 0, a, b)
    for layer, x in enumerate((x_low, x_top)):
        for a in range(2):
            lane = a * 2 * LANES
            z[...] = dot(ordered[: g.used, :], x[:, lane : lane + 2 * LANES])
            for b in range(2):
                k = layer * 4 + a * 2 + b
                factor = scale[k : k + 1, :]

                def load(n):
                    return z[n * d : (n + 1) * d, b * LANES : (b + 1) * LANES] * factor

                if layer == 0:
                    g.add_face(total, d * g.plane, a, b, load)
                g.add_layer(total, layer * d * g.plane, a, b, load)
    face_own[...] = dot(ordered[:FACE, :LANES], x_face[...])


def bulk_kernel(
    g, scale, ordered, x_top, slab, pot_wide, mass_wide, wave,
    before, low_step, low_slab, face_own, x_face, total, z, x_low,
):
    bulk_sums(g, scale, ordered, x_top, slab, pot_wide, face_own, x_face, total, z, x_low)
    for p in range(g.e):
        rows = pl.ds(p * g.plane, g.plane)
        wide = mass_wide[rows, :]
        base = wave[p].astype(f32).reshape(g.plane, LANES)
        value = (wide * total[rows, :] - spectrum_center * base) * (1.0 / spectrum_half)
        before[rows, :] = value
        if p < g.d:
            one = value.astype(bf16).astype(f32)
            low_step[rows, :] = one
            low_slab[rows, :] = (wide * one).astype(bf16).astype(f32)


def bulk_last_kernel(
    g, scale, ordered, x_top, slab, pot_wide, mass_wide, wave, step,
    before, low_new, face_own, x_face, total, z, x_low,
):
    bulk_sums(g, scale, ordered, x_top, slab, pot_wide, face_own, x_face, total, z, x_low)
    for p in range(g.e):
        rows = pl.ds(p * g.plane, g.plane)
        base = wave[p].astype(f32).reshape(g.plane, LANES)
        image = mass_wide[rows, :] * total[rows, :]
        value = (image - spectrum_center * step[rows, :]) * (2.0 / spectrum_half) - base
        before[rows, :] = value
        if p < g.d:
            low_new[rows, :] = value.astype(bf16).astype(f32)


def neighbour_terms(
    g, acol, count, both, both_t, own, held, kb, face_low, const, up, down, x_face, next_plane, x_next,
):
    ch = g.ch
    next_plane[...] = down[: g.plane, :].astype(f32)
    for k, (a, b) in enumerate(g.columns):
        g.gather_face(next_plane, x_next, k * LANES, 0, a, b)
    mine = own[...] + down[g.plane :, :].astype(f32)
    column = pl.ds(pl.multiple_of(acol * LANES, LANES), LANES)
    mine = mine + dot(both_t[ch:, :LANES], x_next[:, column])
    mine = (as_column(live_weights(kb[...], count)) * mine).astype(bf16)
    weights_low = as_column(const[12:13, :ch] + const[13:14, :ch])
    low = up[g.plane : g.plane + ch, :].astype(f32) + held[...]
    low = low + dot_chosen(face_low, x_face, const)
    low = (weights_low * low).astype(bf16)
    return mine, low


def dot_chosen(face, x_face, const):
    rows = face.shape[0]
    chosen = jnp.zeros((rows, LANES), f32)
    for k in range(4):
        chosen = chosen + x_face[:rows, k * LANES : (k + 1) * LANES].astype(f32) * const[k : k + 1, :]
    face_t = face.astype(f32).T.astype(bf16)
    return dot(face_t, chosen.astype(bf16))


def rim_sums(g, ucol, const, face_own, face_low, low, lifted_up, up, rim):
    d = g.d
    lifted_low = dot(face_low, low)
    rim[...] = up[: g.plane, :].astype(f32)
    for k, (a, b) in enumerate(g.columns):
        part = face_own[:, k * LANES : (k + 1) * LANES] * (const[4 + k : 5 + k, :] + const[8 + k : 9 + k, :])
        part = part + lifted_low * const[k : k + 1, :]
        g.add_face(rim, 0, a, b, lambda n: part[n * d : (n + 1) * d])
    a, b = split_element(ucol)
    for start, place in zip(g.lower_face_rows, g.face_places(0, a, b)):
        g.put_add(rim, place, lifted_up[start : start + d])


def upper_sums(g, acol, scale, ordered, both, x_next, mine, sums):
    d = g.d
    upper = dot(ordered[: g.used, :LANES], x_next[...])
    lifted = dot(both[: g.used, g.ch :], mine)

    def loader(k):
        here = jnp.where(acol == k, 1.0, 0.0)
        factor = scale[4 + k : 5 + k, :]
        lane = k * LANES

        def load(n):
            rows = slice(n * d, (n + 1) * d)
            return upper[rows, lane : lane + LANES] * factor + lifted[rows] * here

        return load

    for k, (a, b) in enumerate(g.columns):
        load = loader(k)
        near = a * d * g.e + b * d
        for i in range(d):
            for j in range(d):
                sums[pl.ds(near + i * g.plane + j * g.e, d), :] = load(g.face_groups + i * d + j)
    for k, (a, b) in enumerate(g.columns):
        g.add_layer(sums, 0, a, b, loader(k), start=d * d)


def held_places(g, ucol, lifted_up):
    d = g.d
    a, b = split_element(ucol)
    for n, place in enumerate(g.layer_places(0, a, b)):
        row = (g.face_groups + n) * d
        if row not in g.lower_face_rows[:-1]:
            start, stride = place
            rows = pl.ds(start, d, stride=stride) if stride > 1 else pl.ds(start, d)
            yield rows, None if lifted_up is None else lifted_up[row : row + d]


def middle_kernel(
    g, acol, ucol, count, scale, mass_wide, before, low_step, low_slab, face_own, x_face, ordered, both, both_t,
    own, held, kb, inner, outer,
    slab, x_top, step, own_out, held_out, inner_out, outer_out, kept,
    sums, next_plane, x_next, face_sums, up, down, up_out, down_out, rim, x_held,
):
    at = g.plane + g.ch
    d = g.d
    half = d * g.plane
    collect(inner, outer, up, down)
    kept[...] = up[at:, :]
    face_low = up[at : at + FACE, : g.ch]
    const = up[at + FACE :, :].astype(f32)
    mine, low = neighbour_terms(
        g, acol[0], count[0], both, both_t, own, held, kb, face_low, const, up, down, x_face, next_plane, x_next
    )
    lifted_up = dot(both[: g.used, : g.ch], low)
    upper_sums(g, acol[0], scale, ordered, both, x_next, mine, sums)
    a, b = split_element(ucol[0])
    g.add_face(sums, 0, a, b, lambda n: lifted_up[n * d : (n + 1) * d])
    rim_sums(g, ucol[0], const, face_own, face_low, low, lifted_up, up, rim)
    step[:half, :] = low_step[...]
    slab[:half, :] = low_slab[...]

    def finish(rows, added):
        wide = mass_wide[rows, :]
        one = (before[rows, :] + wide * (added * (1.0 / spectrum_half))).astype(bf16).astype(f32)
        step[rows, :] = one
        slab[rows, :] = (wide * one).astype(bf16).astype(f32)

    for rows, added in held_places(g, ucol[0], lifted_up):
        finish(rows, added)
    finish(pl.ds(0, g.plane), rim[...])
    for p in range(d):
        finish(pl.ds(half + p * g.plane, g.plane), sums[p * g.plane : (p + 1) * g.plane, :])
    gather_out(g, slab, x_top, x_held, ucol[0])
    outgoing(
        g, acol[0], scale, slab, x_top, x_held, ordered[:FACE, :], both_t, face_sums, up_out, down_out,
        own_out, held_out,
    )
    post(up_out, down_out, inner_out, outer_out)


def last_low_kernel(
    g, acol, ucol, count, scale, mass_wide, before, face_own, x_face, ordered, both, both_t,
    own, held, kb, kept, inner, outer,
    held_out, new, mine_out, x_next,
    sums, next_plane, x_held, x_rim, up, down, rim,
):
    d, ch = g.d, g.ch
    half = d * g.plane
    collect(inner, outer, up, down)
    face_low = kept[:FACE, :ch]
    const = kept[FACE:, :].astype(f32)
    mine, low = neighbour_terms(
        g, acol[0], count[0], both, both_t, own, held, kb, face_low, const, up, down, x_face, next_plane, x_next
    )
    mine_out[...] = mine
    lifted_up = dot(both[: g.used, :ch], low)
    starts = g.lower_face_rows
    pieces = [slice(starts[0] - d, starts[0] + (d + 1) * d)] + [slice(s - d, s + d) for s in starts[d:]]
    offsets = [d + n * d for n in range(d)] + [(d + 2) * d + n * 2 * d + d for n in range(3)]
    upper = dot(jnp.concatenate([ordered[p, :LANES] for p in pieces], axis=0), x_next[...])
    lifted = dot(jnp.concatenate([both[p, ch:] for p in pieces], axis=0), mine)
    sums[...] = jnp.zeros_like(sums)
    for k, (a, b) in enumerate(g.columns):
        here = jnp.where(acol[0] == k, 1.0, 0.0)
        factor = scale[4 + k : 5 + k, :]
        part = upper[:, k * LANES : (k + 1) * LANES] * factor + lifted * here
        g.add_face(sums, 0, a, b, lambda n: part[offsets[n] : offsets[n] + d])
    a, b = split_element(ucol[0])
    g.add_face(sums, 0, a, b, lambda n: lifted_up[n * d : (n + 1) * d])
    rim_sums(g, ucol[0], const, face_own, face_low, low, lifted_up, up, rim)

    def finish(rows, added):
        value = before[rows, :] + mass_wide[rows, :] * (added * (2.0 / spectrum_half))
        new[rows, :] = value.astype(bf16).astype(f32)

    for rows, added in held_places(g, ucol[0], lifted_up):
        finish(rows, added)
    finish(pl.ds(0, g.plane), rim[...])
    finish(pl.ds(half, g.plane), sums[...])
    g.gather_element(new, x_held, 0, 0, a, b, True)
    for k, (a, b) in enumerate(g.columns):
        g.gather_face(new, x_rim, k * LANES, 0, a, b)
    held_out[...] = dot(both_t[:ch, :], x_held[...]) + dot_chosen(face_low, x_rim, const)


def last_high_kernel(
    g, acol, ucol, count, scale, mass_wide, before, low_new, ordered, both, both_t, new, mine, x_next,
    filtered, own_out, sums, field, x_own,
):
    d = g.d
    half = d * g.plane
    field[:half, :] = low_new[...]
    for rows, _ in held_places(g, ucol[0], None):
        field[rows, :] = new[rows, :]
    field[: g.plane, :] = new[: g.plane, :]
    field[half : half + g.plane, :] = new[half : half + g.plane, :]
    upper_sums(g, acol[0], scale, ordered, both, x_next, mine[...], sums)
    for p in range(1, d):
        rows = pl.ds(half + p * g.plane, g.plane)
        added = sums[p * g.plane : (p + 1) * g.plane, :]
        value = before[rows, :] + mass_wide[rows, :] * (added * (2.0 / spectrum_half))
        field[rows, :] = value.astype(bf16).astype(f32)
    for p in range(g.e):
        filtered[p] = field[p * g.plane : (p + 1) * g.plane, :].astype(bf16).reshape(g.e, g.e, LANES)
    a, b = split_element(acol[0])
    g.gather_element(field, x_own, 0, half, a, b, False)
    own_out[...] = dot(both_t[g.ch :, :], x_own[...])


def call(kernel, name, scalars, operands, outs, scratch, flops, limit=24 << 20, hbm=False):
    smem = pl.BlockSpec(memory_space=pltpu.SMEM)
    vmem = pl.BlockSpec(memory_space=pltpu.VMEM)
    far = pl.BlockSpec(memory_space=pltpu.MemorySpace.HBM)
    moved = sum(v.size * v.dtype.itemsize for v in operands)
    if hbm:
        operands = [pltpu.with_memory_space_constraint(v, pltpu.MemorySpace.HBM) for v in operands]
    return pl.pallas_call(
        kernel,
        name=name,
        out_shape=[jax.ShapeDtypeStruct(s, t) for s, t in outs],
        in_specs=[smem] * len(scalars) + [far if hbm else vmem] * len(operands),
        out_specs=[vmem] * len(outs),
        scratch_shapes=[pltpu.VMEM(*s) if isinstance(s, tuple) else s for s in scratch],
        compiler_params=pltpu.CompilerParams(vmem_limit_bytes=limit),
        cost_estimate=pl.CostEstimate(flops=flops, bytes_accessed=moved, transcendentals=0),
    )(*scalars, *operands)


def per_device(
    wave_in, mass_scale, potential, elem_scale, stiffness, proj_lower, proj_upper, kb_coef,
    atom_column, chan_count, upper_column,
):
    extent = wave_in.shape[0]
    degree = extent // 2
    ch = kb_coef.shape[-1]
    order, used = row_order(degree)
    padded = order.shape[0]
    perm = jnp.asarray(order, f32)[None, :]
    g = Mesh1(degree, ch, used, padded)
    plane, nodes = g.plane, g.nodes
    scalars = (atom_column, upper_column, chan_count)
    part = ((ch, LANES), f32)
    slab_s, half_s, plane_s = ((nodes, LANES), f32), ((nodes // 2, LANES), f32), ((plane, LANES), f32)
    x_s, x_one_s = ((padded, 4 * LANES), bf16), ((padded, LANES), bf16)
    wire_s = ((plane + ch, LANES), bf16)
    wire_first_s = ((plane + ch + FACE + CONST_ROWS, LANES), bf16)
    face_s = ((LANES, 4 * LANES), bf16)
    face_sum_s = ((FACE, 4 * LANES), f32)

    slab, x_top, mass_wide, wave, stiff, scale, order_row, pot, kb, both, both_t, own, held, inner, outer = call(
        functools.partial(start_kernel, g), "start", scalars,
        (wave_in, mass_scale, elem_scale, stiffness, jnp.swapaxes(proj_lower, 1, 2), jnp.swapaxes(proj_upper, 1, 2),
         kb_coef, perm, potential),
        [slab_s, x_s, slab_s, (wave_in.shape, bf16), (stiffness.shape, bf16), ((8, LANES), f32), (perm.shape, f32),
         (potential.shape, f32), (kb_coef.shape, f32), ((padded, 2 * ch), bf16), ((2 * ch, padded), bf16), part, part,
         wire_first_s, wire_first_s],
        [plane_s, wire_first_s, wire_s, (mass_scale.shape, f32), (elem_scale.shape, f32),
         ((2 * ch, stiffness.shape[0]), bf16), x_one_s, pltpu.SemaphoreType.DMA((9,))], 10**8, hbm=True,
    )
    inner, outer = swapped(inner, outer, "space")
    ordered, pot_wide = call(
        functools.partial(order_kernel, g), "order", (), (stiff, order_row, pot),
        [((padded, padded), bf16), slab_s], [], 2 * 10**9,
    )
    bulk_scratch = [slab_s, ((used, 2 * LANES), f32), x_s]
    before, low_step, low_slab, face_own, x_face = call(
        functools.partial(bulk_kernel, g), "bulk", (), (scale, ordered, x_top, slab, pot_wide, mass_wide, wave),
        [slab_s, half_s, half_s, face_sum_s, face_s], bulk_scratch, 2 * 10**9,
    )
    shared = (ordered, both, both_t)
    slab, x_top, step, own, held, inner, outer, kept = call(
        functools.partial(middle_kernel, g), "middle", scalars,
        (scale, mass_wide, before, low_step, low_slab, face_own, x_face, *shared, own, held, kb, inner, outer),
        [slab_s, x_s, slab_s, part, part, wire_s, wire_s, ((FACE + CONST_ROWS, LANES), bf16)],
        [half_s, plane_s, face_s, plane_s, wire_first_s, wire_s, wire_s, wire_s, plane_s, x_one_s], 10**8,
    )
    inner, outer = swapped(inner, outer, "space")
    before, low_new, face_own, x_face = call(
        functools.partial(bulk_last_kernel, g), "bulk_last", (),
        (scale, ordered, x_top, slab, pot_wide, mass_wide, wave, step),
        [slab_s, half_s, face_sum_s, face_s], bulk_scratch, 2 * 10**9,
    )
    held, new, mine, x_next = call(
        functools.partial(last_low_kernel, g), "last_low", scalars,
        (scale, mass_wide, before, face_own, x_face, *shared, own, held, kb, kept, inner, outer),
        [part, ((nodes // 2 + plane, LANES), f32), ((ch, LANES), bf16), face_s],
        [plane_s, plane_s, x_one_s, face_s, wire_s, wire_s, plane_s], 10**8,
    )
    held = shifted(held, "space", -1)
    filtered, own = call(
        functools.partial(last_high_kernel, g), "last_high", scalars,
        (scale, mass_wide, before, low_new, *shared, new, mine, x_next),
        [(wave_in.shape, bf16), part], [half_s, slab_s, x_one_s], 10**9,
    )
    return filtered, (own + held)[None]


def solution(mesh):
    in_specs = (
        P("space", None, None, "band"),
        P("space", None),
        P("space", None),
        P("space", None, None),
        P(),
        P("space", None, None),
        P("space", None, None),
        P("space", None),
        P("space"),
        P("space"),
        P("space"),
    )
    out_specs = (P("space", None, None, "band"), P("space", None, "band"))
    return jax.shard_map(
        per_device, mesh=mesh, in_specs=in_specs, out_specs=out_specs, check_vma=False
    )
```

time: 33.6 us -> 30.8 us (0.917)
  starting transfers between devices: 11.5 us -> 9.93 us
  waiting for transfers between devices: 3.53 us -> 2.2 us
    ppermute x1, waiting for transfers between devices: 1.44 us -> 0.01 us  [shifted(): return lax.ppermute(value, axis, pairs)]
    ppermute x2, starting transfers between devices: 8.27 us -> 7.48 us  [swapped(): lax.ppermute(outer, axis, across)]
    ppermute x1, starting transfers between devices: 2.57 us -> 1.83 us  [shifted(): return lax.ppermute(value, axis, pairs)]
    pallas_call x6 -> x7, Pallas kernels: 15.1 us -> 15.2 us  [call(): pl.pallas_call(kernel, name=name, out_shape=[jax.ShapeDtypeStruct(s, t) f...]
  transfers between devices with their start and end apart: 5 -> 5, of which waited for: 2 -> 1; matrix products, arithmetic and copies ran while one was open for 0% -> 0% of each run, Pallas kernels for 18% -> 31%
where the time goes in v3:
time: 30.8 us; the launch traced here: 30.6 us
  Pallas kernels  15.2 us (49%)
  starting transfers between devices  9.93 us (32%)
  between operations  2.64 us (9%)
  waiting for transfers between devices  2.2 us (7%)
  other arithmetic  0.61 us (2%)
    pallas_call x7, Pallas kernels, call(): pl.pallas_call(kernel, name=name, out_shape=[jax.ShapeDtypeStruct(s, t) f...  15.2 us
    ppermute x2, starting transfers between devices, swapped(): lax.ppermute(outer, axis, across)  7.48 us
    ppermute x2, waiting for transfers between devices, swapped(): lax.ppermute(outer, axis, across)  2.19 us
    ppermute x1, starting transfers between devices, shifted(): return lax.ppermute(value, axis, pairs)  1.83 us
    ppermute x2, starting transfers between devices, swapped(): lax.ppermute(inner, axis, within)  0.62 us
  transfers between devices with their start and end apart: 5, of which 1 were waited for; matrix products, arithmetic and copies ran while one was open for 0% of the time, Pallas kernels for 31%

profile of v3, /device:TPU:0, one launch (start us, length us, event | category | flops | bytes accessed | tf_op | source)
XLA Modules:
  0.0 30.6 jit_solution(15810891504379550649)
XLA Ops:
  2.6 2.6 %start.1 = (f32[4096,128]{1,0:T(8,128)S(1)}, bf16[768,512]{1,0:T(8,128)(2,1)S(1)}, f32[4096,128]{1,0:T(8,128)S(1)}, bf16[16,16,16,128]{3,2,1,0:T(8,128)(2,1)S(1)...) custom-call(s32[1]{0:T(128)S(6)} %copy.14.acol, ...), custom_call_target="tpu_custom_call" | custom-call | flops 100000000 | bytes 2240770 | tf_op jit(solution)/shard_map/start/pallas_call | solution.py:573
  5.2 0.5 %collective-permute-start = (bf16[400,128]{1,0:T(8,128)(2,1)S(1)}, bf16[400,128]{1,0:T(8,128)(2,1)S(1)}, u32[]{:S(2)}, u32[]{:S(2)}) collective-permute-start(bf16[400,128]{1,0:T(8,128)(2,1)S(1)} %get-tuple-element.62), channel_id=1, source_target_pairs={{0,2},{2,0},{4,6},{6,4},{8,10},{10,8},{12,14},{14,12},{16,18},{18,... | collective-permute-start | bytes 307208 | tf_op jit(solution)/shard_map/ppermute | solution.py:30
  5.8 5.6 %collective-permute-start.1 = (bf16[400,128]{1,0:T(8,128)(2,1)S(1)}, bf16[400,128]{1,0:T(8,128)(2,1)S(1)}, u32[]{:S(2)}, u32[]{:S(2)}) collective-permute-start(bf16[400,128]{1,0:T(8,128)(2,1)S(1)} %get-tuple-element.63), channel_id=1, source_target_pairs={{0,30},{2,4},{4,2},{6,8},{8,6},{10,12},{12,10},{14,16},{16,14},{18... | collective-permute-start | bytes 307208 | tf_op jit(solution)/shard_map/ppermute | solution.py:30
  11.4 2.5 %order.1 = (bf16[768,768]{1,0:T(8,128)(2,1)S(1)}, f32[4096,128]{1,0:T(8,128)S(1)}) custom-call(bf16[729,729]{1,0:T(8,128)(2,1)S(1)} %get-tuple-element.44.stiff, f32[1,768]{1,0:T(1,128)S(1)} %get-tuple-element.45.perm, f32[16,256]{1,0:T(8,128)S(1)} %get-tuple-element.46.pot), custom_call_target="tpu_custom_call" | custom-call | flops 2000000000 | bytes 1082338 | tf_op jit(solution)/shard_map/order/pallas_call | solution.py:573
  13.9 2.5 %bulk.1 = (f32[4096,128]{1,0:T(8,128)S(1)}, f32[2048,128]{1,0:T(8,128)S(1)}, f32[2048,128]{1,0:T(8,128)S(1)}, f32[96,512]{1,0:T(8,128)S(1)}, bf16[128,512]{1,0:T(8,128)(2,1)S(1)}) custom-call(f32[8,128]{1,0:T(8,128)S(1)} %get-tuple-element.42.scale, bf16[768,768]{1,0:T(8,128)(2,1)S(1)} %get-tuple-element.47.ordered, ...), custom_call_target="tpu_custom_call" | custom-call | flops 2000000000 | bytes 9310208 | tf_op jit(solution)/shard_map/bulk/pallas_call | solution.py:573
  16.4 0.0 collective-permute-done.inner
  16.4 0.0 collective-permute-done.1.outer
  16.4 2.2 %middle.1 = (f32[4096,128]{1,0:T(8,128)S(1)}, bf16[768,512]{1,0:T(8,128)(2,1)S(1)}, f32[4096,128]{1,0:T(8,128)S(1)}, f32[32,128]{1,0:T(8,128)S(1)}, f32[32,128]{...) custom-call(s32[1]{0:T(128)S(6)} %copy.14.acol, ...), custom_call_target="tpu_custom_call" | custom-call | flops 100000000 | bytes 8237184 | tf_op jit(solution)/shard_map/middle/pallas_call | solution.py:573
  18.6 0.1 collective-permute-start.2
  18.7 1.8 %collective-permute-start.3 = (bf16[288,128]{1,0:T(8,128)(2,1)S(1)}, bf16[288,128]{1,0:T(8,128)(2,1)S(1)}, u32[]{:S(2)}, u32[]{:S(2)}) collective-permute-start(bf16[288,128]{1,0:T(8,128)(2,1)S(1)} %get-tuple-element.75), channel_id=1, source_target_pairs={{0,30},{2,4},{4,2},{6,8},{8,6},{10,12},{12,10},{14,16},{16,14},{18... | collective-permute-start | bytes 221192 | tf_op jit(solution)/shard_map/ppermute | solution.py:30
  20.5 2.5 %bulk_last.1 = (f32[4096,128]{1,0:T(8,128)S(1)}, f32[2048,128]{1,0:T(8,128)S(1)}, f32[96,512]{1,0:T(8,128)S(1)}, bf16[128,512]{1,0:T(8,128)(2,1)S(1)}) custom-call(f32[8,128]{1,0:T(8,128)S(1)} %get-tuple-element.42.scale, bf16[768,768]{1,0:T(8,128)(2,1)S(1)} %get-tuple-element.47.ordered, bf16[768,512]{1,0:T(8,128)(2,1)S(1)} %get-tuple-element.64.x_top, ...), custom_call_target="tpu_custom_call" | custom-call | flops 2000000000 | bytes 11407360 | tf_op jit(solution)/shard_map/bulk_last/pallas_call | solution.py:573
  23.0 0.0 collective-permute-done.2.inner
  23.0 2.2 %collective-permute-done.3.outer = bf16[288,128]{1,0:T(8,128)(2,1)S(1)} collective-permute-done((bf16[288,128]{1,0:T(8,128)(2,1)S(1)}, bf16[288,128]{1,0:T(8,128)(2,1)S(1)}, u32[]{:S(2)}, u32[]{:S(2)}) %collective-permute-start.3) | collective-permute-done | bytes 73760 | tf_op jit(solution)/shard_map/ppermute | solution.py:30
  25.2 0.8 %last_low.1 = (f32[32,128]{1,0:T(8,128)S(1)}, f32[2304,128]{1,0:T(8,128)S(1)}, bf16[32,128]{1,0:T(8,128)(2,1)S(1)}, bf16[128,512]{1,0:T(8,128)(2,1)S(1)}) custom-call(s32[1]{0:T(128)S(6)} %copy.14.acol, s32[1]{0:T(128)S(6)} %copy.16.ucol, s32[1]{0:T(128)S(6)} %copy.15.count, f32[8,128]{1,0:T(8,128)S(1)} %get-tuple-element.42.scale, ...), custom_call_target="tpu_custom_call" | custom-call | flops 100000000 | bytes 6111360 | tf_op jit(solution)/shard_map/last_low/pallas_call | solution.py:573
  26.0 1.8 %collective-permute-start.4 = (f32[32,128]{1,0:T(8,128)S(1)}, f32[32,128]{1,0:T(8,128)S(1)}, u32[]{:S(2)}, u32[]{:S(2)}) collective-permute-start(f32[32,128]{1,0:T(8,128)S(1)} %get-tuple-element.81), channel_id=1, source_target_pairs={{0,30},{2,0},{4,2},{6,4},{8,6},{10,8},{12,10},{14,12},{16,14},{18,... | collective-permute-start | bytes 49160 | tf_op jit(solution)/shard_map/ppermute | solution.py:23
  27.9 2.1 %last_high.1 = (bf16[16,16,16,128]{3,2,1,0:T(8,128)(2,1)}, f32[32,128]{1,0:T(8,128)S(1)}) custom-call(s32[1]{0:T(128)S(6)} %copy.14.acol, s32[1]{0:T(128)S(6)} %copy.16.ucol, s32[1]{0:T(128)S(6)} %copy.15.count, f32[8,128]{1,0:T(8,128)S(1)} %get-tuple-element.42.scale, f32[4096,128]{1,0:T(8,128)S(1)} %get-tuple-element.43.mass_wide, ...), custom_call_target="tpu_custom_call" | custom-call | flops 1000000000 | bytes 7942144 | tf_op jit(solution)/shard_map/last_high/pallas_call | solution.py:573
  30.0 0.0 collective-permute-done.4
  30.0 0.6 %add_bitcast_fusion = f32[1,32,128]{2,1,0:T(8,128)} fusion(f32[32,128]{1,0:T(8,128)S(1)} %get-tuple-element.80, f32[32,128]{1,0:T(8,128)S(1)} %collective-permute-done.4), kind=kLoop, calls=%fused_computation | loop fusion | flops 4096 | bytes 49152 | tf_op jit(solution)/shard_map/broadcast_in_dim | solution.py:651
Async XLA Ops:
  5.2 11.2 %collective-permute-start = (bf16[400,128]{1,0:T(8,128)(2,1)S(1)}, bf16[400,128]{1,0:T(8,128)(2,1)S(1)}, u32[]{:S(2)}, u32[]{:S(2)}) collective-permute-start(bf16[400,128]{1,0:T(8,128)(2,1)S(1)} %get-tuple-element.62), channel_id=1, source_target_pairs={{0,2},{2,0},{4,6},{6,4},{8,10},{10,8},{12,14},{14,12},{16,18},{18,... | collective-permute-start | bytes 307208 | tf_op jit(solution)/shard_map/ppermute | solution.py:30
  5.8 10.6 %collective-permute-start.1 = (bf16[400,128]{1,0:T(8,128)(2,1)S(1)}, bf16[400,128]{1,0:T(8,128)(2,1)S(1)}, u32[]{:S(2)}, u32[]{:S(2)}) collective-permute-start(bf16[400,128]{1,0:T(8,128)(2,1)S(1)} %get-tuple-element.63), channel_id=1, source_target_pairs={{0,30},{2,4},{4,2},{6,8},{8,6},{10,12},{12,10},{14,16},{16,14},{18... | collective-permute-start | bytes 307208 | tf_op jit(solution)/shard_map/ppermute | solution.py:30
  18.6 4.4 %collective-permute-start.2 = (bf16[288,128]{1,0:T(8,128)(2,1)S(1)}, bf16[288,128]{1,0:T(8,128)(2,1)S(1)}, u32[]{:S(2)}, u32[]{:S(2)}) collective-permute-start(bf16[288,128]{1,0:T(8,128)(2,1)S(1)} %get-tuple-element.74), channel_id=1, source_target_pairs={{0,2},{2,0},{4,6},{6,4},{8,10},{10,8},{12,14},{14,12},{16,18},{18,... | collective-permute-start | bytes 221192 | tf_op jit(solution)/shard_map/ppermute | solution.py:30
  18.7 6.5 %collective-permute-start.3 = (bf16[288,128]{1,0:T(8,128)(2,1)S(1)}, bf16[288,128]{1,0:T(8,128)(2,1)S(1)}, u32[]{:S(2)}, u32[]{:S(2)}) collective-permute-start(bf16[288,128]{1,0:T(8,128)(2,1)S(1)} %get-tuple-element.75), channel_id=1, source_target_pairs={{0,30},{2,4},{4,2},{6,8},{8,6},{10,12},{12,10},{14,16},{16,14},{18... | collective-permute-start | bytes 221192 | tf_op jit(solution)/shard_map/ppermute | solution.py:30
  26.0 3.9 %collective-permute-start.4 = (f32[32,128]{1,0:T(8,128)S(1)}, f32[32,128]{1,0:T(8,128)S(1)}, u32[]{:S(2)}, u32[]{:S(2)}) collective-permute-start(f32[32,128]{1,0:T(8,128)S(1)} %get-tuple-element.81), channel_id=1, source_target_pairs={{0,30},{2,0},{4,2},{6,4},{8,6},{10,8},{12,10},{14,12},{16,14},{18,... | collective-permute-start | bytes 49160 | tf_op jit(solution)/shard_map/ppermute | solution.py:23

commit v4 on v3

--- a/solution.py
+++ b/solution.py
@@ -8,12 +8,14 @@
 from jax.experimental.pallas import tpu as pltpu
 from jax.sharding import PartitionSpec as P
 
+
 spectrum_center = 1.0
 spectrum_half = 6.0
 f32 = jnp.float32
 bf16 = jnp.bfloat16
 LANES = 128
 FACE = 96
+FOLD = 32
 CONST_ROWS = 16
 
 
@@ -27,7 +29,9 @@
     count = lax.axis_size(axis)
     within = [(source, source ^ 1) for source in range(count)]
     across = [(source, (source + (1 if source % 2 else -1)) % count) for source in range(count)]
-    return lax.ppermute(inner, axis, within), lax.ppermute(outer, axis, across)
+    outer = lax.ppermute(outer, axis, across)
+    inner = lax.ppermute(inner, axis, within)
+    return inner, outer
 
 
 def is_odd():
@@ -253,28 +257,29 @@
     copies = [
         pltpu.make_async_copy(source, target, sems.at[k])
         for k, (source, target) in enumerate((
-            (mass_hbm, mass), (wave_hbm, wave), (perm_hbm, perm), (up_hbm.at[0], proj.at[:ch]),
+            (mass_hbm, mass), (perm_hbm, perm), (wave_hbm, wave), (up_hbm.at[0], proj.at[:ch]),
             (low_hbm.at[0], proj.at[ch:]), (stiff_hbm, stiff), (scale_hbm, scale_in), (kb_hbm, kb), (pot_hbm, pot),
         ))
     ]
     for copy in copies:
         copy.start()
+    count_rows = stiff.shape[0]
     copies[0].wait()
     widen(g, mass, mass_wide)
     copies[1].wait()
+    sublane = lax.broadcasted_iota(jnp.int32, (count_rows, g.padded), 0).astype(f32)
+    pick_t = (perm[...] == sublane).astype(f32).astype(bf16)
+    copies[2].wait()
     for p in range(g.e):
         rows = pl.ds(p * g.plane, g.plane)
         start = wave[p].astype(f32).reshape(g.plane, LANES)
         slab[rows, :] = (mass_wide[rows, :] * start).astype(bf16).astype(f32)
     gather_out(g, slab, x_top, x_held, ucol[0])
-    for copy in copies[2:]:
+    for copy in copies[3:]:
         copy.wait()
     for k in range(8):
         one = scale_in[k // 4, k % 4 // 2 : k % 4 // 2 + 1, k % 2 : k % 2 + 1]
         scale[k : k + 1, :] = jnp.broadcast_to(one, (1, LANES))
-    count_rows = stiff.shape[0]
-    sublane = lax.broadcasted_iota(jnp.int32, (count_rows, g.padded), 0).astype(f32)
-    pick_t = (perm[...] == sublane).astype(f32).astype(bf16)
     first = g.face_rows // 16 * 16
     left = jnp.concatenate([proj[...], stiff[first:, :]], axis=0)
     ordered = dot(left, pick_t)
@@ -285,8 +290,11 @@
     both[...] = turned
     outgoing(g, acol[0], scale, slab, x_top, x_held, kface, both_t, face_sums, up, down, own_out, held_out)
     at = g.plane + ch
-    up[at : at + FACE, :] = jnp.zeros((FACE, LANES), bf16)
-    up[at : at + FACE, :ch] = turned[:FACE, ch:]
+    folded = [turned[k : k + FOLD, ch:] for k in range(0, FACE, FOLD)]
+    rest = LANES - len(folded) * ch
+    if rest:
+        folded.append(jnp.zeros((FOLD, rest), bf16))
+    up[at : at + FOLD, :] = jnp.concatenate(folded, axis=1)
     shape = (CONST_ROWS, LANES)
     row = lax.broadcasted_iota(jnp.int32, shape, 0)
     values = jnp.zeros(shape, f32)
@@ -303,7 +311,7 @@
     high = full.astype(bf16).astype(f32)
     values = jnp.where(row == 12, high, values)
     values = jnp.where(row == 13, full - high, values)
-    up[at + FACE :, :] = values.astype(bf16)
+    up[at + FOLD :, :] = values.astype(bf16)
     post(up, down, inner, outer)
 
 
@@ -374,9 +382,7 @@
             low_new[rows, :] = value.astype(bf16).astype(f32)
 
 
-def neighbour_terms(
-    g, acol, count, both, both_t, own, held, kb, face_low, const, up, down, x_face, next_plane, x_next,
-):
+def neighbour_terms(g, acol, count, both_t, own, held, kb, face_low, const, up, down, x_face, next_plane, x_next):
     ch = g.ch
     next_plane[...] = down[: g.plane, :].astype(f32)
     for k, (a, b) in enumerate(g.columns):
@@ -461,11 +467,13 @@
     d = g.d
     half = d * g.plane
     collect(inner, outer, up, down)
-    kept[...] = up[at:, :]
-    face_low = up[at : at + FACE, : g.ch]
-    const = up[at + FACE :, :].astype(f32)
+    for k in range(FACE // FOLD):
+        kept[k * FOLD : (k + 1) * FOLD, : g.ch] = up[at : at + FOLD, k * g.ch : (k + 1) * g.ch]
+    kept[FACE:, :] = up[at + FOLD :, :]
+    face_low = kept[:FACE, : g.ch]
+    const = kept[FACE:, :].astype(f32)
     mine, low = neighbour_terms(
-        g, acol[0], count[0], both, both_t, own, held, kb, face_low, const, up, down, x_face, next_plane, x_next
+        g, acol[0], count[0], both_t, own, held, kb, face_low, const, up, down, x_face, next_plane, x_next
     )
     lifted_up = dot(both[: g.used, : g.ch], low)
     upper_sums(g, acol[0], scale, ordered, both, x_next, mine, sums)
@@ -506,7 +514,7 @@
     face_low = kept[:FACE, :ch]
     const = kept[FACE:, :].astype(f32)
     mine, low = neighbour_terms(
-        g, acol[0], count[0], both, both_t, own, held, kb, face_low, const, up, down, x_face, next_plane, x_next
+        g, acol[0], count[0], both_t, own, held, kb, face_low, const, up, down, x_face, next_plane, x_next
     )
     mine_out[...] = mine
     lifted_up = dot(both[: g.used, :ch], low)
@@ -541,14 +549,25 @@
 
 def last_high_kernel(
     g, acol, ucol, count, scale, mass_wide, before, low_new, ordered, both, both_t, new, mine, x_next,
-    filtered, own_out, sums, field, x_own,
+    filtered, own_out, sums, field, x_own, done, sems,
 ):
     d = g.d
     half = d * g.plane
+    copies = [
+        pltpu.make_async_copy(done.at[pl.ds(p, n)], filtered.at[pl.ds(p, n)], sems.at[k])
+        for k, (p, n) in enumerate(((0, d), (d, d)))
+    ]
+
+    def give(planes):
+        for p in planes:
+            done[p] = field[p * g.plane : (p + 1) * g.plane, :].astype(bf16).reshape(g.e, g.e, LANES)
+
     field[:half, :] = low_new[...]
     for rows, _ in held_places(g, ucol[0], None):
         field[rows, :] = new[rows, :]
     field[: g.plane, :] = new[: g.plane, :]
+    give(range(d))
+    copies[0].start()
     field[half : half + g.plane, :] = new[half : half + g.plane, :]
     upper_sums(g, acol[0], scale, ordered, both, x_next, mine[...], sums)
     for p in range(1, d):
@@ -556,14 +575,16 @@
         added = sums[p * g.plane : (p + 1) * g.plane, :]
         value = before[rows, :] + mass_wide[rows, :] * (added * (2.0 / spectrum_half))
         field[rows, :] = value.astype(bf16).astype(f32)
-    for p in range(g.e):
-        filtered[p] = field[p * g.plane : (p + 1) * g.plane, :].astype(bf16).reshape(g.e, g.e, LANES)
+    give(range(d, g.e))
+    copies[1].start()
     a, b = split_element(acol[0])
     g.gather_element(field, x_own, 0, half, a, b, False)
     own_out[...] = dot(both_t[g.ch :, :], x_own[...])
-
-
-def call(kernel, name, scalars, operands, outs, scratch, flops, limit=24 << 20, hbm=False):
+    for copy in copies:
+        copy.wait()
+
+
+def call(kernel, scalars, operands, outs, scratch, flops, limit=24 << 20, hbm=False, far_outs=0):
     smem = pl.BlockSpec(memory_space=pltpu.SMEM)
     vmem = pl.BlockSpec(memory_space=pltpu.VMEM)
     far = pl.BlockSpec(memory_space=pltpu.MemorySpace.HBM)
@@ -572,10 +593,9 @@
         operands = [pltpu.with_memory_space_constraint(v, pltpu.MemorySpace.HBM) for v in operands]
     return pl.pallas_call(
         kernel,
-        name=name,
         out_shape=[jax.ShapeDtypeStruct(s, t) for s, t in outs],
         in_specs=[smem] * len(scalars) + [far if hbm else vmem] * len(operands),
-        out_specs=[vmem] * len(outs),
+        out_specs=[far] * far_outs + [vmem] * (len(outs) - far_outs),
         scratch_shapes=[pltpu.VMEM(*s) if isinstance(s, tuple) else s for s in scratch],
         compiler_params=pltpu.CompilerParams(vmem_limit_bytes=limit),
         cost_estimate=pl.CostEstimate(flops=flops, bytes_accessed=moved, transcendentals=0),
@@ -599,12 +619,12 @@
     slab_s, half_s, plane_s = ((nodes, LANES), f32), ((nodes // 2, LANES), f32), ((plane, LANES), f32)
     x_s, x_one_s = ((padded, 4 * LANES), bf16), ((padded, LANES), bf16)
     wire_s = ((plane + ch, LANES), bf16)
-    wire_first_s = ((plane + ch + FACE + CONST_ROWS, LANES), bf16)
+    wire_first_s = ((plane + ch + FOLD + CONST_ROWS, LANES), bf16)
     face_s = ((LANES, 4 * LANES), bf16)
     face_sum_s = ((FACE, 4 * LANES), f32)
 
     slab, x_top, mass_wide, wave, stiff, scale, order_row, pot, kb, both, both_t, own, held, inner, outer = call(
-        functools.partial(start_kernel, g), "start", scalars,
+        functools.partial(start_kernel, g), scalars,
         (wave_in, mass_scale, elem_scale, stiffness, jnp.swapaxes(proj_lower, 1, 2), jnp.swapaxes(proj_upper, 1, 2),
          kb_coef, perm, potential),
         [slab_s, x_s, slab_s, (wave_in.shape, bf16), (stiffness.shape, bf16), ((8, LANES), f32), (perm.shape, f32),
@@ -615,38 +635,39 @@
     )
     inner, outer = swapped(inner, outer, "space")
     ordered, pot_wide = call(
-        functools.partial(order_kernel, g), "order", (), (stiff, order_row, pot),
+        functools.partial(order_kernel, g), (), (stiff, order_row, pot),
         [((padded, padded), bf16), slab_s], [], 2 * 10**9,
     )
     bulk_scratch = [slab_s, ((used, 2 * LANES), f32), x_s]
     before, low_step, low_slab, face_own, x_face = call(
-        functools.partial(bulk_kernel, g), "bulk", (), (scale, ordered, x_top, slab, pot_wide, mass_wide, wave),
+        functools.partial(bulk_kernel, g), (), (scale, ordered, x_top, slab, pot_wide, mass_wide, wave),
         [slab_s, half_s, half_s, face_sum_s, face_s], bulk_scratch, 2 * 10**9,
     )
     shared = (ordered, both, both_t)
     slab, x_top, step, own, held, inner, outer, kept = call(
-        functools.partial(middle_kernel, g), "middle", scalars,
+        functools.partial(middle_kernel, g), scalars,
         (scale, mass_wide, before, low_step, low_slab, face_own, x_face, *shared, own, held, kb, inner, outer),
         [slab_s, x_s, slab_s, part, part, wire_s, wire_s, ((FACE + CONST_ROWS, LANES), bf16)],
         [half_s, plane_s, face_s, plane_s, wire_first_s, wire_s, wire_s, wire_s, plane_s, x_one_s], 10**8,
     )
     inner, outer = swapped(inner, outer, "space")
     before, low_new, face_own, x_face = call(
-        functools.partial(bulk_last_kernel, g), "bulk_last", (),
+        functools.partial(bulk_last_kernel, g), (),
         (scale, ordered, x_top, slab, pot_wide, mass_wide, wave, step),
         [slab_s, half_s, face_sum_s, face_s], bulk_scratch, 2 * 10**9,
     )
     held, new, mine, x_next = call(
-        functools.partial(last_low_kernel, g), "last_low", scalars,
+        functools.partial(last_low_kernel, g), scalars,
         (scale, mass_wide, before, face_own, x_face, *shared, own, held, kb, kept, inner, outer),
         [part, ((nodes // 2 + plane, LANES), f32), ((ch, LANES), bf16), face_s],
         [plane_s, plane_s, x_one_s, face_s, wire_s, wire_s, plane_s], 10**8,
     )
     held = shifted(held, "space", -1)
     filtered, own = call(
-        functools.partial(last_high_kernel, g), "last_high", scalars,
+        functools.partial(last_high_kernel, g), scalars,
         (scale, mass_wide, before, low_new, *shared, new, mine, x_next),
-        [(wave_in.shape, bf16), part], [half_s, slab_s, x_one_s], 10**9,
+        [(wave_in.shape, bf16), part],
+        [half_s, slab_s, x_one_s, (wave_in.shape, bf16), pltpu.SemaphoreType.DMA((2,))], 10**9, far_outs=1,
     )
     return filtered, (own + held)[None]
 

time: 30.8 us -> 30.7 us (level)
  starting transfers between devices: 9.93 us -> 9.45 us
where the time goes in v4:
time: 30.7 us; the launch traced here: 30.4 us
  Pallas kernels  15.2 us (50%)
  starting transfers between devices  9.45 us (31%)
  between operations  2.66 us (9%)
  waiting for transfers between devices  2.42 us (8%)
  other arithmetic  0.61 us (2%)
    pallas_call x7, Pallas kernels, call(): pl.pallas_call(kernel, out_shape=[jax.ShapeDtypeStruct(s, t) for s, t in...  15.2 us
    ppermute x2, starting transfers between devices, swapped(): outer = lax.ppermute(outer, axis, across)  7.25 us
    ppermute x2, waiting for transfers between devices, swapped(): outer = lax.ppermute(outer, axis, across)  2.42 us
    ppermute x1, starting transfers between devices, shifted(): return lax.ppermute(value, axis, pairs)  1.58 us
    ppermute x2, starting transfers between devices, swapped(): inner = lax.ppermute(inner, axis, within)  0.62 us
  transfers between devices with their start and end apart: 5, of which 1 were waited for; matrix products, arithmetic and copies ran while one was open for 0% of the time, Pallas kernels for 31%

profile of v4, /device:TPU:0, one launch (start us, length us, event | category | flops | bytes accessed | tf_op | source)
XLA Modules:
  0.0 30.4 jit_solution(15306165233695041871)
XLA Ops:
  2.6 2.7 %shard_map.131 = (f32[4096,128]{1,0:T(8,128)S(1)}, bf16[768,512]{1,0:T(8,128)(2,1)S(1)}, f32[4096,128]{1,0:T(8,128)S(1)}, bf16[16,16,16,128]{3,2,1,0:T(8,128)(2,...) custom-call(s32[1]{0:T(128)S(6)} %copy.14.acol, ...), custom_call_target="tpu_custom_call" | custom-call | flops 100000000 | bytes 2240770 | tf_op jit(solution)/shard_map/pallas_call | solution.py:594
  5.2 0.6 %collective-permute-start = (bf16[336,128]{1,0:T(8,128)(2,1)S(1)}, bf16[336,128]{1,0:T(8,128)(2,1)S(1)}, u32[]{:S(2)}, u32[]{:S(2)}) collective-permute-start(bf16[336,128]{1,0:T(8,128)(2,1)S(1)} %get-tuple-element.62), channel_id=1, source_target_pairs={{0,2},{2,0},{4,6},{6,4},{8,10},{10,8},{12,14},{14,12},{16,18},{18,... | collective-permute-start | bytes 258056 | tf_op jit(solution)/shard_map/ppermute | solution.py:33
  5.8 5.6 %collective-permute-start.1 = (bf16[336,128]{1,0:T(8,128)(2,1)S(1)}, bf16[336,128]{1,0:T(8,128)(2,1)S(1)}, u32[]{:S(2)}, u32[]{:S(2)}) collective-permute-start(bf16[336,128]{1,0:T(8,128)(2,1)S(1)} %get-tuple-element.63), channel_id=1, source_target_pairs={{0,30},{2,4},{4,2},{6,8},{8,6},{10,12},{12,10},{14,16},{16,14},{18... | collective-permute-start | bytes 258056 | tf_op jit(solution)/shard_map/ppermute | solution.py:32
  11.4 2.5 %shard_map.132 = (bf16[768,768]{1,0:T(8,128)(2,1)S(1)}, f32[4096,128]{1,0:T(8,128)S(1)}) custom-call(bf16[729,729]{1,0:T(8,128)(2,1)S(1)} %get-tuple-element.44.stiff, f32[1,768]{1,0:T(1,128)S(1)} %get-tuple-element.45.perm, f32[16,256]{1,0:T(8,128)S(1)} %get-tuple-element.46.pot), custom_call_target="tpu_custom_call" | custom-call | flops 2000000000 | bytes 1082338 | tf_op jit(solution)/shard_map/pallas_call | solution.py:594
  13.9 2.5 %shard_map.133 = (f32[4096,128]{1,0:T(8,128)S(1)}, f32[2048,128]{1,0:T(8,128)S(1)}, f32[2048,128]{1,0:T(8,128)S(1)}, f32[96,512]{1,0:T(8,128)S(1)}, bf16[128,512]{1,0:T(8,128)(2,1)S(1)}) custom-call(f32[8,128]{1,0:T(8,128)S(1)} %get-tuple-element.42.scale, bf16[768,768]{1,0:T(8,128)(2,1)S(1)} %get-tuple-element.47.ordered, ...), custom_call_target="tpu_custom_call" | custom-call | flops 2000000000 | bytes 9310208 | tf_op jit(solution)/shard_map/pallas_call | solution.py:594
  16.4 0.0 collective-permute-done.inner
  16.4 0.0 collective-permute-done.1.outer
  16.4 2.3 %shard_map.134 = (f32[4096,128]{1,0:T(8,128)S(1)}, bf16[768,512]{1,0:T(8,128)(2,1)S(1)}, f32[4096,128]{1,0:T(8,128)S(1)}, f32[32,128]{1,0:T(8,128)S(1)}, f32[32,...) custom-call(s32[1]{0:T(128)S(6)} %copy.14.acol, ...), custom_call_target="tpu_custom_call" | custom-call | flops 100000000 | bytes 8204416 | tf_op jit(solution)/shard_map/pallas_call | solution.py:594
  18.8 0.1 collective-permute-start.2
  18.8 1.6 %collective-permute-start.3 = (bf16[288,128]{1,0:T(8,128)(2,1)S(1)}, bf16[288,128]{1,0:T(8,128)(2,1)S(1)}, u32[]{:S(2)}, u32[]{:S(2)}) collective-permute-start(bf16[288,128]{1,0:T(8,128)(2,1)S(1)} %get-tuple-element.75), channel_id=1, source_target_pairs={{0,30},{2,4},{4,2},{6,8},{8,6},{10,12},{12,10},{14,16},{16,14},{18... | collective-permute-start | bytes 221192 | tf_op jit(solution)/shard_map/ppermute | solution.py:32
  20.5 2.5 %shard_map.135 = (f32[4096,128]{1,0:T(8,128)S(1)}, f32[2048,128]{1,0:T(8,128)S(1)}, f32[96,512]{1,0:T(8,128)S(1)}, bf16[128,512]{1,0:T(8,128)(2,1)S(1)}) custom-call(f32[8,128]{1,0:T(8,128)S(1)} %get-tuple-element.42.scale, bf16[768,768]{1,0:T(8,128)(2,1)S(1)} %get-tuple-element.47.ordered, bf16[768,512]{1,0:T(8,128)(2,1)S(1)} %get-tuple-element.64.x_top, ...), custom_call_target="tpu_custom_call" | custom-call | flops 2000000000 | bytes 11407360 | tf_op jit(solution)/shard_map/pallas_call | solution.py:594
  23.0 0.0 collective-permute-done.2.inner
  23.0 2.4 %collective-permute-done.3.outer = bf16[288,128]{1,0:T(8,128)(2,1)S(1)} collective-permute-done((bf16[288,128]{1,0:T(8,128)(2,1)S(1)}, bf16[288,128]{1,0:T(8,128)(2,1)S(1)}, u32[]{:S(2)}, u32[]{:S(2)}) %collective-permute-start.3) | collective-permute-done | bytes 73760 | tf_op jit(solution)/shard_map/ppermute | solution.py:32
  25.4 0.8 %shard_map.136 = (f32[32,128]{1,0:T(8,128)S(1)}, f32[2304,128]{1,0:T(8,128)S(1)}, bf16[32,128]{1,0:T(8,128)(2,1)S(1)}, bf16[128,512]{1,0:T(8,128)(2,1)S(1)}) custom-call(s32[1]{0:T(128)S(6)} %copy.14.acol, s32[1]{0:T(128)S(6)} %copy.16.ucol, s32[1]{0:T(128)S(6)} %copy.15.count, f32[8,128]{1,0:T(8,128)S(1)} %get-tuple-element.42.scale, ...), custom_call_target="tpu_custom_call" | custom-call | flops 100000000 | bytes 6111360 | tf_op jit(solution)/shard_map/pallas_call | solution.py:594
  26.2 1.6 %collective-permute-start.4 = (f32[32,128]{1,0:T(8,128)S(1)}, f32[32,128]{1,0:T(8,128)S(1)}, u32[]{:S(2)}, u32[]{:S(2)}) collective-permute-start(f32[32,128]{1,0:T(8,128)S(1)} %get-tuple-element.81), channel_id=1, source_target_pairs={{0,30},{2,0},{4,2},{6,4},{8,6},{10,8},{12,10},{14,12},{16,14},{18,... | collective-permute-start | bytes 49160 | tf_op jit(solution)/shard_map/ppermute | solution.py:25
  27.8 2.0 %shard_map.137 = (bf16[16,16,16,128]{3,2,1,0:T(8,128)(2,1)}, f32[32,128]{1,0:T(8,128)S(1)}) custom-call(s32[1]{0:T(128)S(6)} %copy.14.acol, s32[1]{0:T(128)S(6)} %copy.16.ucol, s32[1]{0:T(128)S(6)} %copy.15.count, f32[8,128]{1,0:T(8,128)S(1)} %get-tuple-element.42.scale, f32[4096,128]{1,0:T(8,128)S(1)} %get-tuple-element.43.mass_wide, ...), custom_call_target="tpu_custom_call" | custom-call | flops 1000000000 | bytes 7942144 | tf_op jit(solution)/shard_map/pallas_call | solution.py:594
  29.7 0.0 collective-permute-done.4
  29.8 0.6 %add_bitcast_fusion = f32[1,32,128]{2,1,0:T(8,128)} fusion(f32[32,128]{1,0:T(8,128)S(1)} %get-tuple-element.80, f32[32,128]{1,0:T(8,128)S(1)} %collective-permute-done.4), kind=kLoop, calls=%fused_computation | loop fusion | flops 4096 | bytes 49152 | tf_op jit(solution)/shard_map/broadcast_in_dim | solution.py:672
Async XLA Ops:
  5.2 11.2 %collective-permute-start = (bf16[336,128]{1,0:T(8,128)(2,1)S(1)}, bf16[336,128]{1,0:T(8,128)(2,1)S(1)}, u32[]{:S(2)}, u32[]{:S(2)}) collective-permute-start(bf16[336,128]{1,0:T(8,128)(2,1)S(1)} %get-tuple-element.62), channel_id=1, source_target_pairs={{0,2},{2,0},{4,6},{6,4},{8,10},{10,8},{12,14},{14,12},{16,18},{18,... | collective-permute-start | bytes 258056 | tf_op jit(solution)/shard_map/ppermute | solution.py:33
  5.8 10.6 %collective-permute-start.1 = (bf16[336,128]{1,0:T(8,128)(2,1)S(1)}, bf16[336,128]{1,0:T(8,128)(2,1)S(1)}, u32[]{:S(2)}, u32[]{:S(2)}) collective-permute-start(bf16[336,128]{1,0:T(8,128)(2,1)S(1)} %get-tuple-element.63), channel_id=1, source_target_pairs={{0,30},{2,4},{4,2},{6,8},{8,6},{10,12},{12,10},{14,16},{16,14},{18... | collective-permute-start | bytes 258056 | tf_op jit(solution)/shard_map/ppermute | solution.py:32
  18.8 4.2 %collective-permute-start.2 = (bf16[288,128]{1,0:T(8,128)(2,1)S(1)}, bf16[288,128]{1,0:T(8,128)(2,1)S(1)}, u32[]{:S(2)}, u32[]{:S(2)}) collective-permute-start(bf16[288,128]{1,0:T(8,128)(2,1)S(1)} %get-tuple-element.74), channel_id=1, source_target_pairs={{0,2},{2,0},{4,6},{6,4},{8,10},{10,8},{12,14},{14,12},{16,18},{18,... | collective-permute-start | bytes 221192 | tf_op jit(solution)/shard_map/ppermute | solution.py:33
  18.8 6.5 %collective-permute-start.3 = (bf16[288,128]{1,0:T(8,128)(2,1)S(1)}, bf16[288,128]{1,0:T(8,128)(2,1)S(1)}, u32[]{:S(2)}, u32[]{:S(2)}) collective-permute-start(bf16[288,128]{1,0:T(8,128)(2,1)S(1)} %get-tuple-element.75), channel_id=1, source_target_pairs={{0,30},{2,4},{4,2},{6,8},{8,6},{10,12},{12,10},{14,16},{16,14},{18... | collective-permute-start | bytes 221192 | tf_op jit(solution)/shard_map/ppermute | solution.py:32
  26.2 3.5 %collective-permute-start.4 = (f32[32,128]{1,0:T(8,128)S(1)}, f32[32,128]{1,0:T(8,128)S(1)}, u32[]{:S(2)}, u32[]{:S(2)}) collective-permute-start(f32[32,128]{1,0:T(8,128)S(1)} %get-tuple-element.81), channel_id=1, source_target_pairs={{0,30},{2,0},{4,2},{6,4},{8,6},{10,8},{12,10},{14,12},{16,14},{18,... | collective-permute-start | bytes 49160 | tf_op jit(solution)/shard_map/ppermute | solution.py:25

commit v5 on v4

--- a/solution.py
+++ b/solution.py
@@ -251,7 +251,7 @@
 def start_kernel(
     g, acol, ucol, count, wave_hbm, mass_hbm, scale_hbm, stiff_hbm, low_hbm, up_hbm, kb_hbm, perm_hbm, pot_hbm,
     slab, x_top, mass_wide, wave, stiff, scale, perm, pot, kb, both, both_t, own_out, held_out, inner, outer,
-    face_sums, up, down, mass, scale_in, proj, x_held, sems,
+    face_sums, up, down, mass, scale_in, proj, x_held, natural, pair, sems,
 ):
     ch = g.ch
     copies = [
@@ -263,31 +263,30 @@
     ]
     for copy in copies:
         copy.start()
-    count_rows = stiff.shape[0]
     copies[0].wait()
     widen(g, mass, mass_wide)
-    copies[1].wait()
-    sublane = lax.broadcasted_iota(jnp.int32, (count_rows, g.padded), 0).astype(f32)
-    pick_t = (perm[...] == sublane).astype(f32).astype(bf16)
     copies[2].wait()
     for p in range(g.e):
         rows = pl.ds(p * g.plane, g.plane)
         start = wave[p].astype(f32).reshape(g.plane, LANES)
         slab[rows, :] = (mass_wide[rows, :] * start).astype(bf16).astype(f32)
     gather_out(g, slab, x_top, x_held, ucol[0])
-    for copy in copies[3:]:
-        copy.wait()
+    for k, copy in enumerate(copies):
+        if k not in (0, 2):
+            copy.wait()
     for k in range(8):
         one = scale_in[k // 4, k % 4 // 2 : k % 4 // 2 + 1, k % 2 : k % 2 + 1]
         scale[k : k + 1, :] = jnp.broadcast_to(one, (1, LANES))
-    first = g.face_rows // 16 * 16
-    left = jnp.concatenate([proj[...], stiff[first:, :]], axis=0)
-    ordered = dot(left, pick_t)
-    both_t[...] = ordered[: 2 * ch].astype(bf16)
-    kface = dot(onehot_rows(perm[:, :LANES] - first, count_rows - first)[:FACE], ordered[2 * ch :].astype(bf16))
-    kface = kface.astype(bf16)
-    turned = ordered[: 2 * ch].T.astype(bf16)
+    size = stiff.shape[0]
+    first = g.face_rows // LANES * LANES
+    natural[1] = jnp.zeros((g.used, LANES), f32)
+    natural[0, :size, : 2 * ch] = proj[...].astype(f32).T
+    natural[1, :size, : size - first] = stiff[:, first:].astype(f32)
+    reorder_rows(g, natural, pair)
+    turned = pair[:, : 2 * ch]
     both[...] = turned
+    both_t[...] = pair[:, :LANES].astype(f32).T[: 2 * ch].astype(bf16)
+    kface = dot_nt(onehot_rows(perm[:, :LANES] - first, LANES)[:FACE], pair[:, LANES:]).astype(bf16)
     outgoing(g, acol[0], scale, slab, x_top, x_held, kface, both_t, face_sums, up, down, own_out, held_out)
     at = g.plane + ch
     folded = [turned[k : k + FOLD, ch:] for k in range(0, FACE, FOLD)]
@@ -315,14 +314,37 @@
     post(up, down, inner, outer)
 
 
-def order_kernel(g, stiff, perm, pot, ordered, pot_wide):
+def reorder_rows(g, natural, rows):
+    d, n = g.d, g.d + 1
+    places = [((d * n + j) * n, 1) for j in range(n)] + [(d * n * n + d, n), (d * n * n + d * n + d, 0)]
+    places += [((i * n + j) * n, 1) for i in range(d) for j in range(d)]
+    places += [((i * n + d) * n, 1) for i in range(d)]
+    places += [(i * n * n + d, n) for i in range(d)]
+    places += [(d * n + d, n * n)]
+    for t in range(natural.shape[0]):
+        groups = []
+        for start, stride in places:
+            group = natural[t, pl.ds(start, d, stride=max(stride, 1)), :]
+            if stride == 0:
+                group = jnp.where(lax.broadcasted_iota(jnp.int32, group.shape, 0) == 0, group, 0.0)
+            groups.append(group)
+        g.pack(rows, t * LANES, groups)
+    rows[g.used :, :] = jnp.zeros((g.padded - g.used, rows.shape[1]), bf16)
+
+
+def order_kernel(g, stiff, perm, pot, ordered, pot_wide, natural, rows):
+    size = stiff.shape[0]
+    tiles = natural.shape[0]
+    for t in range(tiles):
+        lanes = min(LANES, size - t * LANES)
+        if lanes < LANES:
+            natural[t] = jnp.zeros((g.used, LANES), f32)
+        natural[t, :size, :lanes] = stiff[:, t * LANES : t * LANES + lanes].astype(f32)
+    reorder_rows(g, natural, rows)
+    sublane = lax.broadcasted_iota(jnp.int32, (rows.shape[1], g.padded), 0).astype(f32)
+    pick_t = (perm[...] == sublane).astype(f32).astype(bf16)
+    ordered[...] = dot(rows[...], pick_t).astype(bf16)
     widen(g, pot, pot_wide)
-    pick = onehot_rows(perm[...], stiff.shape[0])
-    part = perm.shape[1] // 3
-    for k in range(3):
-        rows = slice(k * part, (k + 1) * part)
-        half = dot(pick[rows], stiff[...]).astype(bf16)
-        ordered[rows, :] = dot_nt(half, pick).astype(bf16)
 
 
 def bulk_sums(g, scale, ordered, x_top, slab, pot_wide, face_own, x_face, total, z, x_low):
@@ -426,15 +448,9 @@
     lifted = dot(both[: g.used, g.ch :], mine)
 
     def loader(k):
-        here = jnp.where(acol == k, 1.0, 0.0)
         factor = scale[4 + k : 5 + k, :]
         lane = k * LANES
-
-        def load(n):
-            rows = slice(n * d, (n + 1) * d)
-            return upper[rows, lane : lane + LANES] * factor + lifted[rows] * here
-
-        return load
+        return lambda n: upper[n * d : (n + 1) * d, lane : lane + LANES] * factor
 
     for k, (a, b) in enumerate(g.columns):
         load = loader(k)
@@ -444,6 +460,8 @@
                 sums[pl.ds(near + i * g.plane + j * g.e, d), :] = load(g.face_groups + i * d + j)
     for k, (a, b) in enumerate(g.columns):
         g.add_layer(sums, 0, a, b, loader(k), start=d * d)
+    a, b = split_element(acol)
+    g.add_layer(sums, 0, a, b, lambda n: lifted[n * d : (n + 1) * d])
 
 
 def held_places(g, ucol, lifted_up):
@@ -631,12 +649,14 @@
          (potential.shape, f32), (kb_coef.shape, f32), ((padded, 2 * ch), bf16), ((2 * ch, padded), bf16), part, part,
          wire_first_s, wire_first_s],
         [plane_s, wire_first_s, wire_s, (mass_scale.shape, f32), (elem_scale.shape, f32),
-         ((2 * ch, stiffness.shape[0]), bf16), x_one_s, pltpu.SemaphoreType.DMA((9,))], 10**8, hbm=True,
+         ((2 * ch, stiffness.shape[0]), bf16), x_one_s, ((2, used, LANES), f32), ((padded, 2 * LANES), bf16),
+         pltpu.SemaphoreType.DMA((9,))], 10**8, hbm=True,
     )
     inner, outer = swapped(inner, outer, "space")
     ordered, pot_wide = call(
         functools.partial(order_kernel, g), (), (stiff, order_row, pot),
-        [((padded, padded), bf16), slab_s], [], 2 * 10**9,
+        [((padded, padded), bf16), slab_s],
+        [((-(-stiffness.shape[0] // LANES), used, LANES), f32), ((padded, padded), bf16)], 2 * 10**9,
     )
     bulk_scratch = [slab_s, ((used, 2 * LANES), f32), x_s]
     before, low_step, low_slab, face_own, x_face = call(

time: 30.7 us -> 30 us (0.977)
  starting transfers between devices: 9.45 us -> 11.4 us
  Pallas kernels: 15.2 us -> 13.6 us
  waiting for transfers between devices: 2.42 us -> 1.46 us
    pallas_call x7, Pallas kernels: 15.2 us -> 13.6 us  [call(): pl.pallas_call(kernel, out_shape=[jax.ShapeDtypeStruct(s, t) for s, t in...]
    ppermute x2, waiting for transfers between devices: 2.42 us -> 1.45 us  [swapped(): outer = lax.ppermute(outer, axis, across)]
    ppermute x1, starting transfers between devices: 1.58 us -> 2.54 us  [shifted(): return lax.ppermute(value, axis, pairs)]
    ppermute x2, starting transfers between devices: 7.25 us -> 8.21 us  [swapped(): outer = lax.ppermute(outer, axis, across)]
  transfers between devices with their start and end apart: 5 -> 5, of which waited for: 1 -> 1; matrix products, arithmetic and copies ran while one was open for 0% -> 0% of each run, Pallas kernels for 31% -> 28%
where the time goes in v5:
time: 30 us; the launch traced here: 29.7 us
  Pallas kernels  13.6 us (45%)
  starting transfers between devices  11.4 us (38%)
  between operations  2.66 us (9%)
  waiting for transfers between devices  1.46 us (5%)
  other arithmetic  0.61 us (2%)
    pallas_call x7, Pallas kernels, call(): pl.pallas_call(kernel, out_shape=[jax.ShapeDtypeStruct(s, t) for s, t in...  13.6 us
    ppermute x2, starting transfers between devices, swapped(): outer = lax.ppermute(outer, axis, across)  8.21 us
    ppermute x1, starting transfers between devices, shifted(): return lax.ppermute(value, axis, pairs)  2.54 us
    ppermute x2, waiting for transfers between devices, swapped(): outer = lax.ppermute(outer, axis, across)  1.45 us
    ppermute x2, starting transfers between devices, swapped(): inner = lax.ppermute(inner, axis, within)  0.62 us
    broadcast_in_dim x1, other arithmetic, per_device(): return (filtered, (own + held)[None])  0.61 us
  transfers between devices with their start and end apart: 5, of which 1 were waited for; matrix products, arithmetic and copies ran while one was open for 0% of the time, Pallas kernels for 28%

profile of v5, /device:TPU:0, one launch (start us, length us, event | category | flops | bytes accessed | tf_op | source)
XLA Modules:
  0.0 29.7 jit_solution(1453459303636788343)
XLA Ops:
  2.6 2.6 %shard_map.131 = (f32[4096,128]{1,0:T(8,128)S(1)}, bf16[768,512]{1,0:T(8,128)(2,1)S(1)}, f32[4096,128]{1,0:T(8,128)S(1)}, bf16[16,16,16,128]{3,2,1,0:T(8,128)(2,...) custom-call(s32[1]{0:T(128)S(6)} %copy.14.acol, ...), custom_call_target="tpu_custom_call" | custom-call | flops 100000000 | bytes 2240770 | tf_op jit(solution)/shard_map/pallas_call | solution.py:612
  5.2 0.6 %collective-permute-start = (bf16[336,128]{1,0:T(8,128)(2,1)S(1)}, bf16[336,128]{1,0:T(8,128)(2,1)S(1)}, u32[]{:S(2)}, u32[]{:S(2)}) collective-permute-start(bf16[336,128]{1,0:T(8,128)(2,1)S(1)} %get-tuple-element.62), channel_id=1, source_target_pairs={{0,2},{2,0},{4,6},{6,4},{8,10},{10,8},{12,14},{14,12},{16,18},{18,... | collective-permute-start | bytes 258056 | tf_op jit(solution)/shard_map/ppermute | solution.py:33
  5.7 5.6 %collective-permute-start.1 = (bf16[336,128]{1,0:T(8,128)(2,1)S(1)}, bf16[336,128]{1,0:T(8,128)(2,1)S(1)}, u32[]{:S(2)}, u32[]{:S(2)}) collective-permute-start(bf16[336,128]{1,0:T(8,128)(2,1)S(1)} %get-tuple-element.63), channel_id=1, source_target_pairs={{0,30},{2,4},{4,2},{6,8},{8,6},{10,12},{12,10},{14,16},{16,14},{18... | collective-permute-start | bytes 258056 | tf_op jit(solution)/shard_map/ppermute | solution.py:32
  11.4 1.5 %shard_map.132 = (bf16[768,768]{1,0:T(8,128)(2,1)S(1)}, f32[4096,128]{1,0:T(8,128)S(1)}) custom-call(bf16[729,729]{1,0:T(8,128)(2,1)S(1)} %get-tuple-element.44.stiff, f32[1,768]{1,0:T(1,128)S(1)} %get-tuple-element.45.perm, f32[16,256]{1,0:T(8,128)S(1)} %get-tuple-element.46.pot), custom_call_target="tpu_custom_call" | custom-call | flops 2000000000 | bytes 1082338 | tf_op jit(solution)/shard_map/pallas_call | solution.py:612
  12.9 2.5 %shard_map.133 = (f32[4096,128]{1,0:T(8,128)S(1)}, f32[2048,128]{1,0:T(8,128)S(1)}, f32[2048,128]{1,0:T(8,128)S(1)}, f32[96,512]{1,0:T(8,128)S(1)}, bf16[128,512]{1,0:T(8,128)(2,1)S(1)}) custom-call(f32[8,128]{1,0:T(8,128)S(1)} %get-tuple-element.42.scale, bf16[768,768]{1,0:T(8,128)(2,1)S(1)} %get-tuple-element.47.ordered, ...), custom_call_target="tpu_custom_call" | custom-call | flops 2000000000 | bytes 9310208 | tf_op jit(solution)/shard_map/pallas_call | solution.py:612
  15.4 0.0 collective-permute-done.inner
  15.4 0.0 collective-permute-done.1.outer
  15.4 2.0 %shard_map.134 = (f32[4096,128]{1,0:T(8,128)S(1)}, bf16[768,512]{1,0:T(8,128)(2,1)S(1)}, f32[4096,128]{1,0:T(8,128)S(1)}, f32[32,128]{1,0:T(8,128)S(1)}, f32[32,...) custom-call(s32[1]{0:T(128)S(6)} %copy.14.acol, ...), custom_call_target="tpu_custom_call" | custom-call | flops 100000000 | bytes 8204416 | tf_op jit(solution)/shard_map/pallas_call | solution.py:612
  17.4 0.1 collective-permute-start.2
  17.5 2.6 %collective-permute-start.3 = (bf16[288,128]{1,0:T(8,128)(2,1)S(1)}, bf16[288,128]{1,0:T(8,128)(2,1)S(1)}, u32[]{:S(2)}, u32[]{:S(2)}) collective-permute-start(bf16[288,128]{1,0:T(8,128)(2,1)S(1)} %get-tuple-element.75), channel_id=1, source_target_pairs={{0,30},{2,4},{4,2},{6,8},{8,6},{10,12},{12,10},{14,16},{16,14},{18... | collective-permute-start | bytes 221192 | tf_op jit(solution)/shard_map/ppermute | solution.py:32
  20.1 2.5 %shard_map.135 = (f32[4096,128]{1,0:T(8,128)S(1)}, f32[2048,128]{1,0:T(8,128)S(1)}, f32[96,512]{1,0:T(8,128)S(1)}, bf16[128,512]{1,0:T(8,128)(2,1)S(1)}) custom-call(f32[8,128]{1,0:T(8,128)S(1)} %get-tuple-element.42.scale, bf16[768,768]{1,0:T(8,128)(2,1)S(1)} %get-tuple-element.47.ordered, bf16[768,512]{1,0:T(8,128)(2,1)S(1)} %get-tuple-element.64.x_top, ...), custom_call_target="tpu_custom_call" | custom-call | flops 2000000000 | bytes 11407360 | tf_op jit(solution)/shard_map/pallas_call | solution.py:612
  22.6 0.0 collective-permute-done.2.inner
  22.6 1.5 %collective-permute-done.3.outer = bf16[288,128]{1,0:T(8,128)(2,1)S(1)} collective-permute-done((bf16[288,128]{1,0:T(8,128)(2,1)S(1)}, bf16[288,128]{1,0:T(8,128)(2,1)S(1)}, u32[]{:S(2)}, u32[]{:S(2)}) %collective-permute-start.3) | collective-permute-done | bytes 73760 | tf_op jit(solution)/shard_map/ppermute | solution.py:32
  24.0 0.8 %shard_map.136 = (f32[32,128]{1,0:T(8,128)S(1)}, f32[2304,128]{1,0:T(8,128)S(1)}, bf16[32,128]{1,0:T(8,128)(2,1)S(1)}, bf16[128,512]{1,0:T(8,128)(2,1)S(1)}) custom-call(s32[1]{0:T(128)S(6)} %copy.14.acol, s32[1]{0:T(128)S(6)} %copy.16.ucol, s32[1]{0:T(128)S(6)} %copy.15.count, f32[8,128]{1,0:T(8,128)S(1)} %get-tuple-element.42.scale, ...), custom_call_target="tpu_custom_call" | custom-call | flops 100000000 | bytes 6111360 | tf_op jit(solution)/shard_map/pallas_call | solution.py:612
  24.8 2.5 %collective-permute-start.4 = (f32[32,128]{1,0:T(8,128)S(1)}, f32[32,128]{1,0:T(8,128)S(1)}, u32[]{:S(2)}, u32[]{:S(2)}) collective-permute-start(f32[32,128]{1,0:T(8,128)S(1)} %get-tuple-element.81), channel_id=1, source_target_pairs={{0,30},{2,0},{4,2},{6,4},{8,6},{10,8},{12,10},{14,12},{16,14},{18,... | collective-permute-start | bytes 49160 | tf_op jit(solution)/shard_map/ppermute | solution.py:25
  27.4 1.7 %shard_map.137 = (bf16[16,16,16,128]{3,2,1,0:T(8,128)(2,1)}, f32[32,128]{1,0:T(8,128)S(1)}) custom-call(s32[1]{0:T(128)S(6)} %copy.14.acol, s32[1]{0:T(128)S(6)} %copy.16.ucol, s32[1]{0:T(128)S(6)} %copy.15.count, f32[8,128]{1,0:T(8,128)S(1)} %get-tuple-element.42.scale, f32[4096,128]{1,0:T(8,128)S(1)} %get-tuple-element.43.mass_wide, ...), custom_call_target="tpu_custom_call" | custom-call | flops 1000000000 | bytes 7942144 | tf_op jit(solution)/shard_map/pallas_call | solution.py:612
  29.1 0.0 collective-permute-done.4
  29.1 0.6 %add_bitcast_fusion = f32[1,32,128]{2,1,0:T(8,128)} fusion(f32[32,128]{1,0:T(8,128)S(1)} %get-tuple-element.80, f32[32,128]{1,0:T(8,128)S(1)} %collective-permute-done.4), kind=kLoop, calls=%fused_computation | loop fusion | flops 4096 | bytes 49152 | tf_op jit(solution)/shard_map/broadcast_in_dim | solution.py:692
Async XLA Ops:
  5.2 10.2 %collective-permute-start = (bf16[336,128]{1,0:T(8,128)(2,1)S(1)}, bf16[336,128]{1,0:T(8,128)(2,1)S(1)}, u32[]{:S(2)}, u32[]{:S(2)}) collective-permute-start(bf16[336,128]{1,0:T(8,128)(2,1)S(1)} %get-tuple-element.62), channel_id=1, source_target_pairs={{0,2},{2,0},{4,6},{6,4},{8,10},{10,8},{12,14},{14,12},{16,18},{18,... | collective-permute-start | bytes 258056 | tf_op jit(solution)/shard_map/ppermute | solution.py:33
  5.7 9.7 %collective-permute-start.1 = (bf16[336,128]{1,0:T(8,128)(2,1)S(1)}, bf16[336,128]{1,0:T(8,128)(2,1)S(1)}, u32[]{:S(2)}, u32[]{:S(2)}) collective-permute-start(bf16[336,128]{1,0:T(8,128)(2,1)S(1)} %get-tuple-element.63), channel_id=1, source_target_pairs={{0,30},{2,4},{4,2},{6,8},{8,6},{10,12},{12,10},{14,16},{16,14},{18... | collective-permute-start | bytes 258056 | tf_op jit(solution)/shard_map/ppermute | solution.py:32
  17.4 5.2 %collective-permute-start.2 = (bf16[288,128]{1,0:T(8,128)(2,1)S(1)}, bf16[288,128]{1,0:T(8,128)(2,1)S(1)}, u32[]{:S(2)}, u32[]{:S(2)}) collective-permute-start(bf16[288,128]{1,0:T(8,128)(2,1)S(1)} %get-tuple-element.74), channel_id=1, source_target_pairs={{0,2},{2,0},{4,6},{6,4},{8,10},{10,8},{12,14},{14,12},{16,18},{18,... | collective-permute-start | bytes 221192 | tf_op jit(solution)/shard_map/ppermute | solution.py:33
  17.5 6.5 %collective-permute-start.3 = (bf16[288,128]{1,0:T(8,128)(2,1)S(1)}, bf16[288,128]{1,0:T(8,128)(2,1)S(1)}, u32[]{:S(2)}, u32[]{:S(2)}) collective-permute-start(bf16[288,128]{1,0:T(8,128)(2,1)S(1)} %get-tuple-element.75), channel_id=1, source_target_pairs={{0,30},{2,4},{4,2},{6,8},{8,6},{10,12},{12,10},{14,16},{16,14},{18... | collective-permute-start | bytes 221192 | tf_op jit(solution)/shard_map/ppermute | solution.py:32
  24.8 4.3 %collective-permute-start.4 = (f32[32,128]{1,0:T(8,128)S(1)}, f32[32,128]{1,0:T(8,128)S(1)}, u32[]{:S(2)}, u32[]{:S(2)}) collective-permute-start(f32[32,128]{1,0:T(8,128)S(1)} %get-tuple-element.81), channel_id=1, source_target_pairs={{0,30},{2,0},{4,2},{6,4},{8,6},{10,8},{12,10},{14,12},{16,14},{18,... | collective-permute-start | bytes 49160 | tf_op jit(solution)/shard_map/ppermute | solution.py:25

commit v6 on v5

--- a/solution.py
+++ b/solution.py
@@ -254,26 +254,29 @@
     face_sums, up, down, mass, scale_in, proj, x_held, natural, pair, sems,
 ):
     ch = g.ch
+    quarter = g.e // 4
     copies = [
         pltpu.make_async_copy(source, target, sems.at[k])
         for k, (source, target) in enumerate((
-            (mass_hbm, mass), (perm_hbm, perm), (wave_hbm, wave), (up_hbm.at[0], proj.at[:ch]),
-            (low_hbm.at[0], proj.at[ch:]), (stiff_hbm, stiff), (scale_hbm, scale_in), (kb_hbm, kb), (pot_hbm, pot),
+            (mass_hbm, mass),
+            *((wave_hbm.at[pl.ds(p, quarter)], wave.at[pl.ds(p, quarter)]) for p in range(0, g.e, quarter)),
+            (up_hbm.at[0], proj.at[:ch]), (low_hbm.at[0], proj.at[ch:]), (perm_hbm, perm), (stiff_hbm, stiff),
+            (scale_hbm, scale_in), (kb_hbm, kb), (pot_hbm, pot),
         ))
     ]
     for copy in copies:
         copy.start()
     copies[0].wait()
     widen(g, mass, mass_wide)
-    copies[2].wait()
     for p in range(g.e):
+        if p % quarter == 0:
+            copies[1 + p // quarter].wait()
         rows = pl.ds(p * g.plane, g.plane)
         start = wave[p].astype(f32).reshape(g.plane, LANES)
         slab[rows, :] = (mass_wide[rows, :] * start).astype(bf16).astype(f32)
     gather_out(g, slab, x_top, x_held, ucol[0])
-    for k, copy in enumerate(copies):
-        if k not in (0, 2):
-            copy.wait()
+    for copy in copies[5:]:
+        copy.wait()
     for k in range(8):
         one = scale_in[k // 4, k % 4 // 2 : k % 4 // 2 + 1, k % 2 : k % 2 + 1]
         scale[k : k + 1, :] = jnp.broadcast_to(one, (1, LANES))
@@ -573,7 +576,7 @@
     half = d * g.plane
     copies = [
         pltpu.make_async_copy(done.at[pl.ds(p, n)], filtered.at[pl.ds(p, n)], sems.at[k])
-        for k, (p, n) in enumerate(((0, d), (d, d)))
+        for k, (p, n) in enumerate(((0, d), (d, d // 2), (d + d // 2, d // 2)))
     ]
 
     def give(planes):
@@ -588,13 +591,15 @@
     copies[0].start()
     field[half : half + g.plane, :] = new[half : half + g.plane, :]
     upper_sums(g, acol[0], scale, ordered, both, x_next, mine[...], sums)
-    for p in range(1, d):
-        rows = pl.ds(half + p * g.plane, g.plane)
-        added = sums[p * g.plane : (p + 1) * g.plane, :]
-        value = before[rows, :] + mass_wide[rows, :] * (added * (2.0 / spectrum_half))
-        field[rows, :] = value.astype(bf16).astype(f32)
-    give(range(d, g.e))
-    copies[1].start()
+    for p in range(d):
+        if p:
+            rows = pl.ds(half + p * g.plane, g.plane)
+            added = sums[p * g.plane : (p + 1) * g.plane, :]
+            value = before[rows, :] + mass_wide[rows, :] * (added * (2.0 / spectrum_half))
+            field[rows, :] = value.astype(bf16).astype(f32)
+        give([d + p])
+        if (p + 1) % (d // 2) == 0:
+            copies[1 + p // (d // 2)].start()
     a, b = split_element(acol[0])
     g.gather_element(field, x_own, 0, half, a, b, False)
     own_out[...] = dot(both_t[g.ch :, :], x_own[...])
@@ -650,7 +655,7 @@
          wire_first_s, wire_first_s],
         [plane_s, wire_first_s, wire_s, (mass_scale.shape, f32), (elem_scale.shape, f32),
          ((2 * ch, stiffness.shape[0]), bf16), x_one_s, ((2, used, LANES), f32), ((padded, 2 * LANES), bf16),
-         pltpu.SemaphoreType.DMA((9,))], 10**8, hbm=True,
+         pltpu.SemaphoreType.DMA((12,))], 10**8, hbm=True,
     )
     inner, outer = swapped(inner, outer, "space")
     ordered, pot_wide = call(
@@ -687,7 +692,7 @@
         functools.partial(last_high_kernel, g), scalars,
         (scale, mass_wide, before, low_new, *shared, new, mine, x_next),
         [(wave_in.shape, bf16), part],
-        [half_s, slab_s, x_one_s, (wave_in.shape, bf16), pltpu.SemaphoreType.DMA((2,))], 10**9, far_outs=1,
+        [half_s, slab_s, x_one_s, (wave_in.shape, bf16), pltpu.SemaphoreType.DMA((3,))], 10**9, far_outs=1,
     )
     return filtered, (own + held)[None]
 

time: 30 us -> 29.9 us (level)
  transfers between devices with their start and end apart: 5 -> 5, of which waited for: 1 -> 1; matrix products, arithmetic and copies ran while one was open for 0% -> 0% of each run, Pallas kernels for 28% -> 27%
where the time goes in v6:
time: 29.9 us; the launch traced here: 29.7 us
  Pallas kernels  13.6 us (45%)
  starting transfers between devices  11.4 us (38%)
  between operations  2.66 us (9%)
  waiting for transfers between devices  1.46 us (5%)
  other arithmetic  0.61 us (2%)
    pallas_call x7, Pallas kernels, call(): pl.pallas_call(kernel, out_shape=[jax.ShapeDtypeStruct(s, t) for s, t in...  13.6 us
    ppermute x2, starting transfers between devices, swapped(): outer = lax.ppermute(outer, axis, across)  8.21 us
    ppermute x1, starting transfers between devices, shifted(): return lax.ppermute(value, axis, pairs)  2.54 us
    ppermute x2, waiting for transfers between devices, swapped(): outer = lax.ppermute(outer, axis, across)  1.45 us
    ppermute x2, starting transfers between devices, swapped(): inner = lax.ppermute(inner, axis, within)  0.62 us
    broadcast_in_dim x1, other arithmetic, per_device(): return (filtered, (own + held)[None])  0.61 us
  transfers between devices with their start and end apart: 5, of which 1 were waited for; matrix products, arithmetic and copies ran while one was open for 0% of the time, Pallas kernels for 27%

profile of v6, /device:TPU:0, one launch (start us, length us, event | category | flops | bytes accessed | tf_op | source)
XLA Modules:
  0.0 29.7 jit_solution(17888338468649355562)
XLA Ops:
  2.6 2.6 %shard_map.131 = (f32[4096,128]{1,0:T(8,128)S(1)}, bf16[768,512]{1,0:T(8,128)(2,1)S(1)}, f32[4096,128]{1,0:T(8,128)S(1)}, bf16[16,16,16,128]{3,2,1,0:T(8,128)(2,...) custom-call(s32[1]{0:T(128)S(6)} %copy.14.acol, ...), custom_call_target="tpu_custom_call" | custom-call | flops 100000000 | bytes 2240770 | tf_op jit(solution)/shard_map/pallas_call | solution.py:617
  5.2 0.6 %collective-permute-start = (bf16[336,128]{1,0:T(8,128)(2,1)S(1)}, bf16[336,128]{1,0:T(8,128)(2,1)S(1)}, u32[]{:S(2)}, u32[]{:S(2)}) collective-permute-start(bf16[336,128]{1,0:T(8,128)(2,1)S(1)} %get-tuple-element.62), channel_id=1, source_target_pairs={{0,2},{2,0},{4,6},{6,4},{8,10},{10,8},{12,14},{14,12},{16,18},{18,... | collective-permute-start | bytes 258056 | tf_op jit(solution)/shard_map/ppermute | solution.py:33
  5.7 5.6 %collective-permute-start.1 = (bf16[336,128]{1,0:T(8,128)(2,1)S(1)}, bf16[336,128]{1,0:T(8,128)(2,1)S(1)}, u32[]{:S(2)}, u32[]{:S(2)}) collective-permute-start(bf16[336,128]{1,0:T(8,128)(2,1)S(1)} %get-tuple-element.63), channel_id=1, source_target_pairs={{0,30},{2,4},{4,2},{6,8},{8,6},{10,12},{12,10},{14,16},{16,14},{18... | collective-permute-start | bytes 258056 | tf_op jit(solution)/shard_map/ppermute | solution.py:32
  11.3 1.6 %shard_map.132 = (bf16[768,768]{1,0:T(8,128)(2,1)S(1)}, f32[4096,128]{1,0:T(8,128)S(1)}) custom-call(bf16[729,729]{1,0:T(8,128)(2,1)S(1)} %get-tuple-element.44.stiff, f32[1,768]{1,0:T(1,128)S(1)} %get-tuple-element.45.perm, f32[16,256]{1,0:T(8,128)S(1)} %get-tuple-element.46.pot), custom_call_target="tpu_custom_call" | custom-call | flops 2000000000 | bytes 1082338 | tf_op jit(solution)/shard_map/pallas_call | solution.py:617
  12.9 2.5 %shard_map.133 = (f32[4096,128]{1,0:T(8,128)S(1)}, f32[2048,128]{1,0:T(8,128)S(1)}, f32[2048,128]{1,0:T(8,128)S(1)}, f32[96,512]{1,0:T(8,128)S(1)}, bf16[128,512]{1,0:T(8,128)(2,1)S(1)}) custom-call(f32[8,128]{1,0:T(8,128)S(1)} %get-tuple-element.42.scale, bf16[768,768]{1,0:T(8,128)(2,1)S(1)} %get-tuple-element.47.ordered, ...), custom_call_target="tpu_custom_call" | custom-call | flops 2000000000 | bytes 9310208 | tf_op jit(solution)/shard_map/pallas_call | solution.py:617
  15.4 0.0 collective-permute-done.inner
  15.4 0.0 collective-permute-done.1.outer
  15.4 2.0 %shard_map.134 = (f32[4096,128]{1,0:T(8,128)S(1)}, bf16[768,512]{1,0:T(8,128)(2,1)S(1)}, f32[4096,128]{1,0:T(8,128)S(1)}, f32[32,128]{1,0:T(8,128)S(1)}, f32[32,...) custom-call(s32[1]{0:T(128)S(6)} %copy.14.acol, ...), custom_call_target="tpu_custom_call" | custom-call | flops 100000000 | bytes 8204416 | tf_op jit(solution)/shard_map/pallas_call | solution.py:617
  17.4 0.1 collective-permute-start.2
  17.5 2.6 %collective-permute-start.3 = (bf16[288,128]{1,0:T(8,128)(2,1)S(1)}, bf16[288,128]{1,0:T(8,128)(2,1)S(1)}, u32[]{:S(2)}, u32[]{:S(2)}) collective-permute-start(bf16[288,128]{1,0:T(8,128)(2,1)S(1)} %get-tuple-element.75), channel_id=1, source_target_pairs={{0,30},{2,4},{4,2},{6,8},{8,6},{10,12},{12,10},{14,16},{16,14},{18... | collective-permute-start | bytes 221192 | tf_op jit(solution)/shard_map/ppermute | solution.py:32
  20.0 2.5 %shard_map.135 = (f32[4096,128]{1,0:T(8,128)S(1)}, f32[2048,128]{1,0:T(8,128)S(1)}, f32[96,512]{1,0:T(8,128)S(1)}, bf16[128,512]{1,0:T(8,128)(2,1)S(1)}) custom-call(f32[8,128]{1,0:T(8,128)S(1)} %get-tuple-element.42.scale, bf16[768,768]{1,0:T(8,128)(2,1)S(1)} %get-tuple-element.47.ordered, bf16[768,512]{1,0:T(8,128)(2,1)S(1)} %get-tuple-element.64.x_top, ...), custom_call_target="tpu_custom_call" | custom-call | flops 2000000000 | bytes 11407360 | tf_op jit(solution)/shard_map/pallas_call | solution.py:617
  22.5 0.0 collective-permute-done.2.inner
  22.6 1.5 %collective-permute-done.3.outer = bf16[288,128]{1,0:T(8,128)(2,1)S(1)} collective-permute-done((bf16[288,128]{1,0:T(8,128)(2,1)S(1)}, bf16[288,128]{1,0:T(8,128)(2,1)S(1)}, u32[]{:S(2)}, u32[]{:S(2)}) %collective-permute-start.3) | collective-permute-done | bytes 73760 | tf_op jit(solution)/shard_map/ppermute | solution.py:32
  24.0 0.8 %shard_map.136 = (f32[32,128]{1,0:T(8,128)S(1)}, f32[2304,128]{1,0:T(8,128)S(1)}, bf16[32,128]{1,0:T(8,128)(2,1)S(1)}, bf16[128,512]{1,0:T(8,128)(2,1)S(1)}) custom-call(s32[1]{0:T(128)S(6)} %copy.14.acol, s32[1]{0:T(128)S(6)} %copy.16.ucol, s32[1]{0:T(128)S(6)} %copy.15.count, f32[8,128]{1,0:T(8,128)S(1)} %get-tuple-element.42.scale, ...), custom_call_target="tpu_custom_call" | custom-call | flops 100000000 | bytes 6111360 | tf_op jit(solution)/shard_map/pallas_call | solution.py:617
  24.8 2.5 %collective-permute-start.4 = (f32[32,128]{1,0:T(8,128)S(1)}, f32[32,128]{1,0:T(8,128)S(1)}, u32[]{:S(2)}, u32[]{:S(2)}) collective-permute-start(f32[32,128]{1,0:T(8,128)S(1)} %get-tuple-element.81), channel_id=1, source_target_pairs={{0,30},{2,0},{4,2},{6,4},{8,6},{10,8},{12,10},{14,12},{16,14},{18,... | collective-permute-start | bytes 49160 | tf_op jit(solution)/shard_map/ppermute | solution.py:25
  27.4 1.7 %shard_map.137 = (bf16[16,16,16,128]{3,2,1,0:T(8,128)(2,1)}, f32[32,128]{1,0:T(8,128)S(1)}) custom-call(s32[1]{0:T(128)S(6)} %copy.14.acol, s32[1]{0:T(128)S(6)} %copy.16.ucol, s32[1]{0:T(128)S(6)} %copy.15.count, f32[8,128]{1,0:T(8,128)S(1)} %get-tuple-element.42.scale, f32[4096,128]{1,0:T(8,128)S(1)} %get-tuple-element.43.mass_wide, ...), custom_call_target="tpu_custom_call" | custom-call | flops 1000000000 | bytes 7942144 | tf_op jit(solution)/shard_map/pallas_call | solution.py:617
  29.0 0.0 collective-permute-done.4
  29.0 0.6 %add_bitcast_fusion = f32[1,32,128]{2,1,0:T(8,128)} fusion(f32[32,128]{1,0:T(8,128)S(1)} %get-tuple-element.80, f32[32,128]{1,0:T(8,128)S(1)} %collective-permute-done.4), kind=kLoop, calls=%fused_computation | loop fusion | flops 4096 | bytes 49152 | tf_op jit(solution)/shard_map/broadcast_in_dim | solution.py:697
Async XLA Ops:
  5.2 10.2 %collective-permute-start = (bf16[336,128]{1,0:T(8,128)(2,1)S(1)}, bf16[336,128]{1,0:T(8,128)(2,1)S(1)}, u32[]{:S(2)}, u32[]{:S(2)}) collective-permute-start(bf16[336,128]{1,0:T(8,128)(2,1)S(1)} %get-tuple-element.62), channel_id=1, source_target_pairs={{0,2},{2,0},{4,6},{6,4},{8,10},{10,8},{12,14},{14,12},{16,18},{18,... | collective-permute-start | bytes 258056 | tf_op jit(solution)/shard_map/ppermute | solution.py:33
  5.7 9.7 %collective-permute-start.1 = (bf16[336,128]{1,0:T(8,128)(2,1)S(1)}, bf16[336,128]{1,0:T(8,128)(2,1)S(1)}, u32[]{:S(2)}, u32[]{:S(2)}) collective-permute-start(bf16[336,128]{1,0:T(8,128)(2,1)S(1)} %get-tuple-element.63), channel_id=1, source_target_pairs={{0,30},{2,4},{4,2},{6,8},{8,6},{10,12},{12,10},{14,16},{16,14},{18... | collective-permute-start | bytes 258056 | tf_op jit(solution)/shard_map/ppermute | solution.py:32
  17.4 5.2 %collective-permute-start.2 = (bf16[288,128]{1,0:T(8,128)(2,1)S(1)}, bf16[288,128]{1,0:T(8,128)(2,1)S(1)}, u32[]{:S(2)}, u32[]{:S(2)}) collective-permute-start(bf16[288,128]{1,0:T(8,128)(2,1)S(1)} %get-tuple-element.74), channel_id=1, source_target_pairs={{0,2},{2,0},{4,6},{6,4},{8,10},{10,8},{12,14},{14,12},{16,18},{18,... | collective-permute-start | bytes 221192 | tf_op jit(solution)/shard_map/ppermute | solution.py:33
  17.5 6.5 %collective-permute-start.3 = (bf16[288,128]{1,0:T(8,128)(2,1)S(1)}, bf16[288,128]{1,0:T(8,128)(2,1)S(1)}, u32[]{:S(2)}, u32[]{:S(2)}) collective-permute-start(bf16[288,128]{1,0:T(8,128)(2,1)S(1)} %get-tuple-element.75), channel_id=1, source_target_pairs={{0,30},{2,4},{4,2},{6,8},{8,6},{10,12},{12,10},{14,16},{16,14},{18... | collective-permute-start | bytes 221192 | tf_op jit(solution)/shard_map/ppermute | solution.py:32
  24.8 4.2 %collective-permute-start.4 = (f32[32,128]{1,0:T(8,128)S(1)}, f32[32,128]{1,0:T(8,128)S(1)}, u32[]{:S(2)}, u32[]{:S(2)}) collective-permute-start(f32[32,128]{1,0:T(8,128)S(1)} %get-tuple-element.81), channel_id=1, source_target_pairs={{0,30},{2,0},{4,2},{6,4},{8,6},{10,8},{12,10},{14,12},{16,14},{18,... | collective-permute-start | bytes 49160 | tf_op jit(solution)/shard_map/ppermute | solution.py:25

commit v7 on v6

--- a/solution.py
+++ b/solution.py
@@ -447,13 +447,14 @@
 
 def upper_sums(g, acol, scale, ordered, both, x_next, mine, sums):
     d = g.d
-    upper = dot(ordered[: g.used, :LANES], x_next[...])
-    lifted = dot(both[: g.used, g.ch :], mine)
+    skip = g.face_groups * d // 16 * 16
+    upper = dot(ordered[skip : g.used, :LANES], x_next[...])
+    lifted = dot(both[skip : g.used, g.ch :], mine)
 
     def loader(k):
         factor = scale[4 + k : 5 + k, :]
         lane = k * LANES
-        return lambda n: upper[n * d : (n + 1) * d, lane : lane + LANES] * factor
+        return lambda n: upper[n * d - skip : (n + 1) * d - skip, lane : lane + LANES] * factor
 
     for k, (a, b) in enumerate(g.columns):
         load = loader(k)
@@ -464,7 +465,7 @@
     for k, (a, b) in enumerate(g.columns):
         g.add_layer(sums, 0, a, b, loader(k), start=d * d)
     a, b = split_element(acol)
-    g.add_layer(sums, 0, a, b, lambda n: lifted[n * d : (n + 1) * d])
+    g.add_layer(sums, 0, a, b, lambda n: lifted[n * d - skip : (n + 1) * d - skip])
 
 
 def held_places(g, ucol, lifted_up):

time: 29.9 us -> 29.9 us (level)
  transfers between devices with their start and end apart: 5 -> 5, of which waited for: 1 -> 1; matrix products, arithmetic and copies ran while one was open for 0% -> 0% of each run, Pallas kernels for 27% -> 28%
where the time goes in v7:
time: 29.9 us; the launch traced here: 29.6 us
  Pallas kernels  13.5 us (45%)
  starting transfers between devices  11.4 us (38%)
  between operations  2.66 us (9%)
  waiting for transfers between devices  1.46 us (5%)
  other arithmetic  0.61 us (2%)
    pallas_call x7, Pallas kernels, call(): pl.pallas_call(kernel, out_shape=[jax.ShapeDtypeStruct(s, t) for s, t in...  13.5 us
    ppermute x2, starting transfers between devices, swapped(): outer = lax.ppermute(outer, axis, across)  8.22 us
    ppermute x1, starting transfers between devices, shifted(): return lax.ppermute(value, axis, pairs)  2.55 us
    ppermute x2, waiting for transfers between devices, swapped(): outer = lax.ppermute(outer, axis, across)  1.45 us
    ppermute x2, starting transfers between devices, swapped(): inner = lax.ppermute(inner, axis, within)  0.62 us
    broadcast_in_dim x1, other arithmetic, per_device(): return (filtered, (own + held)[None])  0.61 us
  transfers between devices with their start and end apart: 5, of which 1 were waited for; matrix products, arithmetic and copies ran while one was open for 0% of the time, Pallas kernels for 28%

profile of v7, /device:TPU:0, one launch (start us, length us, event | category | flops | bytes accessed | tf_op | source)
XLA Modules:
  0.0 29.6 jit_solution(11381290140969367365)
XLA Ops:
  2.6 2.6 %shard_map.131 = (f32[4096,128]{1,0:T(8,128)S(1)}, bf16[768,512]{1,0:T(8,128)(2,1)S(1)}, f32[4096,128]{1,0:T(8,128)S(1)}, bf16[16,16,16,128]{3,2,1,0:T(8,128)(2,...) custom-call(s32[1]{0:T(128)S(6)} %copy.14.acol, ...), custom_call_target="tpu_custom_call" | custom-call | flops 100000000 | bytes 2240770 | tf_op jit(solution)/shard_map/pallas_call | solution.py:618
  5.2 0.6 %collective-permute-start = (bf16[336,128]{1,0:T(8,128)(2,1)S(1)}, bf16[336,128]{1,0:T(8,128)(2,1)S(1)}, u32[]{:S(2)}, u32[]{:S(2)}) collective-permute-start(bf16[336,128]{1,0:T(8,128)(2,1)S(1)} %get-tuple-element.62), channel_id=1, source_target_pairs={{0,2},{2,0},{4,6},{6,4},{8,10},{10,8},{12,14},{14,12},{16,18},{18,... | collective-permute-start | bytes 258056 | tf_op jit(solution)/shard_map/ppermute | solution.py:33
  5.7 5.6 %collective-permute-start.1 = (bf16[336,128]{1,0:T(8,128)(2,1)S(1)}, bf16[336,128]{1,0:T(8,128)(2,1)S(1)}, u32[]{:S(2)}, u32[]{:S(2)}) collective-permute-start(bf16[336,128]{1,0:T(8,128)(2,1)S(1)} %get-tuple-element.63), channel_id=1, source_target_pairs={{0,30},{2,4},{4,2},{6,8},{8,6},{10,12},{12,10},{14,16},{16,14},{18... | collective-permute-start | bytes 258056 | tf_op jit(solution)/shard_map/ppermute | solution.py:32
  11.3 1.6 %shard_map.132 = (bf16[768,768]{1,0:T(8,128)(2,1)S(1)}, f32[4096,128]{1,0:T(8,128)S(1)}) custom-call(bf16[729,729]{1,0:T(8,128)(2,1)S(1)} %get-tuple-element.44.stiff, f32[1,768]{1,0:T(1,128)S(1)} %get-tuple-element.45.perm, f32[16,256]{1,0:T(8,128)S(1)} %get-tuple-element.46.pot), custom_call_target="tpu_custom_call" | custom-call | flops 2000000000 | bytes 1082338 | tf_op jit(solution)/shard_map/pallas_call | solution.py:618
  12.9 2.5 %shard_map.133 = (f32[4096,128]{1,0:T(8,128)S(1)}, f32[2048,128]{1,0:T(8,128)S(1)}, f32[2048,128]{1,0:T(8,128)S(1)}, f32[96,512]{1,0:T(8,128)S(1)}, bf16[128,512]{1,0:T(8,128)(2,1)S(1)}) custom-call(f32[8,128]{1,0:T(8,128)S(1)} %get-tuple-element.42.scale, bf16[768,768]{1,0:T(8,128)(2,1)S(1)} %get-tuple-element.47.ordered, ...), custom_call_target="tpu_custom_call" | custom-call | flops 2000000000 | bytes 9310208 | tf_op jit(solution)/shard_map/pallas_call | solution.py:618
  15.4 0.0 collective-permute-done.inner
  15.4 0.0 collective-permute-done.1.outer
  15.4 2.0 %shard_map.134 = (f32[4096,128]{1,0:T(8,128)S(1)}, bf16[768,512]{1,0:T(8,128)(2,1)S(1)}, f32[4096,128]{1,0:T(8,128)S(1)}, f32[32,128]{1,0:T(8,128)S(1)}, f32[32,...) custom-call(s32[1]{0:T(128)S(6)} %copy.14.acol, ...), custom_call_target="tpu_custom_call" | custom-call | flops 100000000 | bytes 8204416 | tf_op jit(solution)/shard_map/pallas_call | solution.py:618
  17.4 0.1 collective-permute-start.2
  17.4 2.6 %collective-permute-start.3 = (bf16[288,128]{1,0:T(8,128)(2,1)S(1)}, bf16[288,128]{1,0:T(8,128)(2,1)S(1)}, u32[]{:S(2)}, u32[]{:S(2)}) collective-permute-start(bf16[288,128]{1,0:T(8,128)(2,1)S(1)} %get-tuple-element.75), channel_id=1, source_target_pairs={{0,30},{2,4},{4,2},{6,8},{8,6},{10,12},{12,10},{14,16},{16,14},{18... | collective-permute-start | bytes 221192 | tf_op jit(solution)/shard_map/ppermute | solution.py:32
  20.0 2.5 %shard_map.135 = (f32[4096,128]{1,0:T(8,128)S(1)}, f32[2048,128]{1,0:T(8,128)S(1)}, f32[96,512]{1,0:T(8,128)S(1)}, bf16[128,512]{1,0:T(8,128)(2,1)S(1)}) custom-call(f32[8,128]{1,0:T(8,128)S(1)} %get-tuple-element.42.scale, bf16[768,768]{1,0:T(8,128)(2,1)S(1)} %get-tuple-element.47.ordered, bf16[768,512]{1,0:T(8,128)(2,1)S(1)} %get-tuple-element.64.x_top, ...), custom_call_target="tpu_custom_call" | custom-call | flops 2000000000 | bytes 11407360 | tf_op jit(solution)/shard_map/pallas_call | solution.py:618
  22.5 0.0 collective-permute-done.2.inner
  22.5 1.4 %collective-permute-done.3.outer = bf16[288,128]{1,0:T(8,128)(2,1)S(1)} collective-permute-done((bf16[288,128]{1,0:T(8,128)(2,1)S(1)}, bf16[288,128]{1,0:T(8,128)(2,1)S(1)}, u32[]{:S(2)}, u32[]{:S(2)}) %collective-permute-start.3) | collective-permute-done | bytes 73760 | tf_op jit(solution)/shard_map/ppermute | solution.py:32
  24.0 0.8 %shard_map.136 = (f32[32,128]{1,0:T(8,128)S(1)}, f32[2304,128]{1,0:T(8,128)S(1)}, bf16[32,128]{1,0:T(8,128)(2,1)S(1)}, bf16[128,512]{1,0:T(8,128)(2,1)S(1)}) custom-call(s32[1]{0:T(128)S(6)} %copy.14.acol, s32[1]{0:T(128)S(6)} %copy.16.ucol, s32[1]{0:T(128)S(6)} %copy.15.count, f32[8,128]{1,0:T(8,128)S(1)} %get-tuple-element.42.scale, ...), custom_call_target="tpu_custom_call" | custom-call | flops 100000000 | bytes 6111360 | tf_op jit(solution)/shard_map/pallas_call | solution.py:618
  24.8 2.5 %collective-permute-start.4 = (f32[32,128]{1,0:T(8,128)S(1)}, f32[32,128]{1,0:T(8,128)S(1)}, u32[]{:S(2)}, u32[]{:S(2)}) collective-permute-start(f32[32,128]{1,0:T(8,128)S(1)} %get-tuple-element.81), channel_id=1, source_target_pairs={{0,30},{2,0},{4,2},{6,4},{8,6},{10,8},{12,10},{14,12},{16,14},{18,... | collective-permute-start | bytes 49160 | tf_op jit(solution)/shard_map/ppermute | solution.py:25
  27.4 1.7 %shard_map.137 = (bf16[16,16,16,128]{3,2,1,0:T(8,128)(2,1)}, f32[32,128]{1,0:T(8,128)S(1)}) custom-call(s32[1]{0:T(128)S(6)} %copy.14.acol, s32[1]{0:T(128)S(6)} %copy.16.ucol, s32[1]{0:T(128)S(6)} %copy.15.count, f32[8,128]{1,0:T(8,128)S(1)} %get-tuple-element.42.scale, f32[4096,128]{1,0:T(8,128)S(1)} %get-tuple-element.43.mass_wide, ...), custom_call_target="tpu_custom_call" | custom-call | flops 1000000000 | bytes 7942144 | tf_op jit(solution)/shard_map/pallas_call | solution.py:618
  29.0 0.0 collective-permute-done.4
  29.0 0.6 %add_bitcast_fusion = f32[1,32,128]{2,1,0:T(8,128)} fusion(f32[32,128]{1,0:T(8,128)S(1)} %get-tuple-element.80, f32[32,128]{1,0:T(8,128)S(1)} %collective-permute-done.4), kind=kLoop, calls=%fused_computation | loop fusion | flops 4096 | bytes 49152 | tf_op jit(solution)/shard_map/broadcast_in_dim | solution.py:698
Async XLA Ops:
  5.2 10.2 %collective-permute-start = (bf16[336,128]{1,0:T(8,128)(2,1)S(1)}, bf16[336,128]{1,0:T(8,128)(2,1)S(1)}, u32[]{:S(2)}, u32[]{:S(2)}) collective-permute-start(bf16[336,128]{1,0:T(8,128)(2,1)S(1)} %get-tuple-element.62), channel_id=1, source_target_pairs={{0,2},{2,0},{4,6},{6,4},{8,10},{10,8},{12,14},{14,12},{16,18},{18,... | collective-permute-start | bytes 258056 | tf_op jit(solution)/shard_map/ppermute | solution.py:33
  5.7 9.7 %collective-permute-start.1 = (bf16[336,128]{1,0:T(8,128)(2,1)S(1)}, bf16[336,128]{1,0:T(8,128)(2,1)S(1)}, u32[]{:S(2)}, u32[]{:S(2)}) collective-permute-start(bf16[336,128]{1,0:T(8,128)(2,1)S(1)} %get-tuple-element.63), channel_id=1, source_target_pairs={{0,30},{2,4},{4,2},{6,8},{8,6},{10,12},{12,10},{14,16},{16,14},{18... | collective-permute-start | bytes 258056 | tf_op jit(solution)/shard_map/ppermute | solution.py:32
  17.4 5.2 %collective-permute-start.2 = (bf16[288,128]{1,0:T(8,128)(2,1)S(1)}, bf16[288,128]{1,0:T(8,128)(2,1)S(1)}, u32[]{:S(2)}, u32[]{:S(2)}) collective-permute-start(bf16[288,128]{1,0:T(8,128)(2,1)S(1)} %get-tuple-element.74), channel_id=1, source_target_pairs={{0,2},{2,0},{4,6},{6,4},{8,10},{10,8},{12,14},{14,12},{16,18},{18,... | collective-permute-start | bytes 221192 | tf_op jit(solution)/shard_map/ppermute | solution.py:33
  17.4 6.5 %collective-permute-start.3 = (bf16[288,128]{1,0:T(8,128)(2,1)S(1)}, bf16[288,128]{1,0:T(8,128)(2,1)S(1)}, u32[]{:S(2)}, u32[]{:S(2)}) collective-permute-start(bf16[288,128]{1,0:T(8,128)(2,1)S(1)} %get-tuple-element.75), channel_id=1, source_target_pairs={{0,30},{2,4},{4,2},{6,8},{8,6},{10,12},{12,10},{14,16},{16,14},{18... | collective-permute-start | bytes 221192 | tf_op jit(solution)/shard_map/ppermute | solution.py:32
  24.8 4.2 %collective-permute-start.4 = (f32[32,128]{1,0:T(8,128)S(1)}, f32[32,128]{1,0:T(8,128)S(1)}, u32[]{:S(2)}, u32[]{:S(2)}) collective-permute-start(f32[32,128]{1,0:T(8,128)S(1)} %get-tuple-element.81), channel_id=1, source_target_pairs={{0,30},{2,0},{4,2},{6,4},{8,6},{10,8},{12,10},{14,12},{16,14},{18,... | collective-permute-start | bytes 49160 | tf_op jit(solution)/shard_map/ppermute | solution.py:25
